TPU v7x, 32 devices: a whole 2x2x4 slice. The times are simulated.
32 devices in a mesh: rows: 32 (over z, y, x, core).
Axes of the slice: x: 2, y: 2, z: 4, core: 2. Of those that a mesh axis runs over, the one named last changes fastest.
Arguments:
- inputs: bfloat16 [32768, 768], P('rows'), may hold values from -6 to 6
- context_count: int32 [32], P('rows'), may hold values from 64 to 768, as said below
- query_count: int32 [32], P('rows'), may hold values from 1 to 256, as said below
- row_mask: int32 [32768], P('rows'), may hold values 0 or 1
- ln1_gain: float32 [768], replicated, may hold values from 0.25 to 1.75
- ln1_bias: float32 [768], replicated, may hold values from -3 to 3
- w_qkv: bfloat16 [768, 2304], replicated, may hold values from -0.21875 to 0.21875
- w_out: bfloat16 [768, 768], replicated, may hold values from -2 to 2
- ln2_gain: float32 [768], replicated, may hold values from 0.25 to 1.75
- ln2_bias: float32 [768], replicated, may hold values from -3 to 3
- w_up: bfloat16 [768, 3072], replicated, may hold values from -0.21875 to 0.21875
- w_down: bfloat16 [3072, 768], replicated, may hold values from -0.109375 to 0.109375
- cotangent: bfloat16 [32768, 768], P('rows'), may hold values from -6 to 6
Outputs:
- layer_out: bfloat16 [32768, 768], P('rows')
- grad_inputs: float32 [32768, 768], P('rows')
- grad_ln1_gain: float32 [768], replicated
- grad_ln1_bias: float32 [768], replicated
- grad_qkv: float32 [768, 2304], replicated
- grad_out: float32 [768, 768], replicated
- grad_ln2_gain: float32 [768], replicated
- grad_ln2_bias: float32 [768], replicated
- grad_up: float32 [768, 3072], P(None, 'rows')
- grad_down: float32 [3072, 768], P('rows')
Inputs may be any that keep to these rules, and one draw needn't show every extreme that they name: `context_count`: context rows of each table; in every draw some table has exactly 768 and some exactly 64. `query_count`: query rows of each table; in every draw some table has exactly 256.
All inputs are finite; a program needn't handle non-finite values. No bound on the sum of `row_mask` on one device may be relied on, other than what follows from the above.
Results may differ from a plain program's by a relative error of at most 0.0096.
Values sent between devices are 32-bit elements; how exact they have to be, the bound alone decides.
No kernel may reach another device: no remote copies, remote signals or barrier semaphores. Data moves between devices by JAX's collectives and lax.ppermute only.
A program may use at most 256 MiB of HBM per device.

v0:
```python
from functools import partial
import math

import jax
import jax.numpy as jnp
from jax import lax
from jax.experimental import pallas as pl
from jax.experimental.pallas import tpu as pltpu
from jax.sharding import PartitionSpec as P

HEADS = 12
HEAD = 64
WINDOW = 256
SHARE = 64
PIECE = 256

epsilon = 1e-05
score_factor = 1.0 / math.sqrt(HEAD)
masked_score = -3e38
root_half = math.sqrt(0.5)
root_two_pi = math.sqrt(2.0 / math.pi) * 0.5


def dot(left, right, left_dim=1, right_dim=0):
    return lax.dot_general(
        left, right, (((left_dim,), (right_dim,)), ((), ())), preferred_element_type=jnp.float32
    )


def cost(flops, transcendentals, bytes_accessed):
    return pl.CostEstimate(
        flops=flops // SHARE,
        transcendentals=transcendentals // SHARE,
        bytes_accessed=bytes_accessed // SHARE,
    )


def lane_masks(width):
    lanes = lax.broadcasted_iota(jnp.int32, (1, width), 1)
    return (lanes < HEAD, lanes >= HEAD)


def both_heads(rows):
    none = jnp.zeros_like(rows)
    return jnp.concatenate([jnp.where(lanes, rows, none) for lanes in lane_masks(2 * HEAD)], axis=0)


def one_head(rows):
    size = rows.shape[0] // 2
    return jnp.where(lane_masks(2 * HEAD)[0], rows[:size], rows[size:])


def columns(values):
    rows = values[0].shape[0]
    lanes = lax.broadcasted_iota(jnp.int32, (rows, 2 * HEAD), 1)
    block = jnp.zeros((rows, 2 * HEAD), jnp.float32)
    for lane, value in enumerate(values):
        block = jnp.where(lanes == lane, value, block)
    return block.astype(jnp.bfloat16)


def ones_block(rows):
    return jnp.ones((rows, 2 * HEAD), jnp.bfloat16)


def norm_rows(values):
    centre = jnp.mean(values, axis=-1, keepdims=True)
    centred = values - centre
    inverse = lax.rsqrt(jnp.mean(centred * centred, axis=-1, keepdims=True) + epsilon)
    return (centred * inverse, inverse)


def norm_rows_back(grad_norm, unit_rows, inverse, gain):
    grad_unit = grad_norm * gain
    grad_mean = jnp.mean(grad_unit, axis=-1, keepdims=True)
    grad_proj = jnp.mean(grad_unit * unit_rows, axis=-1, keepdims=True)
    return inverse * (grad_unit - grad_mean - unit_rows * grad_proj)


def column_sums(grad_norm, unit_rows):
    return jnp.concatenate(
        [
            jnp.sum(grad_norm * unit_rows, axis=0, keepdims=True),
            jnp.sum(grad_norm, axis=0, keepdims=True),
        ],
        axis=0,
    )


def shift_rows(count):
    taken = lax.broadcasted_iota(jnp.int32, (WINDOW, WINDOW + 16), 1)
    given = lax.broadcasted_iota(jnp.int32, (WINDOW, WINDOW + 16), 0) + count
    return jnp.where(taken == given, 1.0, 0.0).astype(jnp.bfloat16)


def project_kernel(
    context_ref,
    queries_ref,
    rows_ref,
    mask_ref,
    cotangent_ref,
    norms_ref,
    weight_ref,
    rolled_ref,
    norm_ref,
    query_ref,
    packed_ref,
    live_ref,
    dead_ref,
    upstream_ref,
    twice,
    present,
):
    step = pl.program_id(0)
    slots, width = rows_ref.shape

    @pl.when(step == 0)
    def _():
        context, queries = context_ref[0], queries_ref[0]
        start = pl.multiple_of(context // 16 * 16, 16)
        shifted = shift_rows(context - start)
        for half in (slice(0, slots), slice(slots, 2 * slots)):
            twice[half] = rows_ref[...]
        across = lax.broadcasted_iota(jnp.int32, (128, 128), 1)
        down = lax.broadcasted_iota(jnp.int32, (128, 128), 0)
        for group in range(slots // 128):
            kept = (across == down) & (mask_ref[group : group + 1] == 1)
            if group == 0:
                kept = kept | ((across == 0) & (down == 0))
            kept = jnp.where(kept, 1.0, 0.0).astype(jnp.bfloat16)
            marks = dot(kept, jnp.ones((128, 128), jnp.bfloat16)).astype(jnp.bfloat16)
            for first in (0, slots):
                present[first + group * 128 : first + (group + 1) * 128] = marks
        for first in range(0, slots, WINDOW):
            rows = dot(shifted, twice[pl.ds(start + first, WINDOW + 16), :])
            rolled_ref[first : first + WINDOW] = rows.astype(jnp.bfloat16)
            unit_rows = norm_rows(rows)[0]
            norm_ref[first : first + WINDOW] = (
                unit_rows * norms_ref[0:1] + norms_ref[1:2]
            ).astype(jnp.bfloat16)
            here = dot(shifted, present[pl.ds(start + first, WINDOW + 16), :])
            place = lax.broadcasted_iota(jnp.int32, here.shape, 0) + (first + context)
            place = jnp.where(place >= slots, place - slots, place)
            live_ref[first : first + WINDOW] = jnp.where(place < context + queries, here, 0.0)[:, 0:1]
            lanes = lax.broadcasted_iota(jnp.int32, here.shape, 1)
            if first > 0:
                known = (here > 0) & (place < context)
                split = lanes & (HEAD - 1)
                ones = jnp.where((split >= 1) & (split <= 3), 1.0, 0.0)
                dead = jnp.where((lanes == 0) & jnp.logical_not(known), masked_score, ones)
                dead_ref[first - WINDOW : first] = dead.astype(jnp.bfloat16)
            else:
                asked = jnp.where(place < context + queries, here, 0.0)[:, 0:1]
        twice[:slots] = cotangent_ref[...]
        near = jnp.minimum(start, slots - WINDOW - 16)
        near = pl.multiple_of(near, 16)
        upstream_ref[...] = dot(shift_rows(context - near), twice[pl.ds(near, WINDOW + 16), :]) * asked
        query_ref[...] = dot(norm_ref[:WINDOW], weight_ref[...]).astype(jnp.bfloat16)

    @pl.when(step > 0)
    def _():
        packed_ref[...] = dot(norm_ref[WINDOW:], weight_ref[...]).astype(jnp.bfloat16)


def project(context, queries, inputs, row_mask, cotangent, norms, w_qkv):
    slots, width = inputs.shape

    def fixed(shape):
        return pl.BlockSpec(shape, lambda j, at, more: (0, 0))

    whole = fixed((slots, width))
    outs = (
        ((slots, width), jnp.bfloat16),
        ((slots, width), jnp.bfloat16),
        ((WINDOW, width), jnp.bfloat16),
        ((slots - WINDOW, 2 * width), jnp.bfloat16),
        ((slots, 1), jnp.float32),
        ((slots - WINDOW, 128), jnp.bfloat16),
        ((WINDOW, width), jnp.float32),
    )
    specs = [fixed(shape) for shape, _ in outs]
    specs[3] = pl.BlockSpec((slots - WINDOW, width), lambda j, at, more: (0, jnp.maximum(j - 1, 0)))
    return pl.pallas_call(
        project_kernel,
        grid_spec=pltpu.PrefetchScalarGridSpec(
            num_scalar_prefetch=2,
            grid=(3,),
            in_specs=[
                whole,
                fixed((slots // 128, 128)),
                whole,
                fixed(norms.shape),
                pl.BlockSpec((width, width), lambda j, at, more: (0, j)),
            ],
            out_specs=specs,
            scratch_shapes=[
                pltpu.VMEM((2 * slots, width), jnp.bfloat16),
                pltpu.VMEM((2 * slots, 128), jnp.bfloat16),
            ],
        ),
        out_shape=[jax.ShapeDtypeStruct(shape, dtype) for shape, dtype in outs],
        cost_estimate=cost(
            flops=2 * slots * width * 2 * width,
            transcendentals=slots,
            bytes_accessed=14 * slots * width,
        ),
    )(context, queries, inputs, row_mask.reshape(slots // 128, 128), cotangent, norms, w_qkv)


def attend_kernel(
    keep_logs, query_ref, key_ref, value_ref, dead_ref, row_ref, rows_ref, wout_ref, *outs
):
    attended_ref, hidden_ref, unit_ref, inverse_ref = outs[:4]
    log_ref, attended = outs[-2:]
    step = pl.program_id(1)
    block = query_ref.shape[0]
    first_lane = columns([jnp.ones((2 * block, 1), jnp.float32)])
    queries = both_heads(query_ref[...] * jnp.bfloat16(score_factor))
    queries = jnp.concatenate([queries, first_lane], axis=1)
    keys = jnp.concatenate([key_ref[...], dead_ref[...]], axis=1)
    values = jnp.concatenate([value_ref[...], ones_block(key_ref.shape[0])], axis=1)
    scores = [dot(queries[k : k + PIECE], keys, 1, 1) for k in range(0, 2 * block, PIECE)]
    exponents = [
        jnp.exp(part - jnp.max(part, axis=-1, keepdims=True)).astype(jnp.bfloat16) for part in scores
    ]
    parts, totals = [], []
    for exponent in exponents:
        summed = dot(exponent, values)
        totals.append(summed[:, 2 * HEAD :])
        parts.append(summed[:, : 2 * HEAD] / summed[:, 2 * HEAD :])
    if keep_logs:
        logs = [
            jnp.max(part, axis=-1, keepdims=True) + jnp.log(total) for part, total in zip(scores, totals)
        ]
        log_ref[...] = one_head(jnp.concatenate(logs, axis=0))
    both = one_head(jnp.concatenate(parts, axis=0))
    both = jnp.where(row_ref[...] > 0, both, 0.0).astype(jnp.bfloat16)
    attended_ref[...] = both
    attended[:, pl.ds(pl.multiple_of(step * 2 * HEAD, 2 * HEAD), 2 * HEAD)] = both

    @pl.when(step == pl.num_programs(1) - 1)
    def _():
        hidden = rows_ref[...].astype(jnp.float32) + dot(attended[...], wout_ref[...])
        hidden_ref[...] = hidden
        unit_ref[...], inverse_ref[...] = norm_rows(hidden)


def attend(query_rows, packed_keys, key_dead, row_live, rows, w_out, from_query, from_row, keep_logs):
    slots, block, width = WINDOW, WINDOW, query_rows.shape[1]
    keys_len = packed_keys.shape[0]
    pairs = width // (2 * HEAD)
    whole = pl.BlockSpec((block, width), lambda r, p: (r, 0))
    return pl.pallas_call(
        partial(attend_kernel, keep_logs),
        grid=(slots // block, pairs),
        in_specs=[
            pl.BlockSpec((block, 2 * HEAD), lambda r, p: (from_query, p)),
            pl.BlockSpec((keys_len, 2 * HEAD), lambda r, p: (0, p)),
            pl.BlockSpec((keys_len, 2 * HEAD), lambda r, p: (0, pairs + p)),
            pl.BlockSpec((keys_len, 2 * HEAD), lambda r, p: (0, 0)),
            pl.BlockSpec((block, 1), lambda r, p: (from_row, 0)),
            pl.BlockSpec((block, width), lambda r, p: (from_row, 0)),
            pl.BlockSpec((width, width), lambda r, p: (0, 0)),
        ],
        out_specs=(
            pl.BlockSpec((block, 2 * HEAD), lambda r, p: (r, p)),
            whole,
            whole,
            pl.BlockSpec((block, 1), lambda r, p: (r, 0)),
            *([pl.BlockSpec((block, 2 * HEAD), lambda r, p: (r, p))] if keep_logs else ()),
        ),
        scratch_shapes=[pltpu.VMEM((block, width), jnp.bfloat16)],
        out_shape=(
            jax.ShapeDtypeStruct((slots, width), jnp.bfloat16),
            jax.ShapeDtypeStruct((slots, width), jnp.float32),
            jax.ShapeDtypeStruct((slots, width), jnp.float32),
            jax.ShapeDtypeStruct((slots, 1), jnp.float32),
            *([jax.ShapeDtypeStruct((slots, width), jnp.float32)] if keep_logs else ()),
        ),
        cost_estimate=cost(
            flops=4 * slots * keys_len * width * 4,
            transcendentals=slots * keys_len * HEADS,
            bytes_accessed=12 * slots * width + 4 * keys_len * width,
        ),
    )(query_rows, packed_keys, packed_keys, key_dead, row_live, rows, w_out)


def units_kernel(
    bits, at_ref, own_ref, got_ref, norms_ref, grad_ref, grad_got_ref, up_ref, down_ref, *outs
):
    keep_refs, act_ref, (own_grad, give_grad), (normed, upstream) = outs[:8], outs[8], outs[9:11], outs[11:]
    width = own_ref.shape[1]
    cut = width // 2

    @pl.when(pl.program_id(0) == 0)
    def _():
        for first, part, grad in ((0, own_ref, grad_ref), (WINDOW, got_ref, grad_got_ref)):
            rows = part[...] * norms_ref[2:3] + norms_ref[3:4]
            normed[first : first + WINDOW] = rows.astype(jnp.bfloat16)
            upstream[first : first + WINDOW] = grad[...].astype(jnp.bfloat16)

    pre_act = dot(normed[...], up_ref[...])
    share = gelu_parts(pre_act)
    activated = (pre_act * share).astype(jnp.bfloat16)
    slope = share + pre_act * (root_two_pi * jnp.exp(-0.5 * pre_act * pre_act))
    grad_pre = (dot(upstream[...], down_ref[...], 1, 1) * slope).astype(jnp.bfloat16)
    act_ref[...] = activated
    part = dot(grad_pre, up_ref[...], 1, 1)

    @pl.when(pl.program_id(0) == 0)
    def _():
        own_grad[...], give_grad[...] = part[:WINDOW], part[WINDOW:]

    @pl.when(pl.program_id(0) > 0)
    def _():
        own_grad[...] += part[:WINDOW]
        give_grad[...] += part[WINDOW:]

    for index, (left, right) in enumerate(((activated, upstream), (grad_pre, normed))):
        product = dot(left, right[...], 0, 0)
        mine = (at_ref[0] & bits[index]) != 0
        rows = keep_refs[4 * index].shape[1]
        product = product.reshape(-1, 2, rows, width)
        keep = jnp.where(mine, product[:, 1], product[:, 0])
        give = jnp.where(mine, product[:, 0], product[:, 1])
        for place, (low, high) in enumerate(((0, cut), (cut, width))):
            keep_refs[4 * index + 2 * place][...] = keep[:, :, low:high]
            keep_refs[4 * index + 2 * place + 1][...] = give[:, :, low:high]


def units(me, bits, rows, unit_own, unit_got, norms, upstream, upstream_got, w_up, w_down):
    width, hidden = w_up.shape
    half = hidden // 2
    tile = 8 * rows if 8 * rows >= 384 else 384
    tiles = half // tile
    whole = pl.BlockSpec((WINDOW, width), lambda j, at: (0, 0))
    pieces, shapes = [], []
    for index in range(2):
        size = 2 * rows * (index + 1)
        for _ in range(4):
            pieces.append(
                pl.BlockSpec((tile // (2 * size), size, width // 2), lambda j, at: (j, 0, 0))
            )
            shapes.append(
                jax.ShapeDtypeStruct((half // (2 * size), size, width // 2), jnp.float32)
            )
    acts = pl.BlockSpec((2 * WINDOW, tile), lambda j, at: (0, j))
    return pl.pallas_call(
        partial(units_kernel, bits),
        grid_spec=pltpu.PrefetchScalarGridSpec(
            num_scalar_prefetch=1,
            grid=(tiles,),
            in_specs=[
                whole,
                whole,
                pl.BlockSpec(norms.shape, lambda j, at: (0, 0)),
                whole,
                whole,
                pl.BlockSpec((width, tile), lambda j, at: (0, (at[0] & 1) * tiles + j)),
                pl.BlockSpec((tile, width), lambda j, at: ((at[0] & 1) * tiles + j, 0)),
            ],
            out_specs=(*pieces, acts, whole, whole),
            scratch_shapes=[
                pltpu.VMEM((2 * WINDOW, width), jnp.bfloat16),
                pltpu.VMEM((2 * WINDOW, width), jnp.bfloat16),
            ],
        ),
        out_shape=(
            *shapes,
            jax.ShapeDtypeStruct((2 * WINDOW, half), jnp.bfloat16),
            jax.ShapeDtypeStruct((WINDOW, width), jnp.float32),
            jax.ShapeDtypeStruct((WINDOW, width), jnp.float32),
        ),
        cost_estimate=cost(
            flops=16 * WINDOW * width * half,
            transcendentals=4 * WINDOW * half,
            bytes_accessed=12 * width * half,
        ),
    )(
        me.reshape(1),
        unit_own,
        unit_got,
        norms,
        upstream,
        upstream_got,
        w_up,
        w_down,
    )


def halves_kernel(right_dim, at_ref, left_ref, right_ref, own_ref, give_ref):
    product = dot(left_ref[...], right_ref[...], 1, right_dim)
    own_ref[...], give_ref[...] = product[:WINDOW], product[WINDOW:]


def halves(me, left, right, right_dim):
    rows, half = left.shape
    width = right.shape[1 - right_dim]
    tile = 256
    if right_dim == 1:
        spec = pl.BlockSpec((tile, half), lambda j, at: (j, at[0] & 1))
    else:
        spec = pl.BlockSpec((half, tile), lambda j, at: (at[0] & 1, j))
    out = pl.BlockSpec((WINDOW, tile), lambda j, at: (0, j))
    return pl.pallas_call(
        partial(halves_kernel, right_dim),
        grid_spec=pltpu.PrefetchScalarGridSpec(
            num_scalar_prefetch=1,
            grid=(width // tile,),
            in_specs=[pl.BlockSpec((rows, half), lambda j, at: (0, 0)), spec],
            out_specs=(out, out),
        ),
        out_shape=(jax.ShapeDtypeStruct((WINDOW, width), jnp.float32),) * 2,
        cost_estimate=cost(
            flops=2 * rows * width * half, transcendentals=0, bytes_accessed=4 * width * half
        ),
    )(me.reshape(1), left, right)


def attend_back_kernel(
    query_ref,
    key_ref,
    value_ref,
    dead_ref,
    row_ref,
    attended_ref,
    log_ref,
    own_ref,
    got_ref,
    unit_ref,
    inverse_ref,
    norms_ref,
    upstream_ref,
    wout_ref,
    dq_ref,
    dk_ref,
    dv_ref,
    grad_hidden_ref,
    low_ref,
    sums_ref,
):
    @pl.when(pl.program_id(0) == 0)
    def _():
        grad_norm = own_ref[...] + got_ref[...]
        unit_rows = unit_ref[...]
        sums_ref[...] = column_sums(grad_norm, unit_rows)
        grad_rows = norm_rows_back(grad_norm, unit_rows, inverse_ref[...], norms_ref[2:3])
        grad_hidden = upstream_ref[...] + grad_rows
        grad_hidden_ref[...] = grad_hidden
        low_ref[...] = grad_hidden.astype(jnp.bfloat16)

    block = query_ref.shape[0]
    key_rows = key_ref[...]
    grad = dot(low_ref[...], wout_ref[...], 1, 1)
    grad = jnp.where(row_ref[...] > 0, grad, 0.0).astype(jnp.bfloat16)
    product = grad.astype(jnp.float32) * attended_ref[...].astype(jnp.float32)
    grads = both_heads(grad)
    grads_wide = jnp.concatenate([grads, both_heads((-product).astype(jnp.bfloat16))], axis=1)
    values_wide = jnp.concatenate([value_ref[...], ones_block(key_rows.shape[0])], axis=1)
    lanes = lax.broadcasted_iota(jnp.int32, (block, 2 * HEAD), 1)
    rest = -log_ref[...]
    extra = jnp.zeros((block, 2 * HEAD), jnp.float32)
    for lane in range(1, 4):
        part = rest.astype(jnp.bfloat16).astype(jnp.float32)
        rest = rest - part
        extra = jnp.where((lanes & (HEAD - 1)) == lane, part, extra)
    extra = both_heads(extra)
    wide_lanes = lax.broadcasted_iota(jnp.int32, (2 * block, 2 * HEAD), 1)
    extra = jnp.where(wide_lanes == 0, 1.0, extra).astype(jnp.bfloat16)
    queries = both_heads(query_ref[...] * jnp.bfloat16(score_factor))
    queries_wide = jnp.concatenate([queries, extra], axis=1)
    keys_wide = jnp.concatenate([key_rows, dead_ref[...]], axis=1)
    pieces = [slice(k, k + PIECE) for k in range(0, 2 * block, PIECE)]
    probs = [jnp.exp(dot(queries_wide[piece], keys_wide, 1, 1)) for piece in pieces]
    grad_scores = [
        (prob * dot(grads_wide[piece], values_wide, 1, 1)).astype(jnp.bfloat16)
        for prob, piece in zip(probs, pieces)
    ]
    probs = jnp.concatenate([prob.astype(jnp.bfloat16) for prob in probs], axis=0)
    grad_scores = jnp.concatenate(grad_scores, axis=0)
    dq_ref[...] = (one_head(dot(grad_scores, key_rows)) * score_factor).astype(jnp.bfloat16)
    dk_ref[...] = dot(grad_scores, queries, 0, 0).astype(jnp.bfloat16)
    dv_ref[...] = dot(probs, grads, 0, 0).astype(jnp.bfloat16)


def attend_back(
    query_rows, packed_keys, key_dead, row_live, attended, logs, own, got, unit, inverse, norms, upstream, w_out
):
    slots, width = query_rows.shape
    keys_len = packed_keys.shape[0]
    pairs = width // (2 * HEAD)
    rows_spec = pl.BlockSpec((slots, 2 * HEAD), lambda p: (0, p))
    keys_spec = pl.BlockSpec((keys_len, 2 * HEAD), lambda p: (0, p))
    whole = pl.BlockSpec((slots, width), lambda p: (0, 0))
    column = pl.BlockSpec((slots, 1), lambda p: (0, 0))
    return pl.pallas_call(
        attend_back_kernel,
        grid=(pairs,),
        in_specs=[
            rows_spec,
            keys_spec,
            pl.BlockSpec((keys_len, 2 * HEAD), lambda p: (0, pairs + p)),
            pl.BlockSpec((keys_len, 2 * HEAD), lambda p: (0, 0)),
            column,
            rows_spec,
            rows_spec,
            whole,
            whole,
            whole,
            column,
            pl.BlockSpec(norms.shape, lambda p: (0, 0)),
            whole,
            pl.BlockSpec((2 * HEAD, width), lambda p: (p, 0)),
        ],
        out_specs=(
            rows_spec,
            keys_spec,
            keys_spec,
            whole,
            whole,
            pl.BlockSpec((2, width), lambda p: (0, 0)),
        ),
        out_shape=(
            jax.ShapeDtypeStruct((slots, width), jnp.bfloat16),
            jax.ShapeDtypeStruct((keys_len, width), jnp.bfloat16),
            jax.ShapeDtypeStruct((keys_len, width), jnp.bfloat16),
            jax.ShapeDtypeStruct((slots, width), jnp.float32),
            jax.ShapeDtypeStruct((slots, width), jnp.bfloat16),
            jax.ShapeDtypeStruct((2, width), jnp.float32),
        ),
        cost_estimate=cost(
            flops=10 * slots * keys_len * width * 4,
            transcendentals=slots * keys_len * HEADS,
            bytes_accessed=6 * slots * width + 8 * keys_len * width,
        ),
    )(
        query_rows,
        packed_keys,
        packed_keys,
        key_dead,
        row_live,
        attended,
        logs,
        own,
        got,
        unit,
        inverse,
        norms,
        upstream,
        w_out,
    )


def weights_kernel(
    at_ref, norm_ref, attended_ref, dq_ref, dk_ref, dv_ref, low_ref, keep_a, keep_b, give_a, give_b
):
    for odd, (even_a, even_b, odd_a, odd_b) in (
        (0, (keep_a, keep_b, give_a, give_b)),
        (1, (give_a, give_b, keep_a, keep_b)),
    ):

        @pl.when((at_ref[0] & 1) == odd)
        def _(even_a=even_a, even_b=even_b, odd_a=odd_a, odd_b=odd_b):
            even_a[...] = dot(norm_ref[:WINDOW], dq_ref[...], 0, 0)
            odd_a[...] = dot(norm_ref[WINDOW:], dk_ref[...], 0, 0)
            odd_b[...] = dot(norm_ref[WINDOW:], dv_ref[...], 0, 0)
            even_b[...] = dot(attended_ref[...], low_ref[...], 0, 0)


def weights(me, normed, attended, dq, dk, dv, low):
    slots, width = normed.shape
    tile = 256

    def full(value):
        return pl.BlockSpec(value.shape, lambda j, at: (0, 0))

    out = pl.BlockSpec((tile, width), lambda j, at: (j, 0))
    return pl.pallas_call(
        weights_kernel,
        grid_spec=pltpu.PrefetchScalarGridSpec(
            num_scalar_prefetch=1,
            grid=(width // tile,),
            in_specs=[
                pl.BlockSpec((slots, tile), lambda j, at: (0, j)),
                pl.BlockSpec((WINDOW, tile), lambda j, at: (0, j)),
                full(dq),
                full(dk),
                full(dv),
                full(low),
            ],
            out_specs=(out,) * 4,
        ),
        out_shape=(jax.ShapeDtypeStruct((width, width), jnp.float32),) * 4,
        cost_estimate=cost(
            flops=4 * slots * width * width, transcendentals=0, bytes_accessed=20 * width * width
        ),
    )(me.reshape(1), normed, attended, dq, dk, dv, low)


def rows_back_kernel(dq_ref, dk_ref, dv_ref, rows_ref, hidden_ref, norms_ref, wq, wk, wv, out_ref, sums_ref):
    step = pl.program_id(0)
    unit_rows, inverse = norm_rows(rows_ref[...].astype(jnp.float32))

    def finish(grad_norm):
        sums = column_sums(grad_norm, unit_rows)
        return (norm_rows_back(grad_norm, unit_rows, inverse, norms_ref[0:1]), sums)

    @pl.when(step == 0)
    def _():
        grad_rows, sums = finish(dot(dq_ref[...], wq[...], 1, 1))
        out_ref[...] = grad_rows + hidden_ref[...]
        sums_ref[...] = sums

    @pl.when(step > 0)
    def _():
        grad_rows, sums = finish(dot(dk_ref[...], wk[...], 1, 1) + dot(dv_ref[...], wv[...], 1, 1))
        out_ref[...] = grad_rows
        sums_ref[...] += sums


def rows_back(dq, dk, dv, rows, grad_hidden, norms, w_qkv):
    slots, width = rows.shape
    fixed = pl.BlockSpec((WINDOW, width), lambda r: (0, 0))
    keys = pl.BlockSpec((WINDOW, width), lambda r: (jnp.maximum(r - 1, 0), 0))
    tile = pl.BlockSpec((WINDOW, width), lambda r: (r, 0))
    return pl.pallas_call(
        rows_back_kernel,
        grid=(slots // WINDOW,),
        in_specs=[
            fixed,
            keys,
            keys,
            tile,
            fixed,
            pl.BlockSpec(norms.shape, lambda r: (0, 0)),
            pl.BlockSpec((width, width), lambda r: (0, 0)),
            pl.BlockSpec((width, width), lambda r: (0, 1)),
            pl.BlockSpec((width, width), lambda r: (0, 2)),
        ],
        out_specs=(tile, pl.BlockSpec((2, width), lambda r: (0, 0))),
        out_shape=(
            jax.ShapeDtypeStruct((slots, width), jnp.float32),
            jax.ShapeDtypeStruct((2, width), jnp.float32),
        ),
        cost_estimate=cost(
            flops=4 * slots * width * width, transcendentals=slots, bytes_accessed=12 * slots * width
        ),
    )(dq, dk, dv, rows, grad_hidden, norms, w_qkv, w_qkv, w_qkv)


def place_kernel(bits, far, got, me_ref, factor_ref, a_ref, b_ref, *refs):
    qkv_ref, out_ref, a_wide, b_wide, semaphores = refs[-5:]
    size, width = a_ref.shape
    me = me_ref[0]
    a_wide[...] = a_ref[...] * factor_ref[0, 0]
    b_wide[...] = b_ref[...] * factor_ref[0, 0]
    odd = (me & 1) != 0
    rows = []
    for bit in bits:
        high = (me & bit) != 0
        rows.append(jnp.where(high, 0 if far else size, size if far else 0))
    rows_a, rows_b = (pl.ds(pl.multiple_of(row, size), size) for row in rows)

    def place(targets):
        copies = [
            pltpu.make_async_copy(source, target, semaphores.at[index])
            for index, (source, target) in enumerate(zip((a_wide, b_wide), targets))
        ]
        for copy in copies:
            copy.start()
        for copy in copies:
            copy.wait()

    @pl.when(odd == got)
    def _():
        place((qkv_ref.at[rows_a, pl.ds(0, width)], out_ref.at[rows_b]))

    @pl.when(odd != got)
    def _():
        place((qkv_ref.at[rows_a, pl.ds(width, width)], qkv_ref.at[rows_b, pl.ds(2 * width, width)]))


def put(me, bits, far, got, factor, pieces, held):
    size, width = pieces[0].shape
    scalar = pl.BlockSpec(memory_space=pltpu.SMEM)
    anywhere = pl.BlockSpec(memory_space=pl.ANY)
    vmem = pl.BlockSpec(memory_space=pltpu.VMEM)
    operands = [*pieces, *(held or ())]
    return pl.pallas_call(
        partial(place_kernel, bits, far, got),
        in_specs=[scalar, scalar, vmem, vmem] + [anywhere] * (2 if held else 0),
        out_specs=(anywhere, anywhere),
        out_shape=(
            jax.ShapeDtypeStruct((2 * size, 3 * width), jnp.float32),
            jax.ShapeDtypeStruct((2 * size, width), jnp.float32),
        ),
        scratch_shapes=[
            pltpu.VMEM((size, width), jnp.float32),
            pltpu.VMEM((size, width), jnp.float32),
            pltpu.SemaphoreType.DMA((2,)),
        ],
        input_output_aliases={4: 0, 5: 1} if held else {},
        cost_estimate=cost(flops=0, transcendentals=0, bytes_accessed=8 * width * width),
    )(me.reshape(1), factor, *operands)


def output_kernel(
    at_ref, *refs
):
    units, hiddens, (own_ref, got_ref, base_ref, norms_ref, up_ref, down_ref) = refs[:3], refs[3:6], refs[6:12]
    out_ref, normed, total, twice = refs[12:]
    step = pl.program_id(0)
    slots, width = out_ref.shape

    @pl.when(step == 0)
    def _():
        for index in range(3):
            rows = slice(index * WINDOW, (index + 1) * WINDOW)
            normed[rows] = (units[index][...] * norms_ref[2:3] + norms_ref[3:4]).astype(jnp.bfloat16)
            total[rows] = hiddens[index][...]

    pre_act = dot(normed[...], up_ref[...])
    total[...] += dot((pre_act * gelu_parts(pre_act)).astype(jnp.bfloat16), down_ref[...])

    @pl.when(step == pl.num_programs(0) - 1)
    def _():
        window = (base_ref[...] + (own_ref[...] + got_ref[...])).astype(jnp.bfloat16)
        rest = total[...].astype(jnp.bfloat16)
        for first in (0, slots):
            twice[first : first + WINDOW] = window
            twice[first + WINDOW : first + slots] = rest
        begin = slots - at_ref[0]
        start = pl.multiple_of(begin // 16 * 16, 16)
        shifted = shift_rows(begin - start)
        for first in range(0, slots, WINDOW):
            rows = dot(shifted, twice[pl.ds(start + first, WINDOW + 16), :])
            out_ref[first : first + WINDOW] = rows.astype(jnp.bfloat16)


def output(context, units, hiddens, own, got, base, norms, w_up, w_down):
    width, hidden = w_up.shape
    slots = 4 * WINDOW
    tile = 512
    part = pl.BlockSpec((WINDOW, width), lambda j, at: (0, 0))
    return pl.pallas_call(
        output_kernel,
        grid_spec=pltpu.PrefetchScalarGridSpec(
            num_scalar_prefetch=1,
            grid=(hidden // tile,),
            in_specs=[part] * 9
            + [
                pl.BlockSpec(norms.shape, lambda j, at: (0, 0)),
                pl.BlockSpec((width, tile), lambda j, at: (0, j)),
                pl.BlockSpec((tile, width), lambda j, at: (j, 0)),
            ],
            out_specs=pl.BlockSpec((slots, width), lambda j, at: (0, 0)),
            scratch_shapes=[
                pltpu.VMEM((slots - WINDOW, width), jnp.bfloat16),
                pltpu.VMEM((slots - WINDOW, width), jnp.float32),
                pltpu.VMEM((2 * slots + 16, width), jnp.bfloat16),
            ],
        ),
        out_shape=jax.ShapeDtypeStruct((slots, width), jnp.bfloat16),
        cost_estimate=pl.CostEstimate(
            flops=12 * WINDOW * width * hidden,
            transcendentals=3 * WINDOW * hidden,
            bytes_accessed=8 * width * hidden,
        ),
    )(context, *units, *hiddens, own, got, base, norms, w_up, w_down)


def gelu_parts(values):
    share = 0.5 * (1.0 + lax.erf(values * root_half))
    return share


def local(
    devices,
    inputs,
    context_count,
    query_count,
    row_mask,
    ln1_gain,
    ln1_bias,
    w_qkv,
    w_out,
    ln2_gain,
    ln2_bias,
    w_up,
    w_down,
    cotangent,
):
    slots, width = inputs.shape
    hidden = w_up.shape[1]
    half = hidden // 2
    me = lax.axis_index("rows")
    core = me & 1

    def bit_of(bit):
        return ((me & bit) != 0).astype(jnp.int32)

    def swap(value, bit):
        return lax.ppermute(value, "rows", [(i, i ^ bit) for i in range(devices)])

    def pick(value, axis, index):
        return lax.dynamic_index_in_dim(value, index, axis, keepdims=False)

    bits = []
    bit = 2
    while bit < devices:
        bits.append(bit)
        bit *= 2
    top = bits[-1]

    def order_of(list_of_bits, flip):
        if flip and len(list_of_bits) > 1:
            return [list_of_bits[1], list_of_bits[0]] + list_of_bits[2:]
        return list_of_bits

    context = context_count[0]
    queries = query_count[0]
    norms = jnp.concatenate([ln1_gain, ln1_bias, ln2_gain, ln2_bias]).reshape(4, width)
    tie = lax.optimization_barrier
    rows, normed_low, query_window, packed_keys, row_column, key_dead, upstream = project(
        context_count, query_count, inputs, row_mask, cotangent, norms, w_qkv
    )
    upstream_got = swap(upstream, 1)
    attended_q, hidden_q, unit_two, inverse_two, log_sums = attend(
        query_window, packed_keys, key_dead, row_column, rows, w_out, 0, 0, True
    )
    ff_rows = half // (devices // 2)
    ff_bits = bits[:-1]
    pieces = units(
        me,
        bits[:2],
        ff_rows,
        unit_two,
        swap(unit_two, 1),
        norms,
        upstream,
        upstream_got,
        w_up,
        w_down,
    )
    activated, grad_own, grad_give = pieces[8:]
    pieces = pieces[:8]
    first_bits, second_bits = order_of(bits, False), order_of(bits, True)

    class Halving:
        def __init__(self, terms, axes):
            self.terms, self.axes = terms, list(axes)

        def split(self, bit):
            axis = self.axes.index(bit)
            mine = bit_of(bit)
            self.axes.remove(bit)
            self.kept = sum(pick(term, axis, mine) for term in self.terms)
            self.sent = sum(pick(term, axis, 1 - mine) for term in self.terms)

        def go(self, bit):
            self.terms = [self.kept, swap(self.sent, bit)]

        def send(self, bit):
            self.split(bit)
            self.go(bit)

    def got_of(chains):
        return tuple(chain.terms[1] for chain in chains)

    def set_got(chains, values):
        for chain, value in zip(chains, values):
            chain.terms[1] = value

    def feed_forward(index, place):
        keep, give = pieces[4 * index + 2 * place : 4 * index + 2 * place + 2]
        axes = ff_bits[::-1] + [1]
        axes.remove(ff_order[index][0])
        shape = [2] * len(axes) + [ff_rows, width // 2]
        got = swap(give, ff_order[index][0])
        return Halving([keep.reshape(shape), got.reshape(shape)], axes)

    def to_top(chain):
        pairs = [(i, i ^ top) for i in range(devices) if ((i & top) != 0) != ((i & 1) != 0)]
        value = chain.terms[0] + chain.terms[1]
        chain.terms = [value, lax.ppermute(value, "rows", pairs)]

    def hand_over(chain):
        mine = sum(pick(term, 1, core) for term in chain.terms)
        other = swap(sum(pick(term, 1, 1 - core) for term in chain.terms), 1)
        return jnp.where(bit_of(top) == core, mine, other)

    ff_order = (order_of(ff_bits, False), order_of(ff_bits, True))

    down_one = feed_forward(0, 0)
    up_one = feed_forward(1, 0)
    ones = (down_one, up_one)

    grad_query, grad_key, grad_value, grad_hidden, grad_low, sums_two = attend_back(
        query_window,
        packed_keys,
        key_dead,
        row_column,
        attended_q,
        log_sums,
        grad_own,
        swap(grad_give, 1),
        unit_two,
        inverse_two,
        norms,
        upstream,
        w_out,
    )
    keep_first, keep_second, *give = weights(
        me, normed_low, attended_q, grad_query, grad_key, grad_value, grad_low
    )

    def unroll(value):
        return lax.dynamic_slice(
            jnp.concatenate([value, value], axis=0), (slots - context, 0), (slots, width)
        )

    def joined(chains):
        terms = [jnp.stack([c.terms[k] for c in chains]) for k in range(2)]
        return Halving(terms, [None] + chains[0].axes)

    ones_got, give = tie((got_of(ones), give))
    set_got(ones, ones_got)
    for chain, order in zip(ones, ff_order):
        chain.send(order[1])
    give_first, give_second = swap(give[0], 1), swap(give[1], 1)
    shape = [2] * len(bits) + [width // (2 ** len(bits)), width]
    first = Halving([keep_first.reshape(shape), give_first.reshape(shape)], first_bits)
    second = Halving([keep_second.reshape(shape), give_second.reshape(shape)], second_bits)
    both = (first, second)

    first.send(first_bits[0])
    second.send(second_bits[0])
    grad_query, grad_key, grad_value, ones_got, _ = tie(
        (grad_query, grad_key, grad_value, got_of(ones), give_first)
    )
    set_got(ones, ones_got)
    ones = joined(ones)
    for bit in ff_bits[2:]:
        ones.send(bit)
    grad_rows, sums_one = rows_back(
        grad_query, grad_key, grad_value, rows, grad_hidden, norms, w_qkv
    )
    context_norms, _ = tie((normed_low[WINDOW:], grad_rows))
    context_queries = dot(context_norms, w_qkv[:, :width]).astype(jnp.bfloat16)

    def context_part(index, queries):
        return attend(
            queries, packed_keys, key_dead, row_column, rows, w_out, index, index + 1, False
        )[1:3]

    both_got, ones_got, context_queries, sums_one = tie(
        (got_of(both), ones.terms[1], context_queries, sums_one)
    )
    set_got(both, both_got)
    ones.terms[1] = ones_got

    first.split(first_bits[1])
    second.split(second_bits[1])
    first.sent, second.sent, ones.terms = tie((first.sent, second.sent, ones.terms))
    first.go(first_bits[1])
    second.go(second_bits[1])
    small = jnp.concatenate(
        [sums_one, sums_two, jnp.full((4, width), queries, jnp.float32)], axis=0
    )
    small = small + swap(small, 1)
    small_got = swap(small, top)
    to_top(ones)
    out_own, out_give = halves(me, activated, w_down, 0)
    out_give = swap(out_give, 1)
    both_got, ones_got, pieces, small_got, context_queries, out_own, out_give = tie(
        (got_of(both), ones.terms[1], pieces, small_got, context_queries, out_own, out_give)
    )
    set_got(both, both_got)
    ones.terms[1] = ones_got
    small = small + small_got

    for bit in bits[:2]:
        small = small + swap(small, bit)
    small, pieces = tie((small, pieces))
    down_two = feed_forward(0, 1)
    up_two = feed_forward(1, 1)
    twos = (down_two, up_two)
    both = joined(both)
    for bit in bits[2:-1]:
        both.send(bit)
    for bit in bits[2:-1]:
        small = small + swap(small, bit)
    part_one = context_part(0, context_queries)
    both_got, part_one, small, context_queries = tie(
        (both.terms[1], part_one, small, context_queries)
    )
    both.terms[1] = both_got

    value = both.terms[0] + both.terms[1]
    value_got = swap(value, top)
    part_two = context_part(1, context_queries)
    part_three = context_part(2, context_queries)
    twos_got, part_three = tie((got_of(twos), part_three))
    set_got(twos, twos_got)
    for chain, order in zip(twos, ff_order):
        chain.send(order[1])
    value_got, part_two, part_three, ones.terms = tie(
        (value_got, part_two, part_three, ones.terms)
    )
    value = value + value_got

    def widen(value, bit, axis):
        got = swap(value, bit)
        high = bit_of(bit) == 1
        return jnp.stack(
            [jnp.where(high, got, value), jnp.where(high, value, got)], axis=axis
        )

    for bit in bits[2:-1][::-1]:
        value = widen(value, bit, 1)
    ones = hand_over(ones)
    hiddens, units_c = zip(part_one, part_two, part_three)
    layer_out = output(
        context_count, units_c, hiddens, out_own, out_give, hidden_q, norms, w_up, w_down
    )
    twos_got, value, layer_out, ones = tie((got_of(twos), value, layer_out, ones))
    set_got(twos, twos_got)
    twos = joined(twos)

    first_value = widen(value[0], first_bits[1], 0)
    second_value = widen(value[1], second_bits[1], 0)
    for bit in ff_bits[2:]:
        twos.send(bit)
    grad_rows = unroll(grad_rows)
    first_value, second_value, twos_got, grad_rows, small = tie(
        (first_value, second_value, twos.terms[1], grad_rows, small)
    )
    twos.terms[1] = twos_got
    loss_factor = math.sqrt(devices) * (slots // 4) / small[4, 0]
    factor = loss_factor.reshape(1, 1)

    first_value, second_value = first_value.reshape(-1, width), second_value.reshape(-1, width)
    first_far = swap(first_value, first_bits[0])
    second_far = swap(second_value, second_bits[0])
    first_near = swap(first_value, 1)
    second_near = swap(second_value, 1)
    to_top(twos)
    twos = hand_over(twos)
    small = small * loss_factor
    grad_inputs = grad_rows * loss_factor
    ends = (first_bits[0], second_bits[0])
    held = put(me, ends, False, False, factor, (first_value, second_value), None)
    held = put(me, ends, False, True, factor, (first_near, second_near), held)
    down_share = loss_factor * jnp.concatenate([ones[0], twos[0]], axis=1)
    up_share = loss_factor * jnp.concatenate([ones[1], twos[1]], axis=1).T
    first_far, second_far, down_share, up_share, small, grad_inputs, held = tie(
        (first_far, second_far, down_share, up_share, small, grad_inputs, held)
    )

    first_got = swap(first_far, 1)
    second_got = swap(second_far, 1)
    held = put(me, ends, True, False, factor, (first_far, second_far), held)
    grad_qkv, grad_out = put(me, ends, True, True, factor, (first_got, second_got), held)
    return (
        layer_out,
        grad_inputs,
        small[0],
        small[1],
        grad_qkv,
        grad_out,
        small[2],
        small[3],
        up_share,
        down_share,
    )


def solution(mesh):
    placed = (
        P("rows", None),
        P("rows"),
        P("rows"),
        P("rows"),
        P(),
        P(),
        P(),
        P(),
        P(),
        P(),
        P(),
        P(),
        P("rows", None),
    )
    return jax.shard_map(
        partial(local, mesh.shape["rows"]),
        mesh=mesh,
        in_specs=placed,
        out_specs=(
            P("rows", None),
            P("rows", None),
            P(),
            P(),
            P(),
            P(),
            P(),
            P(),
            P(None, "rows"),
            P("rows", None),
        ),
        check_vma=False,
    )
```

profile of v0, /device:TPU:0, one launch (start us, length us, event | category | flops | bytes accessed | tf_op | source)
XLA Modules:
  0.0 277.4 jit_solution(6358223741530618667)
XLA Ops:
  3.3 10.0 %shard_map.204 = (bf16[1024,768]{1,0:T(8,128)(2,1)}, bf16[1024,768]{1,0:T(8,128)(2,1)}, bf16[256,768]{1,0:T(8,128)(2,1)}, bf16[768,1536]{1,0:T(8,128)(2,1)}, f32...) custom-call(s32[1]{0:T(128)S(6)} %copy.86.context_ref.at_ref, s32[1]{0:T(128)S(6)} %copy.87.queries_ref, ...), custom_call_target="tpu_custom_call" | custom-call | flops 37748736 | bytes 172032 | tf_op jit(solution)/shard_map/pallas_call | solution.py:183
  13.7 9.4 %shard_map.205 = (bf16[256,768]{1,0:T(8,128)(2,1)}, f32[256,768]{1,0:T(8,128)}, f32[256,768]{1,0:T(8,128)}, f32[256,1]{1,0:T(8,128)}, f32[256,768]{1,0:T(8,128)}) custom-call(bf16[256,768]{1,0:T(8,128)(2,1)} %get-tuple-element.131.query_ref, bf16[768,1536]{1,0:T(8,128)(2,1)} %get-tuple-element.132.key_ref.value_ref, ...), custom_call_target="tpu_custom_call" | custom-call | flops 37748736 | bytes 73728 | tf_op jit(solution)/shard_map/pallas_call | solution.py:253
  23.2 2.5 collective-permute-done.got_ref
  26.5 13.2 %shard_map.206 = (f32[4,192,384]{2,1,0:T(8,128)}, f32[4,192,384]{2,1,0:T(8,128)}, f32[4,192,384]{2,1,0:T(8,128)}, f32[4,192,384]{2,1,0:T(8,128)}, f32[2,384,384]...) custom-call(s32[1]{0:T(128)} %bitcast.at_ref.me_ref, ...), custom_call_target="tpu_custom_call" | custom-call | flops 75497472 | bytes 221184 | tf_op jit(solution)/shard_map/pallas_call | solution.py:348
  39.7 2.6 collective-permute-start.3
  43.8 2.5 collective-permute-done.2.got_ref
  47.2 12.2 %shard_map.207 = (bf16[256,768]{1,0:T(8,128)(2,1)}, bf16[768,768]{1,0:T(8,128)(2,1)}, bf16[768,768]{1,0:T(8,128)(2,1)}, f32[256,768]{1,0:T(8,128)}, bf16[256,768]{1,0:T(8,128)(2,1)}, /*index=5*/f32[2,768]{1,0:T(2,128)}) custom-call(bf16[256,768]{1,0:T(8,128)(2,1)} %get-tuple-element.131.query_ref, bf16[768,1536]{1,0:T(8,128)(2,1)} %get-tuple-element.132.key_ref.value_ref, ...), custom_call_target="tpu_custom_call" | custom-call | flops 94371840 | bytes 92160 | tf_op jit(solution)/shard_map/pallas_call | solution.py:496
  59.5 7.7 %shard_map.208 = (f32[768,768]{1,0:T(8,128)}, f32[768,768]{1,0:T(8,128)}, f32[768,768]{1,0:T(8,128)}, f32[768,768]{1,0:T(8,128)}) custom-call(s32[1]{0:T(128)} %bitcast.at_ref.me_ref, bf16[1024,768]{1,0:T(8,128)(2,1)} %get-tuple-element.130.norm_ref, bf16[256,768]{1,0:T(8,128)(2,1)} %get-tuple-element.136.attended_ref, ...), custom_call_target="tpu_custom_call" | custom-call | flops 37748736 | bytes 184320 | tf_op jit(solution)/shard_map/pallas_call | solution.py:578
  71.1 3.0 %fusion.36 = (f32[1,2,2,96,384]{4,3,0,2,1:T(8,128)S(1)}, f32[2,2,96,384]{3,2,1,0:T(8,128)}, f32[2,2,96,384]{3,2,1,0:T(8,128)S(1)}, f32[1,2,2,96,384]{4,3,0,2,1:T(8,128)}) fusion(s32[]{:T(128)S(6)} %select_n.123, f32[2,2,2,96,384]{4,3,2,1,0:T(8,128)S(1)} %bitcast.178, s32[]{:T(128)S(6)} %select_n.120, s32[]{:T(128)S(6)} %select_n.121, ...), kind=kLoop, calls=%fused_computation.78 | loop fusion | flops 589824 | bytes 7077904 | tf_op jit(solution)/shard_map/add | solution.py:857
  84.6 6.0 %collective-permute-done.10 = f32[2,2,96,384]{3,2,1,0:T(8,128)} collective-permute-done((f32[2,2,96,384]{3,2,1,0:T(8,128)}, f32[2,2,96,384]{3,2,1,0:T(8,128)}, u32[]{:S(2)}, u32[]{:S(2)}) %collective-permute-start.10) | collective-permute-done | bytes 589856 | tf_op jit(solution)/shard_map/ppermute | solution.py:803
  90.8 2.5 fusion.24
  96.1 4.9 %shard_map.210 = (f32[256,768]{1,0:T(8,128)}, f32[256,768]{1,0:T(8,128)}) custom-call(s32[1]{0:T(128)} %bitcast.at_ref.me_ref, bf16[512,1536]{1,0:T(8,128)(2,1)} %get-tuple-element.182.left_ref, bf16[3072,768]{1,0:T(8,128)(2,1)} %refs_11_.1), custom_call_target="tpu_custom_call" | custom-call | flops 18874368 | bytes 73728 | tf_op jit(solution)/shard_map/pallas_call | solution.py:405
  101.0 8.8 %shard_map.209 = (f32[1024,768]{1,0:T(8,128)}, f32[2,768]{1,0:T(2,128)}) custom-call(bf16[256,768]{1,0:T(8,128)(2,1)} %get-tuple-element.161.dq_ref, bf16[768,768]{1,0:T(8,128)(2,1)} %get-tuple-element.162.dk_ref, bf16[768,768]{1,0:T(8,128)(2,1)} %get-tuple-element.163.dv_ref, bf16[1024,768]{1,0:T(8,128)(2,1)} %get-tuple-element.135.rows_ref, ...), custom_call_target="tpu_custom_call" | custom-call | flops 37748736 | bytes 147456 | tf_op jit(solution)/shard_map/pallas_call | solution.py:626
  109.8 3.7 %convolution_convert_fusion.query_ref = bf16[768,768]{1,0:T(8,128)(2,1)} fusion(bf16[768,768]{1,0:T(8,128)(2,1)} %slice.39, bf16[768,2304]{1,0:T(8,128)(2,1)} %wv.1), kind=kOutput, calls=%fused_computation.4 | convolution fusion | flops 906559488 | bytes 3538944 | tf_op jit(solution)/shard_map/dot_general | solution.py:25
  122.5 2.3 collective-permute-start.12
  127.4 10.6 %collective-permute-done.16 = f32[8,768]{1,0:T(8,128)S(1)} collective-permute-done((f32[8,768]{1,0:T(8,128)S(1)}, f32[8,768]{1,0:T(8,128)S(1)}, u32[]{:S(2)}, u32[]{:S(2)}) %collective-permute-start.16) | collective-permute-done | bytes 24608 | tf_op jit(solution)/shard_map/ppermute | solution.py:803
  140.7 2.3 collective-permute-done.18
  149.9 2.2 collective-permute-start.23
  152.1 9.6 %shard_map.211 = (bf16[256,768]{1,0:T(8,128)(2,1)}, f32[256,768]{1,0:T(8,128)}, f32[256,768]{1,0:T(8,128)}, f32[256,1]{1,0:T(8,128)}) custom-call(bf16[768,768]{1,0:T(8,128)(2,1)} %convolution_convert_fusion.query_ref, bf16[768,1536]{1,0:T(8,128)(2,1)} %get-tuple-element.132.key_ref.value_ref, bf16[768,1536]{1,0:T(8,128)(2,1)} %get-tuple-element.132.key_ref.value_ref, ...), custom_call_target="tpu_custom_call" | custom-call | flops 37748736 | bytes 73728 | tf_op jit(solution)/shard_map/pallas_call | solution.py:253
  163.6 9.7 %shard_map.213 = (bf16[256,768]{1,0:T(8,128)(2,1)}, f32[256,768]{1,0:T(8,128)}, f32[256,768]{1,0:T(8,128)}, f32[256,1]{1,0:T(8,128)}) custom-call(bf16[768,768]{1,0:T(8,128)(2,1)} %convolution_convert_fusion.query_ref, bf16[768,1536]{1,0:T(8,128)(2,1)} %get-tuple-element.132.key_ref.value_ref, bf16[768,1536]{1,0:T(8,128)(2,1)} %get-tuple-element.132.key_ref.value_ref, ...), custom_call_target="tpu_custom_call" | custom-call | flops 37748736 | bytes 73728 | tf_op jit(solution)/shard_map/pallas_call | solution.py:253
  173.2 9.7 %shard_map.212 = (bf16[256,768]{1,0:T(8,128)(2,1)}, f32[256,768]{1,0:T(8,128)}, f32[256,768]{1,0:T(8,128)}, f32[256,1]{1,0:T(8,128)}) custom-call(bf16[768,768]{1,0:T(8,128)(2,1)} %convolution_convert_fusion.query_ref, bf16[768,1536]{1,0:T(8,128)(2,1)} %get-tuple-element.132.key_ref.value_ref, bf16[768,1536]{1,0:T(8,128)(2,1)} %get-tuple-element.132.key_ref.value_ref, ...), custom_call_target="tpu_custom_call" | custom-call | flops 37748736 | bytes 73728 | tf_op jit(solution)/shard_map/pallas_call | solution.py:253
  182.9 4.4 %collective-permute-done.26 = f32[2,2,48,768]{3,2,1,0:T(8,128)S(1)} collective-permute-done((f32[2,2,48,768]{3,2,1,0:T(8,128)S(1)}, f32[2,2,48,768]{3,2,1,0:T(8,128)S(1)}, u32[]{:S(2)}, u32[]{:S(2)}) %collective-permute-start.26) | collective-permute-done | bytes 589856 | tf_op jit(solution)/shard_map/ppermute | solution.py:803
  188.9 2.3 fusion.30
  195.1 15.6 %shard_map.214 = bf16[1024,768]{1,0:T(8,128)(2,1)} custom-call(s32[1]{0:T(128)S(6)} %copy.86.context_ref.at_ref, f32[256,768]{1,0:T(8,128)} %get-tuple-element.212.refs_0_, f32[256,768]{1,0:T(8,128)} %get-tuple-element.213.refs_1_, f32[256,768]{1,0:T(8,128)} %get-tuple-element.214.refs_2_, f32[256,768]{1,0:T(8,128)} %get-tuple-element.215.refs_3_, ...), custom_call_target="tpu_custom_call" | custom-call | flops 7247757312 | bytes 18874368 | tf_op jit(solution)/shard_map/pallas_call | solution.py:745
  217.5 3.1 %fusion = f32[1024,768]{1,0:T(8,128)S(1)} fusion(s32[]{:T(128)S(6)} %select_n.139, f32[1024,768]{1,0:T(8,128)} %get-tuple-element.165), kind=kLoop, calls=%fused_computation.2 | loop fusion | flops 786432 | bytes 6291460 | tf_op jit(solution)/shard_map/concatenate | solution.py:919
  222.0 8.1 %collective-permute-done.30 = f32[2,2,48,768]{3,2,1,0:T(8,128)} collective-permute-done((f32[2,2,48,768]{3,2,1,0:T(8,128)}, f32[2,2,48,768]{3,2,1,0:T(8,128)}, u32[]{:S(2)}, u32[]{:S(2)}) %collective-permute-start.30) | collective-permute-done | bytes 589856 | tf_op jit(solution)/shard_map/ppermute | solution.py:803
  232.9 2.3 collective-permute-done.31
  242.4 11.9 %collective-permute-done.34 = f32[2,2,96,384]{3,2,0,1:T(8,128)S(1)} collective-permute-done((f32[2,2,96,384]{3,2,0,1:T(8,128)S(1)}, f32[2,2,96,384]{3,2,0,1:T(8,128)S(1)}, u32[]{:S(2)}, u32[]{:S(2)}) %collective-permute-start.34) | collective-permute-done | bytes 589856 | tf_op jit(solution)/shard_map/ppermute | solution.py:885
  257.1 3.2 %shard_map.215 = (f32[768,2304]{1,0:T(8,128)}, f32[768,768]{1,0:T(8,128)}) custom-call(s32[1]{0:T(128)} %bitcast.at_ref.me_ref, f32[1,1]{1,0:T(1,128)} %div.6.factor_ref, f32[384,768]{1,0:T(8,128)} %bitcast.164, f32[384,768]{1,0:T(8,128)} %bitcast.161), custom_call_target="tpu_custom_call" | custom-call | bytes 73728 | tf_op jit(solution)/shard_map/pallas_call | solution.py:689
  264.1 3.2 %shard_map.216 = (f32[768,2304]{1,0:T(8,128)}, f32[768,768]{1,0:T(8,128)}) custom-call(s32[1]{0:T(128)} %bitcast.at_ref.me_ref, f32[1,1]{1,0:T(1,128)} %div.6.factor_ref, f32[384,768]{1,0:T(8,128)} %collective-permute-done.36.a_ref, f32[384,768]{1,0:T(8,128)} %collective-permute-done.37.b_ref, ...), custom_call_target="tpu_custom_call", output_to_operand_aliasing={{0}: (4, {}), {1}: (5, {})} | custom-call | bytes 73728 | tf_op jit(solution)/shard_map/pallas_call | solution.py:689
  268.7 3.1 %shard_map.217 = (f32[768,2304]{1,0:T(8,128)}, f32[768,768]{1,0:T(8,128)}) custom-call(s32[1]{0:T(128)} %bitcast.at_ref.me_ref, f32[1,1]{1,0:T(1,128)} %div.6.factor_ref, f32[384,768]{1,0:T(8,128)} %collective-permute-done.32.a_ref, f32[384,768]{1,0:T(8,128)} %collective-permute-done.33.b_ref, ...), custom_call_target="tpu_custom_call", output_to_operand_aliasing={{0}: (4, {}), {1}: (5, {})} | custom-call | bytes 73728 | tf_op jit(solution)/shard_map/pallas_call | solution.py:689
  274.0 3.2 %shard_map.218 = (f32[768,2304]{1,0:T(8,128)}, f32[768,768]{1,0:T(8,128)}) custom-call(s32[1]{0:T(128)} %bitcast.at_ref.me_ref, f32[1,1]{1,0:T(1,128)} %div.6.factor_ref, f32[384,768]{1,0:T(8,128)} %copy-done.11, f32[384,768]{1,0:T(8,128)} %copy-done.12, f32[768,2304]{1,0:T(8,128)} %get-tuple-element.244.refs_0_, ...), custom_call_target="tpu_custom_call", output_to_operand_aliasing={{0}: (4, {}), {1}: (5, {})} | custom-call | bytes 73728 | tf_op jit(solution)/shard_map/pallas_call | solution.py:689
  (168 shorter events, 78.2 us)
Async XLA Ops:
  13.3 9.9 %collective-permute-start.1 = (f32[256,768]{1,0:T(8,128)}, f32[256,768]{1,0:T(8,128)S(1)}, u32[]{:S(2)}, u32[]{:S(2)}) collective-permute-start(f32[256,768]{1,0:T(8,128)} %get-tuple-element.139.grad_ref.upstream_ref), channel_id=1, source_target_pairs={{0,1},{1,0},{2,3},{3,2},{4,5},{5,4},{6,7},{7,6},{8,9},{9,8},{10,11... | collective-permute-start | bytes 2359304 | tf_op jit(solution)/shard_map/ppermute | solution.py:803
  39.7 29.4 %collective-permute-start.3 = (f32[4,192,384]{2,1,0:T(8,128)}, f32[4,192,384]{2,1,0:T(8,128)}, u32[]{:S(2)}, u32[]{:S(2)}) collective-permute-start(f32[4,192,384]{2,1,0:T(8,128)} %get-tuple-element.148), channel_id=1, source_target_pairs={{0,2},{1,3},{2,0},{3,1},{4,6},{5,7},{6,4},{7,5},{8,10},{9,11},{10,... | collective-permute-start | bytes 3538952 | tf_op jit(solution)/shard_map/ppermute | solution.py:803
  42.3 28.3 %collective-permute-start.4 = (f32[2,384,384]{2,1,0:T(8,128)}, f32[2,384,384]{2,1,0:T(8,128)}, u32[]{:S(2)}, u32[]{:S(2)}) collective-permute-start(f32[2,384,384]{2,1,0:T(8,128)} %get-tuple-element.149), channel_id=1, source_target_pairs={{0,4},{1,5},{2,6},{3,7},{4,0},{5,1},{6,2},{7,3},{8,12},{9,13},{10,... | collective-permute-start | bytes 3538952 | tf_op jit(solution)/shard_map/ppermute | solution.py:803
  70.6 10.3 %collective-permute-start.7 = (f32[768,768]{1,0:T(8,128)}, f32[768,768]{1,0:T(8,128)}, u32[]{:S(2)}, u32[]{:S(2)}) collective-permute-start(f32[768,768]{1,0:T(8,128)} %get-tuple-element.154), channel_id=1, source_target_pairs={{0,1},{1,0},{2,3},{3,2},{4,5},{5,4},{6,7},{7,6},{8,9},{9,8},{10,11... | collective-permute-start | bytes 7077896 | tf_op jit(solution)/shard_map/ppermute | solution.py:803
  74.2 16.5 %collective-permute-start.10 = (f32[2,2,96,384]{3,2,1,0:T(8,128)}, f32[2,2,96,384]{3,2,1,0:T(8,128)}, u32[]{:S(2)}, u32[]{:S(2)}) collective-permute-start(f32[2,2,96,384]{3,2,1,0:T(8,128)} %get-tuple-element.271), channel_id=1, source_target_pairs={{0,2},{1,3},{2,0},{3,1},{4,6},{5,7},{6,4},{7,5},{8,10},{9,11},{10,... | collective-permute-start | bytes 1769480 | tf_op jit(solution)/shard_map/ppermute | solution.py:803
  74.5 16.3 %collective-permute-start.9 = (f32[2,2,96,384]{3,2,1,0:T(8,128)S(1)}, f32[2,2,96,384]{3,2,1,0:T(8,128)}, u32[]{:S(2)}, u32[]{:S(2)}) collective-permute-start(f32[2,2,96,384]{3,2,1,0:T(8,128)S(1)} %get-tuple-element.288), channel_id=1, source_target_pairs={{0,4},{1,5},{2,6},{3,7},{4,0},{5,1},{6,2},{7,3},{8,12},{9,13},{10,... | collective-permute-start | bytes 1769480 | tf_op jit(solution)/shard_map/ppermute | solution.py:803
  79.5 35.5 %collective-permute-start.6 = (f32[2,2,2,48,768]{4,3,2,0,1:T(8,128)}, f32[2,2,2,48,768]{4,3,2,0,1:T(8,128)}, u32[]{:S(2)}, u32[]{:S(2)}) collective-permute-start(f32[2,2,2,48,768]{4,3,2,0,1:T(8,128)} %fusion.2), channel_id=1, source_target_pairs={{0,2},{1,3},{2,0},{3,1},{4,6},{5,7},{6,4},{7,5},{8,10},{9,11},{10,... | collective-permute-start | bytes 3538952 | tf_op jit(solution)/shard_map/ppermute | solution.py:803
  84.1 30.9 %collective-permute-start.8 = (f32[2,2,2,48,768]{4,3,2,0,1:T(8,128)}, f32[2,2,2,48,768]{4,3,2,0,1:T(8,128)}, u32[]{:S(2)}, u32[]{:S(2)}) collective-permute-start(f32[2,2,2,48,768]{4,3,2,0,1:T(8,128)} %fusion.1), channel_id=1, source_target_pairs={{0,4},{1,5},{2,6},{3,7},{4,0},{5,1},{6,2},{7,3},{8,12},{9,13},{10,... | collective-permute-start | bytes 3538952 | tf_op jit(solution)/shard_map/ppermute | solution.py:803
  93.3 20.3 %collective-permute-start.11 = (f32[2,2,96,384]{3,2,0,1:T(8,128)}, f32[2,2,96,384]{3,2,0,1:T(8,128)S(1)}, u32[]{:S(2)}, u32[]{:S(2)}) collective-permute-start(f32[2,2,96,384]{3,2,0,1:T(8,128)} %get-tuple-element.263), channel_id=1, source_target_pairs={{0,8},{1,9},{2,10},{3,11},{4,12},{5,13},{6,14},{7,15},{8,0},{9,1},... | collective-permute-start | bytes 1769480 | tf_op jit(solution)/shard_map/ppermute | solution.py:803
  101.0 26.4 %collective-permute-start.17 = (f32[256,768]{1,0:T(8,128)}, f32[256,768]{1,0:T(8,128)}, u32[]{:S(2)}, u32[]{:S(2)}) collective-permute-start(f32[256,768]{1,0:T(8,128)} %get-tuple-element.184), channel_id=1, source_target_pairs={{0,1},{1,0},{2,3},{3,2},{4,5},{5,4},{6,7},{7,6},{8,9},{9,8},{10,11... | collective-permute-start | bytes 2359304 | tf_op jit(solution)/shard_map/ppermute | solution.py:803
  118.0 20.1 %collective-permute-start.15 = (f32[2,2,96,384]{3,2,0,1:T(8,128)S(1)}, f32[2,2,96,384]{3,2,0,1:T(8,128)S(1)}, u32[]{:S(2)}, u32[]{:S(2)}) collective-permute-start(f32[2,2,96,384]{3,2,0,1:T(8,128)S(1)} %add.315), channel_id=1, source_target_pairs={{1,17},{3,19},{5,21},{7,23},{9,25},{11,27},{13,29},{15,31},{16,0},... | collective-permute-start | bytes 1769480 | tf_op jit(solution)/shard_map/ppermute | solution.py:885
  119.3 18.8 %collective-permute-start.13 = (f32[2,2,48,768]{3,2,1,0:T(8,128)S(1)}, f32[2,2,48,768]{3,2,1,0:T(8,128)S(1)}, u32[]{:S(2)}, u32[]{:S(2)}) collective-permute-start(f32[2,2,48,768]{3,2,1,0:T(8,128)S(1)} %get-tuple-element.173), channel_id=1, source_target_pairs={{0,4},{1,5},{2,6},{3,7},{4,0},{5,1},{6,2},{7,3},{8,12},{9,13},{10,... | collective-permute-start | bytes 1769480 | tf_op jit(solution)/shard_map/ppermute | solution.py:803
  121.0 17.1 %collective-permute-start.14 = (f32[2,2,48,768]{3,2,1,0:T(8,128)S(1)}, f32[2,2,48,768]{3,2,1,0:T(8,128)S(1)}, u32[]{:S(2)}, u32[]{:S(2)}) collective-permute-start(f32[2,2,48,768]{3,2,1,0:T(8,128)S(1)} %get-tuple-element.174), channel_id=1, source_target_pairs={{0,2},{1,3},{2,0},{3,1},{4,6},{5,7},{6,4},{7,5},{8,10},{9,11},{10,... | collective-permute-start | bytes 1769480 | tf_op jit(solution)/shard_map/ppermute | solution.py:803
  125.8 12.3 %collective-permute-start.16 = (f32[8,768]{1,0:T(8,128)S(1)}, f32[8,768]{1,0:T(8,128)S(1)}, u32[]{:S(2)}, u32[]{:S(2)}) collective-permute-start(f32[8,768]{1,0:T(8,128)S(1)} %fusion.41), channel_id=1, source_target_pairs={{0,16},{1,17},{2,18},{3,19},{4,20},{5,21},{6,22},{7,23},{8,24},{9,... | collective-permute-start | bytes 73736 | tf_op jit(solution)/shard_map/ppermute | solution.py:803
  139.1 23.2 %collective-permute-start.22 = (f32[2,2,48,768]{3,2,1,0:T(8,128)}, f32[2,2,48,768]{3,2,1,0:T(8,128)}, u32[]{:S(2)}, u32[]{:S(2)}) collective-permute-start(f32[2,2,48,768]{3,2,1,0:T(8,128)} %fusion.19), channel_id=1, source_target_pairs={{0,8},{1,9},{2,10},{3,11},{4,12},{5,13},{6,14},{7,15},{8,0},{9,1},... | collective-permute-start | bytes 1769480 | tf_op jit(solution)/shard_map/ppermute | solution.py:803
  146.8 36.1 %collective-permute-start.20 = (f32[4,192,384]{2,1,0:T(8,128)}, f32[4,192,384]{2,1,0:T(8,128)}, u32[]{:S(2)}, u32[]{:S(2)}) collective-permute-start(f32[4,192,384]{2,1,0:T(8,128)} %get-tuple-element.191), channel_id=1, source_target_pairs={{0,2},{1,3},{2,0},{3,1},{4,6},{5,7},{6,4},{7,5},{8,10},{9,11},{10,... | collective-permute-start | bytes 3538952 | tf_op jit(solution)/shard_map/ppermute | solution.py:803
  148.4 34.5 %collective-permute-start.21 = (f32[2,384,384]{2,1,0:T(8,128)}, f32[2,384,384]{2,1,0:T(8,128)}, u32[]{:S(2)}, u32[]{:S(2)}) collective-permute-start(f32[2,384,384]{2,1,0:T(8,128)} %get-tuple-element.192), channel_id=1, source_target_pairs={{0,4},{1,5},{2,6},{3,7},{4,0},{5,1},{6,2},{7,3},{8,12},{9,13},{10,... | collective-permute-start | bytes 3538952 | tf_op jit(solution)/shard_map/ppermute | solution.py:803
  149.9 11.8 %collective-permute-start.23 = (f32[8,768]{1,0:T(8,128)S(1)}, f32[8,768]{1,0:T(8,128)S(1)}, u32[]{:S(2)}, u32[]{:S(2)}) collective-permute-start(f32[8,768]{1,0:T(8,128)S(1)} %add.318), channel_id=1, source_target_pairs={{0,8},{1,9},{2,10},{3,11},{4,12},{5,13},{6,14},{7,15},{8,0},{9,1},... | collective-permute-start | bytes 73736 | tf_op jit(solution)/shard_map/ppermute | solution.py:803
  163.5 23.9 %collective-permute-start.26 = (f32[2,2,48,768]{3,2,1,0:T(8,128)S(1)}, f32[2,2,48,768]{3,2,1,0:T(8,128)S(1)}, u32[]{:S(2)}, u32[]{:S(2)}) collective-permute-start(f32[2,2,48,768]{3,2,1,0:T(8,128)S(1)} %fusion.16), channel_id=1, source_target_pairs={{0,16},{1,17},{2,18},{3,19},{4,20},{5,21},{6,22},{7,23},{8,24},{9,... | collective-permute-start | bytes 1769480 | tf_op jit(solution)/shard_map/ppermute | solution.py:803
  188.2 22.6 %collective-permute-start.28 = (f32[2,96,384]{2,1,0:T(8,128)}, f32[2,96,384]{2,1,0:T(8,128)}, u32[]{:S(2)}, u32[]{:S(2)}) collective-permute-start(f32[2,96,384]{2,1,0:T(8,128)} %add_bitcast_fusion.1), channel_id=1, source_target_pairs={{0,1},{1,0},{2,3},{3,2},{4,5},{5,4},{6,7},{7,6},{8,9},{9,8},{10,11... | collective-permute-start | bytes 884744 | tf_op jit(solution)/shard_map/ppermute | solution.py:803
  188.2 24.3 %collective-permute-start.27 = (f32[2,2,48,768]{3,2,1,0:T(8,128)S(1)}, f32[2,2,48,768]{3,2,1,0:T(8,128)}, u32[]{:S(2)}, u32[]{:S(2)}) collective-permute-start(f32[2,2,48,768]{3,2,1,0:T(8,128)S(1)} %add.331), channel_id=1, source_target_pairs={{0,8},{1,9},{2,10},{3,11},{4,12},{5,13},{6,14},{7,15},{8,0},{9,1},... | collective-permute-start | bytes 1769480 | tf_op jit(solution)/shard_map/ppermute | solution.py:803
  191.3 22.5 %collective-permute-start.25 = (f32[2,2,96,384]{3,2,1,0:T(8,128)}, f32[2,2,96,384]{3,2,1,0:T(8,128)S(1)}, u32[]{:S(2)}, u32[]{:S(2)}) collective-permute-start(f32[2,2,96,384]{3,2,1,0:T(8,128)} %get-tuple-element.255), channel_id=1, source_target_pairs={{0,2},{1,3},{2,0},{3,1},{4,6},{5,7},{6,4},{7,5},{8,10},{9,11},{10,... | collective-permute-start | bytes 1769480 | tf_op jit(solution)/shard_map/ppermute | solution.py:803
  194.3 19.5 %collective-permute-start.24 = (f32[2,2,96,384]{3,2,1,0:T(8,128)}, f32[2,2,96,384]{3,2,1,0:T(8,128)S(1)}, u32[]{:S(2)}, u32[]{:S(2)}) collective-permute-start(f32[2,2,96,384]{3,2,1,0:T(8,128)} %get-tuple-element.257), channel_id=1, source_target_pairs={{0,4},{1,5},{2,6},{3,7},{4,0},{5,1},{6,2},{7,3},{8,12},{9,13},{10,... | collective-permute-start | bytes 1769480 | tf_op jit(solution)/shard_map/ppermute | solution.py:803
  215.0 15.1 %collective-permute-start.30 = (f32[2,2,48,768]{3,2,1,0:T(8,128)}, f32[2,2,48,768]{3,2,1,0:T(8,128)}, u32[]{:S(2)}, u32[]{:S(2)}) collective-permute-start(f32[2,2,48,768]{3,2,1,0:T(8,128)} %get-tuple-element.280), channel_id=1, source_target_pairs={{0,2},{1,3},{2,0},{3,1},{4,6},{5,7},{6,4},{7,5},{8,10},{9,11},{10,... | collective-permute-start | bytes 1769480 | tf_op jit(solution)/shard_map/ppermute | solution.py:803
  216.5 14.8 %collective-permute-start.29 = (f32[2,2,48,768]{3,2,1,0:T(8,128)}, f32[2,2,48,768]{3,2,1,0:T(8,128)}, u32[]{:S(2)}, u32[]{:S(2)}) collective-permute-start(f32[2,2,48,768]{3,2,1,0:T(8,128)} %get-tuple-element.281), channel_id=1, source_target_pairs={{0,4},{1,5},{2,6},{3,7},{4,0},{5,1},{6,2},{7,3},{8,12},{9,13},{10,... | collective-permute-start | bytes 1769480 | tf_op jit(solution)/shard_map/ppermute | solution.py:803
  220.6 14.6 %collective-permute-start.31 = (f32[2,2,96,384]{3,2,0,1:T(8,128)S(1)}, f32[2,2,96,384]{3,2,0,1:T(8,128)S(1)}, u32[]{:S(2)}, u32[]{:S(2)}) collective-permute-start(f32[2,2,96,384]{3,2,0,1:T(8,128)S(1)} %fusion.10), channel_id=1, source_target_pairs={{0,8},{1,9},{2,10},{3,11},{4,12},{5,13},{6,14},{7,15},{8,0},{9,1},... | collective-permute-start | bytes 1769480 | tf_op jit(solution)/shard_map/ppermute | solution.py:803
  235.3 19.0 %collective-permute-start.34 = (f32[2,2,96,384]{3,2,0,1:T(8,128)S(1)}, f32[2,2,96,384]{3,2,0,1:T(8,128)S(1)}, u32[]{:S(2)}, u32[]{:S(2)}) collective-permute-start(f32[2,2,96,384]{3,2,0,1:T(8,128)S(1)} %fusion.7), channel_id=1, source_target_pairs={{1,17},{3,19},{5,21},{7,23},{9,25},{11,27},{13,29},{15,31},{16,0},... | collective-permute-start | bytes 1769480 | tf_op jit(solution)/shard_map/ppermute | solution.py:885
  236.7 27.5 %collective-permute-start.37 = (f32[384,768]{1,0:T(8,128)S(1)}, f32[384,768]{1,0:T(8,128)}, u32[]{:S(2)}, u32[]{:S(2)}) collective-permute-start(f32[384,768]{1,0:T(8,128)S(1)} %bitcast.159), channel_id=1, source_target_pairs={{0,1},{1,0},{2,3},{3,2},{4,5},{5,4},{6,7},{7,6},{8,9},{9,8},{10,11... | collective-permute-start | bytes 3538952 | tf_op jit(solution)/shard_map/ppermute | solution.py:803
  238.5 28.9 %collective-permute-start.33 = (f32[384,768]{1,0:T(8,128)S(1)}, f32[384,768]{1,0:T(8,128)}, u32[]{:S(2)}, u32[]{:S(2)}) collective-permute-start(f32[384,768]{1,0:T(8,128)S(1)} %bitcast.160), channel_id=1, source_target_pairs={{0,4},{1,5},{2,6},{3,7},{4,0},{5,1},{6,2},{7,3},{8,12},{9,13},{10,... | collective-permute-start | bytes 3538952 | tf_op jit(solution)/shard_map/ppermute | solution.py:803
  239.7 24.4 %collective-permute-start.36 = (f32[384,768]{1,0:T(8,128)S(1)}, f32[384,768]{1,0:T(8,128)}, u32[]{:S(2)}, u32[]{:S(2)}) collective-permute-start(f32[384,768]{1,0:T(8,128)S(1)} %bitcast.162), channel_id=1, source_target_pairs={{0,1},{1,0},{2,3},{3,2},{4,5},{5,4},{6,7},{7,6},{8,9},{9,8},{10,11... | collective-permute-start | bytes 3538952 | tf_op jit(solution)/shard_map/ppermute | solution.py:803
  239.7 28.5 %collective-permute-start.32 = (f32[384,768]{1,0:T(8,128)S(1)}, f32[384,768]{1,0:T(8,128)}, u32[]{:S(2)}, u32[]{:S(2)}) collective-permute-start(f32[384,768]{1,0:T(8,128)S(1)} %bitcast.163), channel_id=1, source_target_pairs={{0,2},{1,3},{2,0},{3,1},{4,6},{5,7},{6,4},{7,5},{8,10},{9,11},{10,... | collective-permute-start | bytes 3538952 | tf_op jit(solution)/shard_map/ppermute | solution.py:803
  255.2 6.4 %collective-permute-start.35 = (f32[2,96,384]{2,1,0:T(8,128)S(1)}, f32[2,96,384]{2,1,0:T(8,128)}, u32[]{:S(2)}, u32[]{:S(2)}) collective-permute-start(f32[2,96,384]{2,1,0:T(8,128)S(1)} %add_bitcast_fusion), channel_id=1, source_target_pairs={{0,1},{1,0},{2,3},{3,2},{4,5},{5,4},{6,7},{7,6},{8,9},{9,8},{10,11... | collective-permute-start | bytes 884744 | tf_op jit(solution)/shard_map/ppermute | solution.py:803
  (37 other events, 157.4 us)
where the time goes:
time: 279 us; the launch traced here: 277 us
  Pallas kernels  123 us (44%)
  waiting for transfers between devices  61.4 us (22%)
  starting transfers between devices  39.6 us (14%)
  other arithmetic  37.4 us (13%)
  local copies, waits for them, and re-layouts  8.62 us (3%)
  matrix products  3.73 us (1%)
  between operations  3.28 us (1%)
    ppermute x38, waiting for transfers between devices, swap(): return lax.ppermute(value, 'rows', [(i, i ^ bit) for i in range(devices)])  49.4 us
    pallas_call x4, Pallas kernels, attend(): pl.pallas_call(partial(attend_kernel, keep_logs), grid=(slots // block, p...  38.3 us
    ppermute x38, starting transfers between devices, swap(): return lax.ppermute(value, 'rows', [(i, i ^ bit) for i in range(devices)])  37 us
    add x8, other arithmetic, split(): self.kept = sum((pick(term, axis, mine) for term in self.terms))  16.9 us
    pallas_call x1, Pallas kernels, output(): pl.pallas_call(output_kernel, grid_spec=pltpu.PrefetchScalarGridSpec(num_...  15.6 us
    pallas_call x1, Pallas kernels, units(): pl.pallas_call(partial(units_kernel, bits), grid_spec=pltpu.PrefetchScala...  13.2 us
    pallas_call x4, Pallas kernels, put(): pl.pallas_call(partial(place_kernel, bits, far, got), in_specs=[scalar, s...  12.7 us
    pallas_call x1, Pallas kernels, attend_back(): pl.pallas_call(attend_back_kernel, grid=(pairs,), in_specs=[rows_spec, ke...  12.2 us
  transfers between devices with their start and end apart: 40, of which 18 were waited for; matrix products, arithmetic and copies ran while one was open for 15% of the time, Pallas kernels for 35%

commit v1 on v0

--- a/solution.py
+++ b/solution.py
@@ -13,6 +13,9 @@
 WINDOW = 256
 SHARE = 64
 PIECE = 256
+STRIP = 768
+OUTPUT_TILE = 1024
+FIRST_PART = 256
 
 epsilon = 1e-05
 score_factor = 1.0 / math.sqrt(HEAD)
@@ -290,7 +293,7 @@
 ):
     keep_refs, act_ref, (own_grad, give_grad), (normed, upstream) = outs[:8], outs[8], outs[9:11], outs[11:]
     width = own_ref.shape[1]
-    cut = width // 2
+    cut = FIRST_PART
 
     @pl.when(pl.program_id(0) == 0)
     def _():
@@ -299,12 +302,17 @@
             normed[first : first + WINDOW] = rows.astype(jnp.bfloat16)
             upstream[first : first + WINDOW] = grad[...].astype(jnp.bfloat16)
 
-    pre_act = dot(normed[...], up_ref[...])
-    share = gelu_parts(pre_act)
-    activated = (pre_act * share).astype(jnp.bfloat16)
-    slope = share + pre_act * (root_two_pi * jnp.exp(-0.5 * pre_act * pre_act))
-    grad_pre = (dot(upstream[...], down_ref[...], 1, 1) * slope).astype(jnp.bfloat16)
-    act_ref[...] = activated
+    tile = up_ref.shape[1]
+    acts, pres = [], []
+    for first in range(0, tile, STRIP):
+        strip = slice(first, first + STRIP)
+        pre_act = dot(normed[...], up_ref[:, strip])
+        share = gelu_parts(pre_act)
+        acts.append((pre_act * share).astype(jnp.bfloat16))
+        slope = share + pre_act * (root_two_pi * jnp.exp(-0.5 * pre_act * pre_act))
+        pres.append((dot(upstream[...], down_ref[strip], 1, 1) * slope).astype(jnp.bfloat16))
+    act_ref[...] = jnp.concatenate(acts, axis=1)
+    grad_pre = jnp.concatenate(pres, axis=1)
     part = dot(grad_pre, up_ref[...], 1, 1)
 
     @pl.when(pl.program_id(0) == 0)
@@ -316,8 +324,8 @@
         own_grad[...] += part[:WINDOW]
         give_grad[...] += part[WINDOW:]
 
-    for index, (left, right) in enumerate(((activated, upstream), (grad_pre, normed))):
-        product = dot(left, right[...], 0, 0)
+    for index, (lefts, right) in enumerate(((acts, upstream), (pres, normed))):
+        product = jnp.concatenate([dot(left, right[...], 0, 0) for left in lefts], axis=0)
         mine = (at_ref[0] & bits[index]) != 0
         rows = keep_refs[4 * index].shape[1]
         product = product.reshape(-1, 2, rows, width)
@@ -337,13 +345,9 @@
     pieces, shapes = [], []
     for index in range(2):
         size = 2 * rows * (index + 1)
-        for _ in range(4):
-            pieces.append(
-                pl.BlockSpec((tile // (2 * size), size, width // 2), lambda j, at: (j, 0, 0))
-            )
-            shapes.append(
-                jax.ShapeDtypeStruct((half // (2 * size), size, width // 2), jnp.float32)
-            )
+        for span in (FIRST_PART, FIRST_PART, width - FIRST_PART, width - FIRST_PART):
+            pieces.append(pl.BlockSpec((tile // (2 * size), size, span), lambda j, at: (j, 0, 0)))
+            shapes.append(jax.ShapeDtypeStruct((half // (2 * size), size, span), jnp.float32))
     acts = pl.BlockSpec((2 * WINDOW, tile), lambda j, at: (0, j))
     return pl.pallas_call(
         partial(units_kernel, bits),
@@ -719,8 +723,11 @@
             normed[rows] = (units[index][...] * norms_ref[2:3] + norms_ref[3:4]).astype(jnp.bfloat16)
             total[rows] = hiddens[index][...]
 
-    pre_act = dot(normed[...], up_ref[...])
-    total[...] += dot((pre_act * gelu_parts(pre_act)).astype(jnp.bfloat16), down_ref[...])
+    acts = []
+    for first in range(0, up_ref.shape[1], 512):
+        pre_act = dot(normed[...], up_ref[:, first : first + 512])
+        acts.append((pre_act * gelu_parts(pre_act)).astype(jnp.bfloat16))
+    total[...] += dot(jnp.concatenate(acts, axis=1), down_ref[...])
 
     @pl.when(step == pl.num_programs(0) - 1)
     def _():
@@ -740,7 +747,7 @@
 def output(context, units, hiddens, own, got, base, norms, w_up, w_down):
     width, hidden = w_up.shape
     slots = 4 * WINDOW
-    tile = 512
+    tile = OUTPUT_TILE
     part = pl.BlockSpec((WINDOW, width), lambda j, at: (0, 0))
     return pl.pallas_call(
         output_kernel,
@@ -875,7 +882,7 @@
         keep, give = pieces[4 * index + 2 * place : 4 * index + 2 * place + 2]
         axes = ff_bits[::-1] + [1]
         axes.remove(ff_order[index][0])
-        shape = [2] * len(axes) + [ff_rows, width // 2]
+        shape = [2] * len(axes) + [ff_rows, keep.shape[-1]]
         got = swap(give, ff_order[index][0])
         return Halving([keep.reshape(shape), got.reshape(shape)], axes)
 
@@ -933,15 +940,19 @@
     second = Halving([keep_second.reshape(shape), give_second.reshape(shape)], second_bits)
     both = (first, second)
 
-    first.send(first_bits[0])
-    second.send(second_bits[0])
-    grad_query, grad_key, grad_value, ones_got, _ = tie(
-        (grad_query, grad_key, grad_value, got_of(ones), give_first)
+    first.split(first_bits[0])
+    second.split(second_bits[0])
+    first.sent, second.sent, grad_query, grad_key, grad_value, ones_got = tie(
+        (first.sent, second.sent, grad_query, grad_key, grad_value, got_of(ones))
     )
     set_got(ones, ones_got)
+    first.go(first_bits[0])
+    second.go(second_bits[0])
     ones = joined(ones)
     for bit in ff_bits[2:]:
         ones.send(bit)
+    to_top(ones)
+    grad_query, _ = tie((grad_query, ones.terms[0]))
     grad_rows, sums_one = rows_back(
         grad_query, grad_key, grad_value, rows, grad_hidden, norms, w_qkv
     )
@@ -953,60 +964,73 @@
             queries, packed_keys, key_dead, row_column, rows, w_out, index, index + 1, False
         )[1:3]
 
-    both_got, ones_got, context_queries, sums_one = tie(
-        (got_of(both), ones.terms[1], context_queries, sums_one)
+    out_own, out_give = halves(me, activated, w_down, 0)
+    out_give = swap(out_give, 1)
+    both_got, ones_got, context_queries, sums_one, out_own, out_give = tie(
+        (got_of(both), ones.terms[1], context_queries, sums_one, out_own, out_give)
     )
     set_got(both, both_got)
     ones.terms[1] = ones_got
 
     first.split(first_bits[1])
     second.split(second_bits[1])
-    first.sent, second.sent, ones.terms = tie((first.sent, second.sent, ones.terms))
+    first.sent, second.sent, ones.terms, sums_one, context_queries = tie(
+        (first.sent, second.sent, ones.terms, sums_one, context_queries)
+    )
     first.go(first_bits[1])
     second.go(second_bits[1])
     small = jnp.concatenate(
         [sums_one, sums_two, jnp.full((4, width), queries, jnp.float32)], axis=0
     )
     small = small + swap(small, 1)
-    small_got = swap(small, top)
-    to_top(ones)
-    out_own, out_give = halves(me, activated, w_down, 0)
-    out_give = swap(out_give, 1)
-    both_got, ones_got, pieces, small_got, context_queries, out_own, out_give = tie(
-        (got_of(both), ones.terms[1], pieces, small_got, context_queries, out_own, out_give)
+    part_one = context_part(0, context_queries)
+    both_got, small, context_queries, part_one, pieces = tie(
+        (got_of(both), small, context_queries, part_one, pieces)
     )
     set_got(both, both_got)
-    ones.terms[1] = ones_got
-    small = small + small_got
-
-    for bit in bits[:2]:
-        small = small + swap(small, bit)
-    small, pieces = tie((small, pieces))
     down_two = feed_forward(0, 1)
     up_two = feed_forward(1, 1)
     twos = (down_two, up_two)
+
     both = joined(both)
     for bit in bits[2:-1]:
         both.send(bit)
     for bit in bits[2:-1]:
         small = small + swap(small, bit)
-    part_one = context_part(0, context_queries)
-    both_got, part_one, small, context_queries = tie(
-        (both.terms[1], part_one, small, context_queries)
+    part_two = context_part(1, context_queries)
+    both_got, small, part_two, context_queries = tie(
+        (both.terms[1], small, part_two, context_queries)
     )
     both.terms[1] = both_got
 
     value = both.terms[0] + both.terms[1]
+    value, context_queries = tie((value, context_queries))
     value_got = swap(value, top)
-    part_two = context_part(1, context_queries)
     part_three = context_part(2, context_queries)
-    twos_got, part_three = tie((got_of(twos), part_three))
+    small, part_three, twos_got = tie((small, part_three, got_of(twos)))
     set_got(twos, twos_got)
-    for chain, order in zip(twos, ff_order):
-        chain.send(order[1])
-    value_got, part_two, part_three, ones.terms = tie(
-        (value_got, part_two, part_three, ones.terms)
-    )
+    for bit in bits[:2]:
+        small = small + swap(small, bit)
+    span = (width - FIRST_PART) // 2
+    early, late = (
+        [
+            Halving([term[..., first : first + span] for term in chain.terms], chain.axes)
+            for chain in twos
+        ]
+        for first in (0, span)
+    )
+    for chain, order in zip(early, ff_order):
+        chain.split(order[1])
+    early[0].sent, early[1].sent, small = tie((early[0].sent, early[1].sent, small))
+    for chain, order in zip(early, ff_order):
+        chain.go(order[1])
+    for chain, order in zip(late, ff_order):
+        chain.split(order[1])
+    sent = (late[0].sent, late[1].sent)
+    _, early_got, value_got, small, part_two, part_three, ones.terms, grad_rows = tie(
+        (sent, got_of(early), value_got, small, part_two, part_three, ones.terms, grad_rows)
+    )
+    set_got(early, early_got)
     value = value + value_got
 
     def widen(value, bit, axis):
@@ -1018,26 +1042,26 @@
 
     for bit in bits[2:-1][::-1]:
         value = widen(value, bit, 1)
+    for chain, order in zip(late, ff_order):
+        chain.go(order[1])
     ones = hand_over(ones)
-    hiddens, units_c = zip(part_one, part_two, part_three)
-    layer_out = output(
-        context_count, units_c, hiddens, out_own, out_give, hidden_q, norms, w_up, w_down
-    )
-    twos_got, value, layer_out, ones = tie((got_of(twos), value, layer_out, ones))
-    set_got(twos, twos_got)
-    twos = joined(twos)
+    small = small + swap(small, top)
+    value, small, ones, part_one, late_got = tie((value, small, ones, part_one, got_of(late)))
+    set_got(late, late_got)
+    twos = joined(early + late)
+    loss_factor = math.sqrt(devices) * (slots // 4) / small[4, 0]
+    factor = loss_factor.reshape(1, 1)
 
     first_value = widen(value[0], first_bits[1], 0)
     second_value = widen(value[1], second_bits[1], 0)
     for bit in ff_bits[2:]:
-        twos.send(bit)
-    grad_rows = unroll(grad_rows)
-    first_value, second_value, twos_got, grad_rows, small = tie(
-        (first_value, second_value, twos.terms[1], grad_rows, small)
-    )
-    twos.terms[1] = twos_got
-    loss_factor = math.sqrt(devices) * (slots // 4) / small[4, 0]
-    factor = loss_factor.reshape(1, 1)
+        twos.split(bit)
+        twos.go(bit)
+    grad_inputs = unroll(grad_rows * loss_factor)
+    small = small * loss_factor
+    first_value, second_value, grad_inputs, small, part_one, twos.terms = tie(
+        (first_value, second_value, grad_inputs, small, part_one, twos.terms)
+    )
 
     first_value, second_value = first_value.reshape(-1, width), second_value.reshape(-1, width)
     first_far = swap(first_value, first_bits[0])
@@ -1045,20 +1069,23 @@
     first_near = swap(first_value, 1)
     second_near = swap(second_value, 1)
     to_top(twos)
-    twos = hand_over(twos)
-    small = small * loss_factor
-    grad_inputs = grad_rows * loss_factor
+    hiddens, units_c = zip(part_one, part_two, part_three)
+    layer_out = output(
+        context_count, units_c, hiddens, out_own, out_give, hidden_q, norms, w_up, w_down
+    )
     ends = (first_bits[0], second_bits[0])
     held = put(me, ends, False, False, factor, (first_value, second_value), None)
     held = put(me, ends, False, True, factor, (first_near, second_near), held)
-    down_share = loss_factor * jnp.concatenate([ones[0], twos[0]], axis=1)
-    up_share = loss_factor * jnp.concatenate([ones[1], twos[1]], axis=1).T
-    first_far, second_far, down_share, up_share, small, grad_inputs, held = tie(
-        (first_far, second_far, down_share, up_share, small, grad_inputs, held)
-    )
+    first_far, second_far, twos_got, held, layer_out = tie(
+        (first_far, second_far, twos.terms[1], held, layer_out)
+    )
+    twos.terms[1] = twos_got
 
     first_got = swap(first_far, 1)
     second_got = swap(second_far, 1)
+    twos = hand_over(twos)
+    down_share = loss_factor * jnp.concatenate([ones[0], twos[0], twos[2]], axis=1)
+    up_share = loss_factor * jnp.concatenate([ones[1], twos[1], twos[3]], axis=1).T
     held = put(me, ends, True, False, factor, (first_far, second_far), held)
     grad_qkv, grad_out = put(me, ends, True, True, factor, (first_got, second_got), held)
     return (

time: 279 us -> 270 us (0.968)
  waiting for transfers between devices: 61.4 us -> 53.2 us
  local copies, waits for them, and re-layouts: 8.62 us -> 14 us
  starting transfers between devices: 39.6 us -> 34.7 us
    ppermute x2, waiting for transfers between devices: 12 us -> 0.59 us  [to_top(): chain.terms = [value, lax.ppermute(value, 'rows', pairs)]]
    ppermute x38 -> x40, starting transfers between devices: 37 us -> 32.1 us  [swap(): return lax.ppermute(value, 'rows', [(i, i ^ bit) for i in range(devices)])]
    slice x0 -> x4, local copies, waits for them, and re-layouts: none -> 4.27 us  [local(): term[..., first:first + span]]
    add x8 -> x9, other arithmetic: 16.9 us -> 13.1 us  [split(): self.kept = sum((pick(term, axis, mine) for term in self.terms))]
    ppermute x38 -> x40, waiting for transfers between devices: 49.4 us -> 52.6 us  [swap(): return lax.ppermute(value, 'rows', [(i, i ^ bit) for i in range(devices)])]
    unnamed x58 -> x74, local copies, waits for them, and re-layouts: 3.74 us -> 6.69 us
  transfers between devices with their start and end apart: 40 -> 42, of which waited for: 18 -> 25; matrix products, arithmetic and copies ran while one was open for 15% -> 15% of each run, Pallas kernels for 35% -> 36%
where the time goes in v1:
time: 270 us; the launch traced here: 268 us
  Pallas kernels  123 us (46%)
  waiting for transfers between devices  53.2 us (20%)
  other arithmetic  37 us (14%)
  starting transfers between devices  34.7 us (13%)
  local copies, waits for them, and re-layouts  14 us (5%)
  matrix products  3.37 us (1%)
  between operations  3.36 us (1%)
    ppermute x40, waiting for transfers between devices, swap(): return lax.ppermute(value, 'rows', [(i, i ^ bit) for i in range(devices)])  52.6 us
    pallas_call x4, Pallas kernels, attend(): pl.pallas_call(partial(attend_kernel, keep_logs), grid=(slots // block, p...  38.4 us
    ppermute x40, starting transfers between devices, swap(): return lax.ppermute(value, 'rows', [(i, i ^ bit) for i in range(devices)])  32.1 us
    pallas_call x1, Pallas kernels, output(): pl.pallas_call(output_kernel, grid_spec=pltpu.PrefetchScalarGridSpec(num_...  15.1 us
    pallas_call x1, Pallas kernels, units(): pl.pallas_call(partial(units_kernel, bits), grid_spec=pltpu.PrefetchScala...  13.2 us
    add x9, other arithmetic, split(): self.kept = sum((pick(term, axis, mine) for term in self.terms))  13.1 us
    pallas_call x4, Pallas kernels, put(): pl.pallas_call(partial(place_kernel, bits, far, got), in_specs=[scalar, s...  12.6 us
    pallas_call x1, Pallas kernels, attend_back(): pl.pallas_call(attend_back_kernel, grid=(pairs,), in_specs=[rows_spec, ke...  12.2 us
  transfers between devices with their start and end apart: 42, of which 25 were waited for; matrix products, arithmetic and copies ran while one was open for 15% of the time, Pallas kernels for 36%

profile of v1, /device:TPU:0, one launch (start us, length us, event | category | flops | bytes accessed | tf_op | source)
XLA Modules:
  0.0 268.5 jit_solution(10545696698215271962)
XLA Ops:
  3.3 10.0 %shard_map.204 = (bf16[1024,768]{1,0:T(8,128)(2,1)}, bf16[1024,768]{1,0:T(8,128)(2,1)}, bf16[256,768]{1,0:T(8,128)(2,1)}, bf16[768,1536]{1,0:T(8,128)(2,1)}, f32...) custom-call(s32[1]{0:T(128)S(6)} %copy.98.context_ref.at_ref, s32[1]{0:T(128)S(6)} %copy.99.queries_ref, ...), custom_call_target="tpu_custom_call" | custom-call | flops 37748736 | bytes 172032 | tf_op jit(solution)/shard_map/pallas_call | solution.py:186
  13.8 9.4 %shard_map.205 = (bf16[256,768]{1,0:T(8,128)(2,1)}, f32[256,768]{1,0:T(8,128)}, f32[256,768]{1,0:T(8,128)}, f32[256,1]{1,0:T(8,128)}, f32[256,768]{1,0:T(8,128)}) custom-call(bf16[256,768]{1,0:T(8,128)(2,1)} %get-tuple-element.145.query_ref, bf16[768,1536]{1,0:T(8,128)(2,1)} %get-tuple-element.146.key_ref.value_ref, ...), custom_call_target="tpu_custom_call" | custom-call | flops 37748736 | bytes 73728 | tf_op jit(solution)/shard_map/pallas_call | solution.py:256
  23.2 2.4 collective-permute-done.got_ref
  26.5 13.2 %shard_map.206 = (f32[4,192,256]{2,1,0:T(8,128)}, f32[4,192,256]{2,1,0:T(8,128)}, f32[4,192,512]{2,1,0:T(8,128)}, f32[4,192,512]{2,1,0:T(8,128)}, f32[2,384,256]...) custom-call(s32[1]{0:T(128)} %bitcast.at_ref.me_ref, ...), custom_call_target="tpu_custom_call" | custom-call | flops 75497472 | bytes 221184 | tf_op jit(solution)/shard_map/pallas_call | solution.py:352
  39.9 2.8 %collective-permute-start.3 = (f32[4,192,256]{2,1,0:T(8,128)}, f32[4,192,256]{2,1,0:T(8,128)S(1)}, u32[]{:S(2)}, u32[]{:S(2)}) collective-permute-start(f32[4,192,256]{2,1,0:T(8,128)} %get-tuple-element.162), channel_id=1, source_target_pairs={{0,2},{1,3},{2,0},{3,1},{4,6},{5,7},{6,4},{7,5},{8,10},{9,11},{10,... | collective-permute-start | bytes 2359304 | tf_op jit(solution)/shard_map/ppermute | solution.py:810
  45.2 12.2 %shard_map.207 = (bf16[256,768]{1,0:T(8,128)(2,1)}, bf16[768,768]{1,0:T(8,128)(2,1)}, bf16[768,768]{1,0:T(8,128)(2,1)}, f32[256,768]{1,0:T(8,128)}, bf16[256,768]{1,0:T(8,128)(2,1)}, /*index=5*/f32[2,768]{1,0:T(2,128)}) custom-call(bf16[256,768]{1,0:T(8,128)(2,1)} %get-tuple-element.145.query_ref, bf16[768,1536]{1,0:T(8,128)(2,1)} %get-tuple-element.146.key_ref.value_ref, ...), custom_call_target="tpu_custom_call" | custom-call | flops 94371840 | bytes 92160 | tf_op jit(solution)/shard_map/pallas_call | solution.py:500
  57.5 7.7 %shard_map.208 = (f32[768,768]{1,0:T(8,128)}, f32[768,768]{1,0:T(8,128)}, f32[768,768]{1,0:T(8,128)}, f32[768,768]{1,0:T(8,128)}) custom-call(s32[1]{0:T(128)} %bitcast.at_ref.me_ref, bf16[1024,768]{1,0:T(8,128)(2,1)} %get-tuple-element.144.norm_ref, bf16[256,768]{1,0:T(8,128)(2,1)} %get-tuple-element.150.attended_ref, ...), custom_call_target="tpu_custom_call" | custom-call | flops 37748736 | bytes 184320 | tf_op jit(solution)/shard_map/pallas_call | solution.py:582
  70.1 2.1 dynamic-slice_add_fusion.1
  73.5 3.0 %dynamic-slice_add_fusion = (f32[1,2,2,2,48,768]{5,4,3,2,1,0:T(8,128)}, f32[1,2,2,2,48,768]{5,4,3,2,1,0:T(8,128)S(1)}, f32[1,2,2,2,48,768]{5,4,3,2,1,0:T(8,128)S(1)}) fusion(f32[2,2,2,2,48,768]{5,4,3,2,1,0:T(8,128)} %bitcast.9, s32[]{:T(128)S(6)} %select_n.137, f32[2,2,2,2,48,768]{5,4,3,2,1,0:T(8,128)S(1)} %bitcast.203, s32[]{:T(128)S(6)} %select_n.139), kind=kLoop, calls=%fused_computation.22 | loop fusion | flops 294912 | bytes 8257544 | tf_op jit(solution)/shard_map/add | solution.py:864
  83.7 4.9 %shard_map.210 = (f32[256,768]{1,0:T(8,128)}, f32[256,768]{1,0:T(8,128)}) custom-call(s32[1]{0:T(128)} %bitcast.at_ref.me_ref, bf16[512,1536]{1,0:T(8,128)(2,1)} %get-tuple-element.185.left_ref, bf16[3072,768]{1,0:T(8,128)(2,1)} %refs_11_.1), custom_call_target="tpu_custom_call" | custom-call | flops 18874368 | bytes 73728 | tf_op jit(solution)/shard_map/pallas_call | solution.py:409
  88.5 3.9 %collective-permute-done.11 = f32[2,2,96,256]{3,2,0,1:T(8,128)} collective-permute-done((f32[2,2,96,256]{3,2,0,1:T(8,128)}, f32[2,2,96,256]{3,2,0,1:T(8,128)}, u32[]{:S(2)}, u32[]{:S(2)}) %collective-permute-start.11) | collective-permute-done | bytes 393248 | tf_op jit(solution)/shard_map/ppermute | solution.py:810
  96.8 8.9 %shard_map.209 = (f32[1024,768]{1,0:T(8,128)}, f32[2,768]{1,0:T(2,128)}) custom-call(bf16[256,768]{1,0:T(8,128)(2,1)} %get-tuple-element.178.dq_ref, bf16[768,768]{1,0:T(8,128)(2,1)} %get-tuple-element.179.dk_ref, bf16[768,768]{1,0:T(8,128)(2,1)} %get-tuple-element.180.dv_ref, bf16[1024,768]{1,0:T(8,128)(2,1)} %get-tuple-element.149.rows_ref, ...), custom_call_target="tpu_custom_call" | custom-call | flops 37748736 | bytes 147456 | tf_op jit(solution)/shard_map/pallas_call | solution.py:630
  105.7 3.4 %convolution_convert_fusion.query_ref = bf16[768,768]{1,0:T(8,128)(2,1)} fusion(bf16[768,768]{1,0:T(8,128)(2,1)S(1)} %copy-done.17, bf16[768,2304]{1,0:T(8,128)(2,1)} %wv.1), kind=kOutput, calls=%fused_computation.6 | convolution fusion | flops 906559488 | bytes 3538944 | tf_op jit(solution)/shard_map/dot_general | solution.py:28
  111.8 2.3 bitcast_add_fusion.2
  115.9 9.7 %shard_map.211 = (bf16[256,768]{1,0:T(8,128)(2,1)}, f32[256,768]{1,0:T(8,128)}, f32[256,768]{1,0:T(8,128)}, f32[256,1]{1,0:T(8,128)}) custom-call(bf16[768,768]{1,0:T(8,128)(2,1)} %convolution_convert_fusion.query_ref, bf16[768,1536]{1,0:T(8,128)(2,1)} %get-tuple-element.146.key_ref.value_ref, bf16[768,1536]{1,0:T(8,128)(2,1)} %get-tuple-element.146.key_ref.value_ref, ...), custom_call_target="tpu_custom_call" | custom-call | flops 37748736 | bytes 73728 | tf_op jit(solution)/shard_map/pallas_call | solution.py:256
  126.3 3.6 %collective-permute-done.14 = f32[2,2,48,768]{3,2,1,0:T(8,128)S(1)} collective-permute-done((f32[2,2,48,768]{3,2,1,0:T(8,128)S(1)}, f32[2,2,48,768]{3,2,1,0:T(8,128)S(1)}, u32[]{:S(2)}, u32[]{:S(2)}) %collective-permute-start.14) | collective-permute-done | bytes 589856 | tf_op jit(solution)/shard_map/ppermute | solution.py:810
  137.7 9.7 %shard_map.212 = (bf16[256,768]{1,0:T(8,128)(2,1)}, f32[256,768]{1,0:T(8,128)}, f32[256,768]{1,0:T(8,128)}, f32[256,1]{1,0:T(8,128)}) custom-call(bf16[768,768]{1,0:T(8,128)(2,1)} %convolution_convert_fusion.query_ref, bf16[768,1536]{1,0:T(8,128)(2,1)} %get-tuple-element.146.key_ref.value_ref, bf16[768,1536]{1,0:T(8,128)(2,1)} %get-tuple-element.146.key_ref.value_ref, ...), custom_call_target="tpu_custom_call" | custom-call | flops 37748736 | bytes 73728 | tf_op jit(solution)/shard_map/pallas_call | solution.py:256
  150.2 2.1 fusion.10
  152.4 9.6 %shard_map.213 = (bf16[256,768]{1,0:T(8,128)(2,1)}, f32[256,768]{1,0:T(8,128)}, f32[256,768]{1,0:T(8,128)}, f32[256,1]{1,0:T(8,128)}) custom-call(bf16[768,768]{1,0:T(8,128)(2,1)} %convolution_convert_fusion.query_ref, bf16[768,1536]{1,0:T(8,128)(2,1)} %get-tuple-element.146.key_ref.value_ref, bf16[768,1536]{1,0:T(8,128)(2,1)} %get-tuple-element.146.key_ref.value_ref, ...), custom_call_target="tpu_custom_call" | custom-call | flops 37748736 | bytes 73728 | tf_op jit(solution)/shard_map/pallas_call | solution.py:256
  162.0 4.4 %collective-permute-done.19 = f32[4,192,512]{2,1,0:T(8,128)} collective-permute-done((f32[4,192,512]{2,1,0:T(8,128)}, f32[4,192,512]{2,1,0:T(8,128)}, u32[]{:S(2)}, u32[]{:S(2)}) %collective-permute-start.19) | collective-permute-done | bytes 1572896 | tf_op jit(solution)/shard_map/ppermute | solution.py:810
  181.5 3.6 %collective-permute-done.23 = f32[2,2,96,256]{3,2,1,0:T(8,128)S(1)} collective-permute-done((f32[2,2,96,256]{3,2,1,0:T(8,128)S(1)}, f32[2,2,96,256]{3,2,1,0:T(8,128)S(1)}, u32[]{:S(2)}, u32[]{:S(2)}) %collective-permute-start.23) | collective-permute-done | bytes 393248 | tf_op jit(solution)/shard_map/ppermute | solution.py:810
  193.1 5.1 %collective-permute-done.27 = f32[8,768]{1,0:T(8,128)S(1)} collective-permute-done((f32[8,768]{1,0:T(8,128)}, f32[8,768]{1,0:T(8,128)S(1)}, u32[]{:S(2)}, u32[]{:S(2)}) %collective-permute-start.27) | collective-permute-done | bytes 24608 | tf_op jit(solution)/shard_map/ppermute | solution.py:810
  199.5 3.2 %collective-permute-done.29 = f32[2,2,96,256]{3,2,1,0:T(8,128)S(1)} collective-permute-done((f32[2,2,96,256]{3,2,1,0:T(8,128)}, f32[2,2,96,256]{3,2,1,0:T(8,128)S(1)}, u32[]{:S(2)}, u32[]{:S(2)}) %collective-permute-start.29) | collective-permute-done | bytes 393248 | tf_op jit(solution)/shard_map/ppermute | solution.py:810
  209.8 3.2 %fusion = f32[1024,768]{1,0:T(8,128)} fusion(s32[]{:T(128)S(6)} %select_n.153, f32[1024,768]{1,0:T(8,128)S(1)} %broadcast_multiply_fusion), kind=kLoop, calls=%fused_computation.2 | loop fusion | flops 786432 | bytes 6291460 | tf_op jit(solution)/shard_map/concatenate | solution.py:926
  213.0 6.4 %collective-permute-done.32 = f32[2,2,48,768]{3,2,1,0:T(8,128)S(1)} collective-permute-done((f32[2,2,48,768]{3,2,1,0:T(8,128)S(1)}, f32[2,2,48,768]{3,2,1,0:T(8,128)S(1)}, u32[]{:S(2)}, u32[]{:S(2)}) %collective-permute-start.32) | collective-permute-done | bytes 589856 | tf_op jit(solution)/shard_map/ppermute | solution.py:810
  220.8 5.4 %collective-permute-done.33 = f32[4,2,96,256]{3,2,0,1:T(8,128)S(1)} collective-permute-done((f32[4,2,96,256]{3,2,0,1:T(8,128)S(1)}, f32[4,2,96,256]{3,2,0,1:T(8,128)S(1)}, u32[]{:S(2)}, u32[]{:S(2)}) %collective-permute-start.33) | collective-permute-done | bytes 786464 | tf_op jit(solution)/shard_map/ppermute | solution.py:810
  229.5 3.1 %shard_map.214 = (f32[768,2304]{1,0:T(8,128)}, f32[768,768]{1,0:T(8,128)}) custom-call(s32[1]{0:T(128)} %bitcast.at_ref.me_ref, f32[1,1]{1,0:T(1,128)} %div.6.factor_ref, f32[384,768]{1,0:T(8,128)} %bitcast.202, f32[384,768]{1,0:T(8,128)} %bitcast.199), custom_call_target="tpu_custom_call" | custom-call | bytes 73728 | tf_op jit(solution)/shard_map/pallas_call | solution.py:693
  232.7 15.1 %shard_map.216 = bf16[1024,768]{1,0:T(8,128)(2,1)} custom-call(s32[1]{0:T(128)S(6)} %copy.98.context_ref.at_ref, f32[256,768]{1,0:T(8,128)} %get-tuple-element.256.refs_0_, f32[256,768]{1,0:T(8,128)} %get-tuple-element.257.refs_1_, f32[256,768]{1,0:T(8,128)} %get-tuple-element.258.refs_2_, f32[256,768]{1,0:T(8,128)} %get-tuple-element.259.refs_3_, ...), custom_call_target="tpu_custom_call" | custom-call | flops 7247757312 | bytes 18874368 | tf_op jit(solution)/shard_map/pallas_call | solution.py:752
  247.8 3.2 %shard_map.215 = (f32[768,2304]{1,0:T(8,128)}, f32[768,768]{1,0:T(8,128)}) custom-call(s32[1]{0:T(128)} %bitcast.at_ref.me_ref, f32[1,1]{1,0:T(1,128)} %div.6.factor_ref, f32[384,768]{1,0:T(8,128)} %collective-permute-done.37.a_ref, f32[384,768]{1,0:T(8,128)} %collective-permute-done.38.b_ref, ...), custom_call_target="tpu_custom_call", output_to_operand_aliasing={{0}: (4, {}), {1}: (5, {})} | custom-call | bytes 73728 | tf_op jit(solution)/shard_map/pallas_call | solution.py:693
  251.3 3.4 %collective-permute-done.35.b_ref = f32[384,768]{1,0:T(8,128)} collective-permute-done((f32[384,768]{1,0:T(8,128)S(1)}, f32[384,768]{1,0:T(8,128)}, u32[]{:S(2)}, u32[]{:S(2)}) %collective-permute-start.35) | collective-permute-done | bytes 1179680 | tf_op jit(solution)/shard_map/ppermute | solution.py:810
  258.0 3.1 %shard_map.217 = (f32[768,2304]{1,0:T(8,128)}, f32[768,768]{1,0:T(8,128)}) custom-call(s32[1]{0:T(128)} %bitcast.at_ref.me_ref, f32[1,1]{1,0:T(1,128)} %div.6.factor_ref, f32[384,768]{1,0:T(8,128)} %collective-permute-done.34.a_ref, f32[384,768]{1,0:T(8,128)} %collective-permute-done.35.b_ref, ...), custom_call_target="tpu_custom_call", output_to_operand_aliasing={{0}: (4, {}), {1}: (5, {})} | custom-call | bytes 73728 | tf_op jit(solution)/shard_map/pallas_call | solution.py:693
  265.1 3.2 %shard_map.218 = (f32[768,2304]{1,0:T(8,128)}, f32[768,768]{1,0:T(8,128)}) custom-call(s32[1]{0:T(128)} %bitcast.at_ref.me_ref, f32[1,1]{1,0:T(1,128)} %div.6.factor_ref, f32[384,768]{1,0:T(8,128)} %copy-done.15, f32[384,768]{1,0:T(8,128)} %copy-done.16, f32[768,2304]{1,0:T(8,128)} %get-tuple-element.272.refs_0_, ...), custom_call_target="tpu_custom_call", output_to_operand_aliasing={{0}: (4, {}), {1}: (5, {})} | custom-call | bytes 73728 | tf_op jit(solution)/shard_map/pallas_call | solution.py:693
  (195 shorter events, 81.8 us)
Async XLA Ops:
  13.3 9.9 %collective-permute-start.1 = (f32[256,768]{1,0:T(8,128)}, f32[256,768]{1,0:T(8,128)S(1)}, u32[]{:S(2)}, u32[]{:S(2)}) collective-permute-start(f32[256,768]{1,0:T(8,128)} %get-tuple-element.153.grad_ref.upstream_ref), channel_id=1, source_target_pairs={{0,1},{1,0},{2,3},{3,2},{4,5},{5,4},{6,7},{7,6},{8,9},{9,8},{10,11... | collective-permute-start | bytes 2359304 | tf_op jit(solution)/shard_map/ppermute | solution.py:810
  39.9 25.3 %collective-permute-start.3 = (f32[4,192,256]{2,1,0:T(8,128)}, f32[4,192,256]{2,1,0:T(8,128)S(1)}, u32[]{:S(2)}, u32[]{:S(2)}) collective-permute-start(f32[4,192,256]{2,1,0:T(8,128)} %get-tuple-element.162), channel_id=1, source_target_pairs={{0,2},{1,3},{2,0},{3,1},{4,6},{5,7},{6,4},{7,5},{8,10},{9,11},{10,... | collective-permute-start | bytes 2359304 | tf_op jit(solution)/shard_map/ppermute | solution.py:810
  42.7 22.5 %collective-permute-start.4 = (f32[2,384,256]{2,1,0:T(8,128)}, f32[2,384,256]{2,1,0:T(8,128)S(1)}, u32[]{:S(2)}, u32[]{:S(2)}) collective-permute-start(f32[2,384,256]{2,1,0:T(8,128)} %get-tuple-element.163), channel_id=1, source_target_pairs={{0,4},{1,5},{2,6},{3,7},{4,0},{5,1},{6,2},{7,3},{8,12},{9,13},{10,... | collective-permute-start | bytes 2359304 | tf_op jit(solution)/shard_map/ppermute | solution.py:810
  65.3 8.2 %collective-permute-start.6 = (f32[768,768]{1,0:T(8,128)}, f32[768,768]{1,0:T(8,128)}, u32[]{:S(2)}, u32[]{:S(2)}) collective-permute-start(f32[768,768]{1,0:T(8,128)} %get-tuple-element.168), channel_id=1, source_target_pairs={{0,1},{1,0},{2,3},{3,2},{4,5},{5,4},{6,7},{7,6},{8,9},{9,8},{10,11... | collective-permute-start | bytes 7077896 | tf_op jit(solution)/shard_map/ppermute | solution.py:810
  67.5 10.9 %collective-permute-start.8 = (f32[2,2,96,256]{3,2,1,0:T(8,128)S(1)}, f32[2,2,96,256]{3,2,1,0:T(8,128)S(1)}, u32[]{:S(2)}, u32[]{:S(2)}) collective-permute-start(f32[2,2,96,256]{3,2,1,0:T(8,128)S(1)} %get-tuple-element.315), channel_id=1, source_target_pairs={{0,2},{1,3},{2,0},{3,1},{4,6},{5,7},{6,4},{7,5},{8,10},{9,11},{10,... | collective-permute-start | bytes 1179656 | tf_op jit(solution)/shard_map/ppermute | solution.py:810
  68.1 11.1 %collective-permute-start.7 = (f32[2,2,96,256]{3,2,1,0:T(8,128)S(1)}, f32[2,2,96,256]{3,2,1,0:T(8,128)S(1)}, u32[]{:S(2)}, u32[]{:S(2)}) collective-permute-start(f32[2,2,96,256]{3,2,1,0:T(8,128)S(1)} %get-tuple-element.332), channel_id=1, source_target_pairs={{0,4},{1,5},{2,6},{3,7},{4,0},{5,1},{6,2},{7,3},{8,12},{9,13},{10,... | collective-permute-start | bytes 1179656 | tf_op jit(solution)/shard_map/ppermute | solution.py:810
  79.2 30.1 %collective-permute-start.9 = (f32[2,2,2,48,768]{4,3,2,0,1:T(8,128)}, f32[2,2,2,48,768]{4,3,2,0,1:T(8,128)}, u32[]{:S(2)}, u32[]{:S(2)}) collective-permute-start(f32[2,2,2,48,768]{4,3,2,0,1:T(8,128)} %get-tuple-element.173), channel_id=1, source_target_pairs={{0,2},{1,3},{2,0},{3,1},{4,6},{5,7},{6,4},{7,5},{8,10},{9,11},{10,... | collective-permute-start | bytes 3538952 | tf_op jit(solution)/shard_map/ppermute | solution.py:810
  80.2 29.2 %collective-permute-start.10 = (f32[2,2,2,48,768]{4,3,2,0,1:T(8,128)}, f32[2,2,2,48,768]{4,3,2,0,1:T(8,128)}, u32[]{:S(2)}, u32[]{:S(2)}) collective-permute-start(f32[2,2,2,48,768]{4,3,2,0,1:T(8,128)} %get-tuple-element.174), channel_id=1, source_target_pairs={{0,4},{1,5},{2,6},{3,7},{4,0},{5,1},{6,2},{7,3},{8,12},{9,13},{10,... | collective-permute-start | bytes 3538952 | tf_op jit(solution)/shard_map/ppermute | solution.py:810
  82.1 10.3 %collective-permute-start.11 = (f32[2,2,96,256]{3,2,0,1:T(8,128)}, f32[2,2,96,256]{3,2,0,1:T(8,128)}, u32[]{:S(2)}, u32[]{:S(2)}) collective-permute-start(f32[2,2,96,256]{3,2,0,1:T(8,128)} %fusion.17), channel_id=1, source_target_pairs={{0,8},{1,9},{2,10},{3,11},{4,12},{5,13},{6,14},{7,15},{8,0},{9,1},... | collective-permute-start | bytes 1179656 | tf_op jit(solution)/shard_map/ppermute | solution.py:810
  88.5 20.5 %collective-permute-start.13 = (f32[256,768]{1,0:T(8,128)}, f32[256,768]{1,0:T(8,128)}, u32[]{:S(2)}, u32[]{:S(2)}) collective-permute-start(f32[256,768]{1,0:T(8,128)} %get-tuple-element.187), channel_id=1, source_target_pairs={{0,1},{1,0},{2,3},{3,2},{4,5},{5,4},{6,7},{7,6},{8,9},{9,8},{10,11... | collective-permute-start | bytes 2359304 | tf_op jit(solution)/shard_map/ppermute | solution.py:810
  94.4 15.0 %collective-permute-start.12 = (f32[2,2,96,256]{3,2,0,1:T(8,128)}, f32[2,2,96,256]{3,2,0,1:T(8,128)S(1)}, u32[]{:S(2)}, u32[]{:S(2)}) collective-permute-start(f32[2,2,96,256]{3,2,0,1:T(8,128)} %fusion.21), channel_id=1, source_target_pairs={{1,17},{3,19},{5,21},{7,23},{9,25},{11,27},{13,29},{15,31},{16,0},... | collective-permute-start | bytes 1179656 | tf_op jit(solution)/shard_map/ppermute | solution.py:892
  114.1 15.9 %collective-permute-start.14 = (f32[2,2,48,768]{3,2,1,0:T(8,128)S(1)}, f32[2,2,48,768]{3,2,1,0:T(8,128)S(1)}, u32[]{:S(2)}, u32[]{:S(2)}) collective-permute-start(f32[2,2,48,768]{3,2,1,0:T(8,128)S(1)} %get-tuple-element.193), channel_id=1, source_target_pairs={{0,4},{1,5},{2,6},{3,7},{4,0},{5,1},{6,2},{7,3},{8,12},{9,13},{10,... | collective-permute-start | bytes 1769480 | tf_op jit(solution)/shard_map/ppermute | solution.py:810
  114.5 15.7 %collective-permute-start.15 = (f32[2,2,48,768]{3,2,1,0:T(8,128)}, f32[2,2,48,768]{3,2,1,0:T(8,128)S(1)}, u32[]{:S(2)}, u32[]{:S(2)}) collective-permute-start(f32[2,2,48,768]{3,2,1,0:T(8,128)} %get-tuple-element.194), channel_id=1, source_target_pairs={{0,2},{1,3},{2,0},{3,1},{4,6},{5,7},{6,4},{7,5},{8,10},{9,11},{10,... | collective-permute-start | bytes 1769480 | tf_op jit(solution)/shard_map/ppermute | solution.py:810
  115.9 9.7 %collective-permute-start.16 = (f32[8,768]{1,0:T(8,128)S(1)}, f32[8,768]{1,0:T(8,128)S(1)}, u32[]{:S(2)}, u32[]{:S(2)}) collective-permute-start(f32[8,768]{1,0:T(8,128)S(1)} %maximum_maximum_fusion), channel_id=1, source_target_pairs={{0,1},{1,0},{2,3},{3,2},{4,5},{5,4},{6,7},{7,6},{8,9},{9,8},{10,11... | collective-permute-start | bytes 73736 | tf_op jit(solution)/shard_map/ppermute | solution.py:810
  130.2 36.2 %collective-permute-start.19 = (f32[4,192,512]{2,1,0:T(8,128)}, f32[4,192,512]{2,1,0:T(8,128)}, u32[]{:S(2)}, u32[]{:S(2)}) collective-permute-start(f32[4,192,512]{2,1,0:T(8,128)} %get-tuple-element.218), channel_id=1, source_target_pairs={{0,2},{1,3},{2,0},{3,1},{4,6},{5,7},{6,4},{7,5},{8,10},{9,11},{10,... | collective-permute-start | bytes 4718600 | tf_op jit(solution)/shard_map/ppermute | solution.py:810
  131.5 35.7 %collective-permute-start.20 = (f32[2,384,512]{2,1,0:T(8,128)}, f32[2,384,512]{2,1,0:T(8,128)}, u32[]{:S(2)}, u32[]{:S(2)}) collective-permute-start(f32[2,384,512]{2,1,0:T(8,128)} %get-tuple-element.219), channel_id=1, source_target_pairs={{0,4},{1,5},{2,6},{3,7},{4,0},{5,1},{6,2},{7,3},{8,12},{9,13},{10,... | collective-permute-start | bytes 4718600 | tf_op jit(solution)/shard_map/ppermute | solution.py:810
  133.8 16.4 %collective-permute-start.17 = (f32[2,2,48,768]{3,2,1,0:T(8,128)}, f32[2,2,48,768]{3,2,1,0:T(8,128)}, u32[]{:S(2)}, u32[]{:S(2)}) collective-permute-start(f32[2,2,48,768]{3,2,1,0:T(8,128)} %fusion.6), channel_id=1, source_target_pairs={{0,8},{1,9},{2,10},{3,11},{4,12},{5,13},{6,14},{7,15},{8,0},{9,1},... | collective-permute-start | bytes 1769480 | tf_op jit(solution)/shard_map/ppermute | solution.py:810
  135.4 13.4 %collective-permute-start.18 = (f32[8,768]{1,0:T(8,128)}, f32[8,768]{1,0:T(8,128)}, u32[]{:S(2)}, u32[]{:S(2)}) collective-permute-start(f32[8,768]{1,0:T(8,128)} %fusion.37), channel_id=1, source_target_pairs={{0,8},{1,9},{2,10},{3,11},{4,12},{5,13},{6,14},{7,15},{8,0},{9,1},... | collective-permute-start | bytes 73736 | tf_op jit(solution)/shard_map/ppermute | solution.py:810
  152.3 29.2 %collective-permute-start.25 = (f32[2,2,48,768]{3,2,1,0:T(8,128)}, f32[2,2,48,768]{3,2,1,0:T(8,128)S(1)}, u32[]{:S(2)}, u32[]{:S(2)}) collective-permute-start(f32[2,2,48,768]{3,2,1,0:T(8,128)} %fusion.10), channel_id=1, source_target_pairs={{0,16},{1,17},{2,18},{3,19},{4,20},{5,21},{6,22},{7,23},{8,24},{9,... | collective-permute-start | bytes 1769480 | tf_op jit(solution)/shard_map/ppermute | solution.py:810
  187.9 11.3 %collective-permute-start.26 = (f32[2,2,48,768]{3,2,1,0:T(8,128)S(1)}, f32[2,2,48,768]{3,2,1,0:T(8,128)S(1)}, u32[]{:S(2)}, u32[]{:S(2)}) collective-permute-start(f32[2,2,48,768]{3,2,1,0:T(8,128)S(1)} %add.382), channel_id=1, source_target_pairs={{0,8},{1,9},{2,10},{3,11},{4,12},{5,13},{6,14},{7,15},{8,0},{9,1},... | collective-permute-start | bytes 1769480 | tf_op jit(solution)/shard_map/ppermute | solution.py:810
  191.0 11.7 %collective-permute-start.29 = (f32[2,2,96,256]{3,2,1,0:T(8,128)}, f32[2,2,96,256]{3,2,1,0:T(8,128)S(1)}, u32[]{:S(2)}, u32[]{:S(2)}) collective-permute-start(f32[2,2,96,256]{3,2,1,0:T(8,128)} %get-tuple-element.303), channel_id=1, source_target_pairs={{0,4},{1,5},{2,6},{3,7},{4,0},{5,1},{6,2},{7,3},{8,12},{9,13},{10,... | collective-permute-start | bytes 1179656 | tf_op jit(solution)/shard_map/ppermute | solution.py:810
  191.7 11.3 %collective-permute-start.30 = (f32[2,2,96,256]{3,2,1,0:T(8,128)}, f32[2,2,96,256]{3,2,1,0:T(8,128)S(1)}, u32[]{:S(2)}, u32[]{:S(2)}) collective-permute-start(f32[2,2,96,256]{3,2,1,0:T(8,128)} %get-tuple-element.305), channel_id=1, source_target_pairs={{0,2},{1,3},{2,0},{3,1},{4,6},{5,7},{6,4},{7,5},{8,10},{9,11},{10,... | collective-permute-start | bytes 1179656 | tf_op jit(solution)/shard_map/ppermute | solution.py:810
  204.9 14.6 %collective-permute-start.32 = (f32[2,2,48,768]{3,2,1,0:T(8,128)S(1)}, f32[2,2,48,768]{3,2,1,0:T(8,128)S(1)}, u32[]{:S(2)}, u32[]{:S(2)}) collective-permute-start(f32[2,2,48,768]{3,2,1,0:T(8,128)S(1)} %get-tuple-element.320), channel_id=1, source_target_pairs={{0,2},{1,3},{2,0},{3,1},{4,6},{5,7},{6,4},{7,5},{8,10},{9,11},{10,... | collective-permute-start | bytes 1769480 | tf_op jit(solution)/shard_map/ppermute | solution.py:810
  206.2 14.2 %collective-permute-start.31 = (f32[2,2,48,768]{3,2,1,0:T(8,128)S(1)}, f32[2,2,48,768]{3,2,1,0:T(8,128)S(1)}, u32[]{:S(2)}, u32[]{:S(2)}) collective-permute-start(f32[2,2,48,768]{3,2,1,0:T(8,128)S(1)} %get-tuple-element.321), channel_id=1, source_target_pairs={{0,4},{1,5},{2,6},{3,7},{4,0},{5,1},{6,2},{7,3},{8,12},{9,13},{10,... | collective-permute-start | bytes 1769480 | tf_op jit(solution)/shard_map/ppermute | solution.py:810
  208.0 18.2 %collective-permute-start.33 = (f32[4,2,96,256]{3,2,0,1:T(8,128)S(1)}, f32[4,2,96,256]{3,2,0,1:T(8,128)S(1)}, u32[]{:S(2)}, u32[]{:S(2)}) collective-permute-start(f32[4,2,96,256]{3,2,0,1:T(8,128)S(1)} %get-tuple-element.282), channel_id=1, source_target_pairs={{0,8},{1,9},{2,10},{3,11},{4,12},{5,13},{6,14},{7,15},{8,0},{9,1},... | collective-permute-start | bytes 2359304 | tf_op jit(solution)/shard_map/ppermute | solution.py:810
  226.2 21.6 %collective-permute-start.38 = (f32[384,768]{1,0:T(8,128)S(1)}, f32[384,768]{1,0:T(8,128)}, u32[]{:S(2)}, u32[]{:S(2)}) collective-permute-start(f32[384,768]{1,0:T(8,128)S(1)} %bitcast.197), channel_id=1, source_target_pairs={{0,1},{1,0},{2,3},{3,2},{4,5},{5,4},{6,7},{7,6},{8,9},{9,8},{10,11... | collective-permute-start | bytes 3538952 | tf_op jit(solution)/shard_map/ppermute | solution.py:810
  226.2 21.6 %collective-permute-start.37 = (f32[384,768]{1,0:T(8,128)S(1)}, f32[384,768]{1,0:T(8,128)}, u32[]{:S(2)}, u32[]{:S(2)}) collective-permute-start(f32[384,768]{1,0:T(8,128)S(1)} %bitcast.200), channel_id=1, source_target_pairs={{0,1},{1,0},{2,3},{3,2},{4,5},{5,4},{6,7},{7,6},{8,9},{9,8},{10,11... | collective-permute-start | bytes 3538952 | tf_op jit(solution)/shard_map/ppermute | solution.py:810
  226.7 28.0 %collective-permute-start.35 = (f32[384,768]{1,0:T(8,128)S(1)}, f32[384,768]{1,0:T(8,128)}, u32[]{:S(2)}, u32[]{:S(2)}) collective-permute-start(f32[384,768]{1,0:T(8,128)S(1)} %bitcast.198), channel_id=1, source_target_pairs={{0,4},{1,5},{2,6},{3,7},{4,0},{5,1},{6,2},{7,3},{8,12},{9,13},{10,... | collective-permute-start | bytes 3538952 | tf_op jit(solution)/shard_map/ppermute | solution.py:810
  227.3 27.7 %collective-permute-start.34 = (f32[384,768]{1,0:T(8,128)S(1)}, f32[384,768]{1,0:T(8,128)}, u32[]{:S(2)}, u32[]{:S(2)}) collective-permute-start(f32[384,768]{1,0:T(8,128)S(1)} %bitcast.201), channel_id=1, source_target_pairs={{0,2},{1,3},{2,0},{3,1},{4,6},{5,7},{6,4},{7,5},{8,10},{9,11},{10,... | collective-permute-start | bytes 3538952 | tf_op jit(solution)/shard_map/ppermute | solution.py:810
  228.2 23.0 %collective-permute-start.36 = (f32[4,2,96,256]{3,2,0,1:T(8,128)S(1)}, f32[4,2,96,256]{3,2,0,1:T(8,128)}, u32[]{:S(2)}, u32[]{:S(2)}) collective-permute-start(f32[4,2,96,256]{3,2,0,1:T(8,128)S(1)} %add.404), channel_id=1, source_target_pairs={{1,17},{3,19},{5,21},{7,23},{9,25},{11,27},{13,29},{15,31},{16,0},... | collective-permute-start | bytes 2359304 | tf_op jit(solution)/shard_map/ppermute | solution.py:892
  255.0 8.7 %collective-permute-start.39 = (f32[384,768]{1,0:T(8,128)}, f32[384,768]{1,0:T(8,128)S(1)}, u32[]{:S(2)}, u32[]{:S(2)}) collective-permute-start(f32[384,768]{1,0:T(8,128)} %collective-permute-done.34.a_ref), channel_id=1, source_target_pairs={{0,1},{1,0},{2,3},{3,2},{4,5},{5,4},{6,7},{7,6},{8,9},{9,8},{10,11... | collective-permute-start | bytes 3538952 | tf_op jit(solution)/shard_map/ppermute | solution.py:810
  255.0 8.7 %collective-permute-start.40 = (f32[384,768]{1,0:T(8,128)}, f32[384,768]{1,0:T(8,128)S(1)}, u32[]{:S(2)}, u32[]{:S(2)}) collective-permute-start(f32[384,768]{1,0:T(8,128)} %collective-permute-done.35.b_ref), channel_id=1, source_target_pairs={{0,1},{1,0},{2,3},{3,2},{4,5},{5,4},{6,7},{7,6},{8,9},{9,8},{10,11... | collective-permute-start | bytes 3538952 | tf_op jit(solution)/shard_map/ppermute | solution.py:810
  (47 other events, 229.2 us)

commit v2 on v1

--- a/solution.py
+++ b/solution.py
@@ -1046,22 +1046,31 @@
         chain.go(order[1])
     ones = hand_over(ones)
     small = small + swap(small, top)
+    early = joined(early)
+    for bit in ff_bits[2:3]:
+        early.split(bit)
+        early.sent, small = tie((early.sent, small))
+        early.go(bit)
     value, small, ones, part_one, late_got = tie((value, small, ones, part_one, got_of(late)))
     set_got(late, late_got)
-    twos = joined(early + late)
+    late = joined(late)
     loss_factor = math.sqrt(devices) * (slots // 4) / small[4, 0]
     factor = loss_factor.reshape(1, 1)
 
     first_value = widen(value[0], first_bits[1], 0)
     second_value = widen(value[1], second_bits[1], 0)
-    for bit in ff_bits[2:]:
-        twos.split(bit)
-        twos.go(bit)
+    for bit in ff_bits[2:3]:
+        late.send(bit)
+    for bit in ff_bits[3:]:
+        early.send(bit)
+        late.send(bit)
     grad_inputs = unroll(grad_rows * loss_factor)
     small = small * loss_factor
-    first_value, second_value, grad_inputs, small, part_one, twos.terms = tie(
-        (first_value, second_value, grad_inputs, small, part_one, twos.terms)
-    )
+    first_value, second_value, grad_inputs, small, part_one, early.terms, late.terms = tie(
+        (first_value, second_value, grad_inputs, small, part_one, early.terms, late.terms)
+    )
+    terms = [jnp.concatenate(pair, axis=0) for pair in zip(early.terms, late.terms)]
+    twos = Halving(terms, early.axes)
 
     first_value, second_value = first_value.reshape(-1, width), second_value.reshape(-1, width)
     first_far = swap(first_value, first_bits[0])

time: 270 us -> 266 us (0.985)
  waiting for transfers between devices: 53.2 us -> 42.6 us
  starting transfers between devices: 34.7 us -> 40.4 us
    ppermute x40 -> x41, waiting for transfers between devices: 52.6 us -> 42 us  [swap(): return lax.ppermute(value, 'rows', [(i, i ^ bit) for i in range(devices)])]
    ppermute x40 -> x41, starting transfers between devices: 32.1 us -> 37.8 us  [swap(): return lax.ppermute(value, 'rows', [(i, i ^ bit) for i in range(devices)])]
    unnamed x74 -> x64, local copies, waits for them, and re-layouts: 6.69 us -> 5.3 us
    add x9 -> x10, other arithmetic: 13.1 us -> 14 us  [split(): self.kept = sum((pick(term, axis, mine) for term in self.terms))]
  transfers between devices with their start and end apart: 42 -> 43, of which waited for: 25 -> 21; matrix products, arithmetic and copies ran while one was open for 15% -> 16% of each run, Pallas kernels for 36% -> 37%
where the time goes in v2:
time: 266 us; the launch traced here: 264 us
  Pallas kernels  123 us (46%)
  waiting for transfers between devices  42.6 us (16%)
  starting transfers between devices  40.4 us (15%)
  other arithmetic  38.6 us (15%)
  local copies, waits for them, and re-layouts  12.6 us (5%)
  matrix products  3.76 us (1%)
  between operations  3.38 us (1%)
    ppermute x41, waiting for transfers between devices, swap(): return lax.ppermute(value, 'rows', [(i, i ^ bit) for i in range(devices)])  42 us
    pallas_call x4, Pallas kernels, attend(): pl.pallas_call(partial(attend_kernel, keep_logs), grid=(slots // block, p...  38.3 us
    ppermute x41, starting transfers between devices, swap(): return lax.ppermute(value, 'rows', [(i, i ^ bit) for i in range(devices)])  37.8 us
    pallas_call x1, Pallas kernels, output(): pl.pallas_call(output_kernel, grid_spec=pltpu.PrefetchScalarGridSpec(num_...  15.1 us
    add x10, other arithmetic, split(): self.kept = sum((pick(term, axis, mine) for term in self.terms))  14 us
    pallas_call x1, Pallas kernels, units(): pl.pallas_call(partial(units_kernel, bits), grid_spec=pltpu.PrefetchScala...  13.2 us
    pallas_call x4, Pallas kernels, put(): pl.pallas_call(partial(place_kernel, bits, far, got), in_specs=[scalar, s...  12.6 us
    pallas_call x1, Pallas kernels, attend_back(): pl.pallas_call(attend_back_kernel, grid=(pairs,), in_specs=[rows_spec, ke...  12.2 us
  transfers between devices with their start and end apart: 43, of which 21 were waited for; matrix products, arithmetic and copies ran while one was open for 16% of the time, Pallas kernels for 37%

profile of v2, /device:TPU:0, one launch (start us, length us, event | category | flops | bytes accessed | tf_op | source)
XLA Modules:
  0.0 264.0 jit_solution(4907621317498147690)
XLA Ops:
  3.3 10.0 %shard_map.204 = (bf16[1024,768]{1,0:T(8,128)(2,1)}, bf16[1024,768]{1,0:T(8,128)(2,1)}, bf16[256,768]{1,0:T(8,128)(2,1)}, bf16[768,1536]{1,0:T(8,128)(2,1)}, f32...) custom-call(s32[1]{0:T(128)S(6)} %copy.98.context_ref.at_ref, s32[1]{0:T(128)S(6)} %copy.99.queries_ref, ...), custom_call_target="tpu_custom_call" | custom-call | flops 37748736 | bytes 172032 | tf_op jit(solution)/shard_map/pallas_call | solution.py:186
  13.7 9.4 %shard_map.205 = (bf16[256,768]{1,0:T(8,128)(2,1)}, f32[256,768]{1,0:T(8,128)}, f32[256,768]{1,0:T(8,128)}, f32[256,1]{1,0:T(8,128)}, f32[256,768]{1,0:T(8,128)}) custom-call(bf16[256,768]{1,0:T(8,128)(2,1)} %get-tuple-element.149.query_ref, bf16[768,1536]{1,0:T(8,128)(2,1)} %get-tuple-element.150.key_ref.value_ref, ...), custom_call_target="tpu_custom_call" | custom-call | flops 37748736 | bytes 73728 | tf_op jit(solution)/shard_map/pallas_call | solution.py:256
  23.2 2.4 collective-permute-done.got_ref
  26.4 13.2 %shard_map.206 = (f32[4,192,256]{2,1,0:T(8,128)}, f32[4,192,256]{2,1,0:T(8,128)}, f32[4,192,512]{2,1,0:T(8,128)}, f32[4,192,512]{2,1,0:T(8,128)}, f32[2,384,256]...) custom-call(s32[1]{0:T(128)} %bitcast.at_ref.me_ref, ...), custom_call_target="tpu_custom_call" | custom-call | flops 75497472 | bytes 221184 | tf_op jit(solution)/shard_map/pallas_call | solution.py:352
  39.9 2.9 %collective-permute-start.3 = (f32[4,192,256]{2,1,0:T(8,128)}, f32[4,192,256]{2,1,0:T(8,128)S(1)}, u32[]{:S(2)}, u32[]{:S(2)}) collective-permute-start(f32[4,192,256]{2,1,0:T(8,128)} %get-tuple-element.166), channel_id=1, source_target_pairs={{0,2},{1,3},{2,0},{3,1},{4,6},{5,7},{6,4},{7,5},{8,10},{9,11},{10,... | collective-permute-start | bytes 2359304 | tf_op jit(solution)/shard_map/ppermute | solution.py:810
  45.2 12.2 %shard_map.207 = (bf16[256,768]{1,0:T(8,128)(2,1)}, bf16[768,768]{1,0:T(8,128)(2,1)}, bf16[768,768]{1,0:T(8,128)(2,1)}, f32[256,768]{1,0:T(8,128)}, bf16[256,768]{1,0:T(8,128)(2,1)}, /*index=5*/f32[2,768]{1,0:T(2,128)}) custom-call(bf16[256,768]{1,0:T(8,128)(2,1)} %get-tuple-element.149.query_ref, bf16[768,1536]{1,0:T(8,128)(2,1)} %get-tuple-element.150.key_ref.value_ref, ...), custom_call_target="tpu_custom_call" | custom-call | flops 94371840 | bytes 92160 | tf_op jit(solution)/shard_map/pallas_call | solution.py:500
  57.4 7.7 %shard_map.208 = (f32[768,768]{1,0:T(8,128)}, f32[768,768]{1,0:T(8,128)}, f32[768,768]{1,0:T(8,128)}, f32[768,768]{1,0:T(8,128)}) custom-call(s32[1]{0:T(128)} %bitcast.at_ref.me_ref, bf16[1024,768]{1,0:T(8,128)(2,1)} %get-tuple-element.148.norm_ref, bf16[256,768]{1,0:T(8,128)(2,1)} %get-tuple-element.154.attended_ref, ...), custom_call_target="tpu_custom_call" | custom-call | flops 37748736 | bytes 184320 | tf_op jit(solution)/shard_map/pallas_call | solution.py:582
  70.1 2.1 dynamic-slice_add_fusion.1
  73.4 2.0 dynamic-slice_add_fusion
  84.8 4.9 %shard_map.210 = (f32[256,768]{1,0:T(8,128)}, f32[256,768]{1,0:T(8,128)}) custom-call(s32[1]{0:T(128)} %bitcast.at_ref.me_ref, bf16[512,1536]{1,0:T(8,128)(2,1)} %get-tuple-element.189.left_ref, bf16[3072,768]{1,0:T(8,128)(2,1)} %refs_11_.1), custom_call_target="tpu_custom_call" | custom-call | flops 18874368 | bytes 73728 | tf_op jit(solution)/shard_map/pallas_call | solution.py:409
  89.7 3.6 %collective-permute-done.11 = f32[2,2,96,256]{3,2,0,1:T(8,128)} collective-permute-done((f32[2,2,96,256]{3,2,0,1:T(8,128)}, f32[2,2,96,256]{3,2,0,1:T(8,128)}, u32[]{:S(2)}, u32[]{:S(2)}) %collective-permute-start.11) | collective-permute-done | bytes 393248 | tf_op jit(solution)/shard_map/ppermute | solution.py:810
  93.3 2.0 fusion.37
  97.6 8.8 %shard_map.209 = (f32[1024,768]{1,0:T(8,128)}, f32[2,768]{1,0:T(2,128)}) custom-call(bf16[256,768]{1,0:T(8,128)(2,1)} %get-tuple-element.182.dq_ref, bf16[768,768]{1,0:T(8,128)(2,1)} %get-tuple-element.183.dk_ref, bf16[768,768]{1,0:T(8,128)(2,1)} %get-tuple-element.184.dv_ref, bf16[1024,768]{1,0:T(8,128)(2,1)} %get-tuple-element.153.rows_ref, ...), custom_call_target="tpu_custom_call" | custom-call | flops 37748736 | bytes 147456 | tf_op jit(solution)/shard_map/pallas_call | solution.py:630
  106.5 3.8 %convolution_convert_fusion.query_ref = bf16[768,768]{1,0:T(8,128)(2,1)} fusion(bf16[768,768]{1,0:T(8,128)(2,1)} %slice.69, bf16[768,2304]{1,0:T(8,128)(2,1)} %wv.1), kind=kOutput, calls=%fused_computation.4 | convolution fusion | flops 906559488 | bytes 3538944 | tf_op jit(solution)/shard_map/dot_general | solution.py:28
  112.4 2.2 bitcast_add_fusion.2
  117.0 9.6 %shard_map.211 = (bf16[256,768]{1,0:T(8,128)(2,1)}, f32[256,768]{1,0:T(8,128)}, f32[256,768]{1,0:T(8,128)}, f32[256,1]{1,0:T(8,128)}) custom-call(bf16[768,768]{1,0:T(8,128)(2,1)} %convolution_convert_fusion.query_ref, bf16[768,1536]{1,0:T(8,128)(2,1)} %get-tuple-element.150.key_ref.value_ref, bf16[768,1536]{1,0:T(8,128)(2,1)} %get-tuple-element.150.key_ref.value_ref, ...), custom_call_target="tpu_custom_call" | custom-call | flops 37748736 | bytes 73728 | tf_op jit(solution)/shard_map/pallas_call | solution.py:256
  127.3 3.4 %collective-permute-done.14 = f32[2,2,48,768]{3,2,1,0:T(8,128)S(1)} collective-permute-done((f32[2,2,48,768]{3,2,1,0:T(8,128)S(1)}, f32[2,2,48,768]{3,2,1,0:T(8,128)S(1)}, u32[]{:S(2)}, u32[]{:S(2)}) %collective-permute-start.14) | collective-permute-done | bytes 589856 | tf_op jit(solution)/shard_map/ppermute | solution.py:810
  138.9 9.7 %shard_map.212 = (bf16[256,768]{1,0:T(8,128)(2,1)}, f32[256,768]{1,0:T(8,128)}, f32[256,768]{1,0:T(8,128)}, f32[256,1]{1,0:T(8,128)}) custom-call(bf16[768,768]{1,0:T(8,128)(2,1)} %convolution_convert_fusion.query_ref, bf16[768,1536]{1,0:T(8,128)(2,1)} %get-tuple-element.150.key_ref.value_ref, bf16[768,1536]{1,0:T(8,128)(2,1)} %get-tuple-element.150.key_ref.value_ref, ...), custom_call_target="tpu_custom_call" | custom-call | flops 37748736 | bytes 73728 | tf_op jit(solution)/shard_map/pallas_call | solution.py:256
  151.6 2.1 fusion.10
  153.7 9.6 %shard_map.213 = (bf16[256,768]{1,0:T(8,128)(2,1)}, f32[256,768]{1,0:T(8,128)}, f32[256,768]{1,0:T(8,128)}, f32[256,1]{1,0:T(8,128)}) custom-call(bf16[768,768]{1,0:T(8,128)(2,1)} %convolution_convert_fusion.query_ref, bf16[768,1536]{1,0:T(8,128)(2,1)} %get-tuple-element.150.key_ref.value_ref, bf16[768,1536]{1,0:T(8,128)(2,1)} %get-tuple-element.150.key_ref.value_ref, ...), custom_call_target="tpu_custom_call" | custom-call | flops 37748736 | bytes 73728 | tf_op jit(solution)/shard_map/pallas_call | solution.py:256
  163.4 4.2 %collective-permute-done.19 = f32[4,192,512]{2,1,0:T(8,128)} collective-permute-done((f32[4,192,512]{2,1,0:T(8,128)}, f32[4,192,512]{2,1,0:T(8,128)}, u32[]{:S(2)}, u32[]{:S(2)}) %collective-permute-start.19) | collective-permute-done | bytes 1572896 | tf_op jit(solution)/shard_map/ppermute | solution.py:810
  182.5 4.0 %collective-permute-done.23 = f32[2,2,96,256]{3,2,1,0:T(8,128)S(1)} collective-permute-done((f32[2,2,96,256]{3,2,1,0:T(8,128)S(1)}, f32[2,2,96,256]{3,2,1,0:T(8,128)S(1)}, u32[]{:S(2)}, u32[]{:S(2)}) %collective-permute-start.23) | collective-permute-done | bytes 393248 | tf_op jit(solution)/shard_map/ppermute | solution.py:810
  196.0 3.3 %collective-permute-done.27 = f32[8,768]{1,0:T(8,128)S(1)} collective-permute-done((f32[8,768]{1,0:T(8,128)}, f32[8,768]{1,0:T(8,128)S(1)}, u32[]{:S(2)}, u32[]{:S(2)}) %collective-permute-start.27) | collective-permute-done | bytes 24608 | tf_op jit(solution)/shard_map/ppermute | solution.py:810
  199.3 5.4 %collective-permute-start.33 = (f32[2,2,96,256]{3,2,0,1:T(8,128)S(1)}, f32[2,2,96,256]{3,2,0,1:T(8,128)S(1)}, u32[]{:S(2)}, u32[]{:S(2)}) collective-permute-start(f32[2,2,96,256]{3,2,0,1:T(8,128)S(1)} %get-tuple-element.251), channel_id=1, source_target_pairs={{0,8},{1,9},{2,10},{3,11},{4,12},{5,13},{6,14},{7,15},{8,0},{9,1},... | collective-permute-start | bytes 1179656 | tf_op jit(solution)/shard_map/ppermute | solution.py:810
  209.0 3.2 %fusion = f32[1024,768]{1,0:T(8,128)} fusion(s32[]{:T(128)S(6)} %select_n.156, f32[1024,768]{1,0:T(8,128)S(1)} %broadcast_multiply_fusion), kind=kLoop, calls=%fused_computation.2 | loop fusion | flops 786432 | bytes 6291460 | tf_op jit(solution)/shard_map/concatenate | solution.py:926
  212.8 7.0 %collective-permute-done.32 = f32[2,2,48,768]{3,2,1,0:T(8,128)S(1)} collective-permute-done((f32[2,2,48,768]{3,2,1,0:T(8,128)S(1)}, f32[2,2,48,768]{3,2,1,0:T(8,128)S(1)}, u32[]{:S(2)}, u32[]{:S(2)}) %collective-permute-start.32) | collective-permute-done | bytes 589856 | tf_op jit(solution)/shard_map/ppermute | solution.py:810
  225.5 3.1 %shard_map.214 = (f32[768,2304]{1,0:T(8,128)}, f32[768,768]{1,0:T(8,128)}) custom-call(s32[1]{0:T(128)} %bitcast.at_ref.me_ref, f32[1,1]{1,0:T(1,128)} %div.6.factor_ref, f32[384,768]{1,0:T(8,128)} %bitcast.206, f32[384,768]{1,0:T(8,128)} %bitcast.203), custom_call_target="tpu_custom_call" | custom-call | bytes 73728 | tf_op jit(solution)/shard_map/pallas_call | solution.py:693
  228.6 15.1 %shard_map.216 = bf16[1024,768]{1,0:T(8,128)(2,1)} custom-call(s32[1]{0:T(128)S(6)} %copy.98.context_ref.at_ref, f32[256,768]{1,0:T(8,128)} %get-tuple-element.264.refs_0_, f32[256,768]{1,0:T(8,128)} %get-tuple-element.265.refs_1_, f32[256,768]{1,0:T(8,128)} %get-tuple-element.266.refs_2_, f32[256,768]{1,0:T(8,128)} %get-tuple-element.267.refs_3_, ...), custom_call_target="tpu_custom_call" | custom-call | flops 7247757312 | bytes 18874368 | tf_op jit(solution)/shard_map/pallas_call | solution.py:752
  243.7 3.2 %shard_map.215 = (f32[768,2304]{1,0:T(8,128)}, f32[768,768]{1,0:T(8,128)}) custom-call(s32[1]{0:T(128)} %bitcast.at_ref.me_ref, f32[1,1]{1,0:T(1,128)} %div.6.factor_ref, f32[384,768]{1,0:T(8,128)} %collective-permute-done.38.a_ref, f32[384,768]{1,0:T(8,128)} %collective-permute-done.39.b_ref, ...), custom_call_target="tpu_custom_call", output_to_operand_aliasing={{0}: (4, {}), {1}: (5, {})} | custom-call | bytes 73728 | tf_op jit(solution)/shard_map/pallas_call | solution.py:693
  247.5 2.3 collective-permute-done.36.b_ref
  253.5 3.1 %shard_map.217 = (f32[768,2304]{1,0:T(8,128)}, f32[768,768]{1,0:T(8,128)}) custom-call(s32[1]{0:T(128)} %bitcast.at_ref.me_ref, f32[1,1]{1,0:T(1,128)} %div.6.factor_ref, f32[384,768]{1,0:T(8,128)} %collective-permute-done.35.a_ref, f32[384,768]{1,0:T(8,128)} %collective-permute-done.36.b_ref, ...), custom_call_target="tpu_custom_call", output_to_operand_aliasing={{0}: (4, {}), {1}: (5, {})} | custom-call | bytes 73728 | tf_op jit(solution)/shard_map/pallas_call | solution.py:693
  260.6 3.2 %shard_map.218 = (f32[768,2304]{1,0:T(8,128)}, f32[768,768]{1,0:T(8,128)}) custom-call(s32[1]{0:T(128)} %bitcast.at_ref.me_ref, f32[1,1]{1,0:T(1,128)} %div.6.factor_ref, f32[384,768]{1,0:T(8,128)} %copy-done.13, f32[384,768]{1,0:T(8,128)} %copy-done.14, f32[768,2304]{1,0:T(8,128)} %get-tuple-element.280.refs_0_, ...), custom_call_target="tpu_custom_call", output_to_operand_aliasing={{0}: (4, {}), {1}: (5, {})} | custom-call | bytes 73728 | tf_op jit(solution)/shard_map/pallas_call | solution.py:693
  (186 shorter events, 82.0 us)
Async XLA Ops:
  13.3 9.9 %collective-permute-start.1 = (f32[256,768]{1,0:T(8,128)}, f32[256,768]{1,0:T(8,128)S(1)}, u32[]{:S(2)}, u32[]{:S(2)}) collective-permute-start(f32[256,768]{1,0:T(8,128)} %get-tuple-element.157.grad_ref.upstream_ref), channel_id=1, source_target_pairs={{0,1},{1,0},{2,3},{3,2},{4,5},{5,4},{6,7},{7,6},{8,9},{9,8},{10,11... | collective-permute-start | bytes 2359304 | tf_op jit(solution)/shard_map/ppermute | solution.py:810
  39.9 25.2 %collective-permute-start.3 = (f32[4,192,256]{2,1,0:T(8,128)}, f32[4,192,256]{2,1,0:T(8,128)S(1)}, u32[]{:S(2)}, u32[]{:S(2)}) collective-permute-start(f32[4,192,256]{2,1,0:T(8,128)} %get-tuple-element.166), channel_id=1, source_target_pairs={{0,2},{1,3},{2,0},{3,1},{4,6},{5,7},{6,4},{7,5},{8,10},{9,11},{10,... | collective-permute-start | bytes 2359304 | tf_op jit(solution)/shard_map/ppermute | solution.py:810
  42.8 22.3 %collective-permute-start.4 = (f32[2,384,256]{2,1,0:T(8,128)}, f32[2,384,256]{2,1,0:T(8,128)S(1)}, u32[]{:S(2)}, u32[]{:S(2)}) collective-permute-start(f32[2,384,256]{2,1,0:T(8,128)} %get-tuple-element.167), channel_id=1, source_target_pairs={{0,4},{1,5},{2,6},{3,7},{4,0},{5,1},{6,2},{7,3},{8,12},{9,13},{10,... | collective-permute-start | bytes 2359304 | tf_op jit(solution)/shard_map/ppermute | solution.py:810
  67.5 11.0 %collective-permute-start.8 = (f32[2,2,96,256]{3,2,1,0:T(8,128)S(1)}, f32[2,2,96,256]{3,2,1,0:T(8,128)}, u32[]{:S(2)}, u32[]{:S(2)}) collective-permute-start(f32[2,2,96,256]{3,2,1,0:T(8,128)S(1)} %get-tuple-element.325), channel_id=1, source_target_pairs={{0,2},{1,3},{2,0},{3,1},{4,6},{5,7},{6,4},{7,5},{8,10},{9,11},{10,... | collective-permute-start | bytes 1179656 | tf_op jit(solution)/shard_map/ppermute | solution.py:810
  68.2 11.2 %collective-permute-start.7 = (f32[2,2,96,256]{3,2,1,0:T(8,128)S(1)}, f32[2,2,96,256]{3,2,1,0:T(8,128)}, u32[]{:S(2)}, u32[]{:S(2)}) collective-permute-start(f32[2,2,96,256]{3,2,1,0:T(8,128)S(1)} %get-tuple-element.342), channel_id=1, source_target_pairs={{0,4},{1,5},{2,6},{3,7},{4,0},{5,1},{6,2},{7,3},{8,12},{9,13},{10,... | collective-permute-start | bytes 1179656 | tf_op jit(solution)/shard_map/ppermute | solution.py:810
  79.5 30.8 %collective-permute-start.9 = (f32[2,2,2,48,768]{4,3,2,0,1:T(8,128)}, f32[2,2,2,48,768]{4,3,2,0,1:T(8,128)}, u32[]{:S(2)}, u32[]{:S(2)}) collective-permute-start(f32[2,2,2,48,768]{4,3,2,0,1:T(8,128)} %get-tuple-element.177), channel_id=1, source_target_pairs={{0,2},{1,3},{2,0},{3,1},{4,6},{5,7},{6,4},{7,5},{8,10},{9,11},{10,... | collective-permute-start | bytes 3538952 | tf_op jit(solution)/shard_map/ppermute | solution.py:810
  80.2 30.0 %collective-permute-start.10 = (f32[2,2,2,48,768]{4,3,2,0,1:T(8,128)}, f32[2,2,2,48,768]{4,3,2,0,1:T(8,128)}, u32[]{:S(2)}, u32[]{:S(2)}) collective-permute-start(f32[2,2,2,48,768]{4,3,2,0,1:T(8,128)} %get-tuple-element.178), channel_id=1, source_target_pairs={{0,4},{1,5},{2,6},{3,7},{4,0},{5,1},{6,2},{7,3},{8,12},{9,13},{10,... | collective-permute-start | bytes 3538952 | tf_op jit(solution)/shard_map/ppermute | solution.py:810
  83.3 10.0 %collective-permute-start.11 = (f32[2,2,96,256]{3,2,0,1:T(8,128)}, f32[2,2,96,256]{3,2,0,1:T(8,128)}, u32[]{:S(2)}, u32[]{:S(2)}) collective-permute-start(f32[2,2,96,256]{3,2,0,1:T(8,128)} %fusion.33), channel_id=1, source_target_pairs={{0,8},{1,9},{2,10},{3,11},{4,12},{5,13},{6,14},{7,15},{8,0},{9,1},... | collective-permute-start | bytes 1179656 | tf_op jit(solution)/shard_map/ppermute | solution.py:810
  89.7 20.5 %collective-permute-start.13 = (f32[256,768]{1,0:T(8,128)}, f32[256,768]{1,0:T(8,128)}, u32[]{:S(2)}, u32[]{:S(2)}) collective-permute-start(f32[256,768]{1,0:T(8,128)} %get-tuple-element.191), channel_id=1, source_target_pairs={{0,1},{1,0},{2,3},{3,2},{4,5},{5,4},{6,7},{7,6},{8,9},{9,8},{10,11... | collective-permute-start | bytes 2359304 | tf_op jit(solution)/shard_map/ppermute | solution.py:810
  95.2 15.0 %collective-permute-start.12 = (f32[2,2,96,256]{3,2,0,1:T(8,128)}, f32[2,2,96,256]{3,2,0,1:T(8,128)S(1)}, u32[]{:S(2)}, u32[]{:S(2)}) collective-permute-start(f32[2,2,96,256]{3,2,0,1:T(8,128)} %fusion.37), channel_id=1, source_target_pairs={{1,17},{3,19},{5,21},{7,23},{9,25},{11,27},{13,29},{15,31},{16,0},... | collective-permute-start | bytes 1179656 | tf_op jit(solution)/shard_map/ppermute | solution.py:892
  114.6 16.2 %collective-permute-start.14 = (f32[2,2,48,768]{3,2,1,0:T(8,128)S(1)}, f32[2,2,48,768]{3,2,1,0:T(8,128)S(1)}, u32[]{:S(2)}, u32[]{:S(2)}) collective-permute-start(f32[2,2,48,768]{3,2,1,0:T(8,128)S(1)} %get-tuple-element.197), channel_id=1, source_target_pairs={{0,4},{1,5},{2,6},{3,7},{4,0},{5,1},{6,2},{7,3},{8,12},{9,13},{10,... | collective-permute-start | bytes 1769480 | tf_op jit(solution)/shard_map/ppermute | solution.py:810
  115.2 15.8 %collective-permute-start.15 = (f32[2,2,48,768]{3,2,1,0:T(8,128)}, f32[2,2,48,768]{3,2,1,0:T(8,128)S(1)}, u32[]{:S(2)}, u32[]{:S(2)}) collective-permute-start(f32[2,2,48,768]{3,2,1,0:T(8,128)} %get-tuple-element.198), channel_id=1, source_target_pairs={{0,2},{1,3},{2,0},{3,1},{4,6},{5,7},{6,4},{7,5},{8,10},{9,11},{10,... | collective-permute-start | bytes 1769480 | tf_op jit(solution)/shard_map/ppermute | solution.py:810
  116.8 9.9 %collective-permute-start.16 = (f32[8,768]{1,0:T(8,128)S(1)}, f32[8,768]{1,0:T(8,128)S(1)}, u32[]{:S(2)}, u32[]{:S(2)}) collective-permute-start(f32[8,768]{1,0:T(8,128)S(1)} %maximum_maximum_fusion), channel_id=1, source_target_pairs={{0,1},{1,0},{2,3},{3,2},{4,5},{5,4},{6,7},{7,6},{8,9},{9,8},{10,11... | collective-permute-start | bytes 73736 | tf_op jit(solution)/shard_map/ppermute | solution.py:810
  131.0 36.6 %collective-permute-start.19 = (f32[4,192,512]{2,1,0:T(8,128)}, f32[4,192,512]{2,1,0:T(8,128)}, u32[]{:S(2)}, u32[]{:S(2)}) collective-permute-start(f32[4,192,512]{2,1,0:T(8,128)} %get-tuple-element.222), channel_id=1, source_target_pairs={{0,2},{1,3},{2,0},{3,1},{4,6},{5,7},{6,4},{7,5},{8,10},{9,11},{10,... | collective-permute-start | bytes 4718600 | tf_op jit(solution)/shard_map/ppermute | solution.py:810
  132.6 36.0 %collective-permute-start.20 = (f32[2,384,512]{2,1,0:T(8,128)}, f32[2,384,512]{2,1,0:T(8,128)}, u32[]{:S(2)}, u32[]{:S(2)}) collective-permute-start(f32[2,384,512]{2,1,0:T(8,128)} %get-tuple-element.223), channel_id=1, source_target_pairs={{0,4},{1,5},{2,6},{3,7},{4,0},{5,1},{6,2},{7,3},{8,12},{9,13},{10,... | collective-permute-start | bytes 4718600 | tf_op jit(solution)/shard_map/ppermute | solution.py:810
  135.0 16.6 %collective-permute-start.17 = (f32[2,2,48,768]{3,2,1,0:T(8,128)}, f32[2,2,48,768]{3,2,1,0:T(8,128)}, u32[]{:S(2)}, u32[]{:S(2)}) collective-permute-start(f32[2,2,48,768]{3,2,1,0:T(8,128)} %fusion.6), channel_id=1, source_target_pairs={{0,8},{1,9},{2,10},{3,11},{4,12},{5,13},{6,14},{7,15},{8,0},{9,1},... | collective-permute-start | bytes 1769480 | tf_op jit(solution)/shard_map/ppermute | solution.py:810
  136.5 13.7 %collective-permute-start.18 = (f32[8,768]{1,0:T(8,128)}, f32[8,768]{1,0:T(8,128)}, u32[]{:S(2)}, u32[]{:S(2)}) collective-permute-start(f32[8,768]{1,0:T(8,128)} %fusion.53), channel_id=1, source_target_pairs={{0,8},{1,9},{2,10},{3,11},{4,12},{5,13},{6,14},{7,15},{8,0},{9,1},... | collective-permute-start | bytes 73736 | tf_op jit(solution)/shard_map/ppermute | solution.py:810
  153.7 28.8 %collective-permute-start.25 = (f32[2,2,48,768]{3,2,1,0:T(8,128)}, f32[2,2,48,768]{3,2,1,0:T(8,128)S(1)}, u32[]{:S(2)}, u32[]{:S(2)}) collective-permute-start(f32[2,2,48,768]{3,2,1,0:T(8,128)} %fusion.10), channel_id=1, source_target_pairs={{0,16},{1,17},{2,18},{3,19},{4,20},{5,21},{6,22},{7,23},{8,24},{9,... | collective-permute-start | bytes 1769480 | tf_op jit(solution)/shard_map/ppermute | solution.py:810
  189.3 16.3 %collective-permute-start.26 = (f32[2,2,48,768]{3,2,1,0:T(8,128)S(1)}, f32[2,2,48,768]{3,2,1,0:T(8,128)S(1)}, u32[]{:S(2)}, u32[]{:S(2)}) collective-permute-start(f32[2,2,48,768]{3,2,1,0:T(8,128)S(1)} %add.397), channel_id=1, source_target_pairs={{0,8},{1,9},{2,10},{3,11},{4,12},{5,13},{6,14},{7,15},{8,0},{9,1},... | collective-permute-start | bytes 1769480 | tf_op jit(solution)/shard_map/ppermute | solution.py:810
  192.0 12.6 %collective-permute-start.28 = (f32[2,96,256]{2,1,0:T(8,128)S(1)}, f32[2,96,256]{2,1,0:T(8,128)S(1)}, u32[]{:S(2)}, u32[]{:S(2)}) collective-permute-start(f32[2,96,256]{2,1,0:T(8,128)S(1)} %add_bitcast_fusion.1), channel_id=1, source_target_pairs={{0,1},{1,0},{2,3},{3,2},{4,5},{5,4},{6,7},{7,6},{8,9},{9,8},{10,11... | collective-permute-start | bytes 589832 | tf_op jit(solution)/shard_map/ppermute | solution.py:810
  192.1 13.7 %collective-permute-start.29 = (f32[2,2,96,256]{3,2,1,0:T(8,128)}, f32[2,2,96,256]{3,2,1,0:T(8,128)S(1)}, u32[]{:S(2)}, u32[]{:S(2)}) collective-permute-start(f32[2,2,96,256]{3,2,1,0:T(8,128)} %get-tuple-element.309), channel_id=1, source_target_pairs={{0,4},{1,5},{2,6},{3,7},{4,0},{5,1},{6,2},{7,3},{8,12},{9,13},{10,... | collective-permute-start | bytes 1179656 | tf_op jit(solution)/shard_map/ppermute | solution.py:810
  192.8 13.0 %collective-permute-start.30 = (f32[2,2,96,256]{3,2,1,0:T(8,128)}, f32[2,2,96,256]{3,2,1,0:T(8,128)S(1)}, u32[]{:S(2)}, u32[]{:S(2)}) collective-permute-start(f32[2,2,96,256]{3,2,1,0:T(8,128)} %get-tuple-element.307), channel_id=1, source_target_pairs={{0,2},{1,3},{2,0},{3,1},{4,6},{5,7},{6,4},{7,5},{8,10},{9,11},{10,... | collective-permute-start | bytes 1179656 | tf_op jit(solution)/shard_map/ppermute | solution.py:810
  199.3 21.8 %collective-permute-start.33 = (f32[2,2,96,256]{3,2,0,1:T(8,128)S(1)}, f32[2,2,96,256]{3,2,0,1:T(8,128)S(1)}, u32[]{:S(2)}, u32[]{:S(2)}) collective-permute-start(f32[2,2,96,256]{3,2,0,1:T(8,128)S(1)} %get-tuple-element.251), channel_id=1, source_target_pairs={{0,8},{1,9},{2,10},{3,11},{4,12},{5,13},{6,14},{7,15},{8,0},{9,1},... | collective-permute-start | bytes 1179656 | tf_op jit(solution)/shard_map/ppermute | solution.py:810
  206.4 14.6 %collective-permute-start.34 = (f32[2,2,96,256]{3,2,0,1:T(8,128)S(1)}, f32[2,2,96,256]{3,2,0,1:T(8,128)S(1)}, u32[]{:S(2)}, u32[]{:S(2)}) collective-permute-start(f32[2,2,96,256]{3,2,0,1:T(8,128)S(1)} %get-tuple-element.304), channel_id=1, source_target_pairs={{0,8},{1,9},{2,10},{3,11},{4,12},{5,13},{6,14},{7,15},{8,0},{9,1},... | collective-permute-start | bytes 1179656 | tf_op jit(solution)/shard_map/ppermute | solution.py:810
  206.6 13.2 %collective-permute-start.32 = (f32[2,2,48,768]{3,2,1,0:T(8,128)S(1)}, f32[2,2,48,768]{3,2,1,0:T(8,128)S(1)}, u32[]{:S(2)}, u32[]{:S(2)}) collective-permute-start(f32[2,2,48,768]{3,2,1,0:T(8,128)S(1)} %get-tuple-element.330), channel_id=1, source_target_pairs={{0,2},{1,3},{2,0},{3,1},{4,6},{5,7},{6,4},{7,5},{8,10},{9,11},{10,... | collective-permute-start | bytes 1769480 | tf_op jit(solution)/shard_map/ppermute | solution.py:810
  206.8 13.9 %collective-permute-start.31 = (f32[2,2,48,768]{3,2,1,0:T(8,128)S(1)}, f32[2,2,48,768]{3,2,1,0:T(8,128)S(1)}, u32[]{:S(2)}, u32[]{:S(2)}) collective-permute-start(f32[2,2,48,768]{3,2,1,0:T(8,128)S(1)} %get-tuple-element.331), channel_id=1, source_target_pairs={{0,4},{1,5},{2,6},{3,7},{4,0},{5,1},{6,2},{7,3},{8,12},{9,13},{10,... | collective-permute-start | bytes 1769480 | tf_op jit(solution)/shard_map/ppermute | solution.py:810
  221.1 22.6 %collective-permute-start.39 = (f32[384,768]{1,0:T(8,128)S(1)}, f32[384,768]{1,0:T(8,128)}, u32[]{:S(2)}, u32[]{:S(2)}) collective-permute-start(f32[384,768]{1,0:T(8,128)S(1)} %bitcast.201), channel_id=1, source_target_pairs={{0,1},{1,0},{2,3},{3,2},{4,5},{5,4},{6,7},{7,6},{8,9},{9,8},{10,11... | collective-permute-start | bytes 3538952 | tf_op jit(solution)/shard_map/ppermute | solution.py:810
  221.2 22.5 %collective-permute-start.38 = (f32[384,768]{1,0:T(8,128)S(1)}, f32[384,768]{1,0:T(8,128)}, u32[]{:S(2)}, u32[]{:S(2)}) collective-permute-start(f32[384,768]{1,0:T(8,128)S(1)} %bitcast.204), channel_id=1, source_target_pairs={{0,1},{1,0},{2,3},{3,2},{4,5},{5,4},{6,7},{7,6},{8,9},{9,8},{10,11... | collective-permute-start | bytes 3538952 | tf_op jit(solution)/shard_map/ppermute | solution.py:810
  222.0 27.7 %collective-permute-start.36 = (f32[384,768]{1,0:T(8,128)S(1)}, f32[384,768]{1,0:T(8,128)}, u32[]{:S(2)}, u32[]{:S(2)}) collective-permute-start(f32[384,768]{1,0:T(8,128)S(1)} %bitcast.202), channel_id=1, source_target_pairs={{0,4},{1,5},{2,6},{3,7},{4,0},{5,1},{6,2},{7,3},{8,12},{9,13},{10,... | collective-permute-start | bytes 3538952 | tf_op jit(solution)/shard_map/ppermute | solution.py:810
  223.1 27.5 %collective-permute-start.35 = (f32[384,768]{1,0:T(8,128)S(1)}, f32[384,768]{1,0:T(8,128)}, u32[]{:S(2)}, u32[]{:S(2)}) collective-permute-start(f32[384,768]{1,0:T(8,128)S(1)} %bitcast.205), channel_id=1, source_target_pairs={{0,2},{1,3},{2,0},{3,1},{4,6},{5,7},{6,4},{7,5},{8,10},{9,11},{10,... | collective-permute-start | bytes 3538952 | tf_op jit(solution)/shard_map/ppermute | solution.py:810
  224.2 23.3 %collective-permute-start.37 = (f32[4,2,96,256]{3,2,0,1:T(8,128)S(1)}, f32[4,2,96,256]{3,2,0,1:T(8,128)}, u32[]{:S(2)}, u32[]{:S(2)}) collective-permute-start(f32[4,2,96,256]{3,2,0,1:T(8,128)S(1)} %maximum_add_fusion), channel_id=1, source_target_pairs={{1,17},{3,19},{5,21},{7,23},{9,25},{11,27},{13,29},{15,31},{16,0},... | collective-permute-start | bytes 2359304 | tf_op jit(solution)/shard_map/ppermute | solution.py:892
  250.6 8.7 %collective-permute-start.41 = (f32[384,768]{1,0:T(8,128)}, f32[384,768]{1,0:T(8,128)S(1)}, u32[]{:S(2)}, u32[]{:S(2)}) collective-permute-start(f32[384,768]{1,0:T(8,128)} %collective-permute-done.36.b_ref), channel_id=1, source_target_pairs={{0,1},{1,0},{2,3},{3,2},{4,5},{5,4},{6,7},{7,6},{8,9},{9,8},{10,11... | collective-permute-start | bytes 3538952 | tf_op jit(solution)/shard_map/ppermute | solution.py:810
  (43 other events, 189.8 us)

commit v3 on v2

--- a/solution.py
+++ b/solution.py
@@ -983,6 +983,7 @@
         [sums_one, sums_two, jnp.full((4, width), queries, jnp.float32)], axis=0
     )
     small = small + swap(small, 1)
+    small = small + swap(small, bits[0])
     part_one = context_part(0, context_queries)
     both_got, small, context_queries, part_one, pieces = tie(
         (got_of(both), small, context_queries, part_one, pieces)
@@ -1009,8 +1010,7 @@
     part_three = context_part(2, context_queries)
     small, part_three, twos_got = tie((small, part_three, got_of(twos)))
     set_got(twos, twos_got)
-    for bit in bits[:2]:
-        small = small + swap(small, bit)
+    small = small + swap(small, bits[1])
     span = (width - FIRST_PART) // 2
     early, late = (
         [

time: 266 us -> 264 us (level)
  starting transfers between devices: 40.4 us -> 37.1 us
    ppermute x41, starting transfers between devices: 37.8 us -> 34.5 us  [swap(): return lax.ppermute(value, 'rows', [(i, i ^ bit) for i in range(devices)])]
  transfers between devices with their start and end apart: 43 -> 43, of which waited for: 21 -> 20; matrix products, arithmetic and copies ran while one was open for 16% -> 16% of each run, Pallas kernels for 37% -> 37%
where the time goes in v3:
time: 264 us; the launch traced here: 262 us
  Pallas kernels  123 us (47%)
  waiting for transfers between devices  43.8 us (17%)
  other arithmetic  38.4 us (15%)
  starting transfers between devices  37.1 us (14%)
  local copies, waits for them, and re-layouts  13 us (5%)
  matrix products  3.76 us (1%)
  between operations  3.38 us (1%)
    ppermute x41, waiting for transfers between devices, swap(): return lax.ppermute(value, 'rows', [(i, i ^ bit) for i in range(devices)])  43.3 us
    pallas_call x4, Pallas kernels, attend(): pl.pallas_call(partial(attend_kernel, keep_logs), grid=(slots // block, p...  38.3 us
    ppermute x41, starting transfers between devices, swap(): return lax.ppermute(value, 'rows', [(i, i ^ bit) for i in range(devices)])  34.5 us
    pallas_call x1, Pallas kernels, output(): pl.pallas_call(output_kernel, grid_spec=pltpu.PrefetchScalarGridSpec(num_...  15.1 us
    add x10, other arithmetic, split(): self.kept = sum((pick(term, axis, mine) for term in self.terms))  14 us
    pallas_call x1, Pallas kernels, units(): pl.pallas_call(partial(units_kernel, bits), grid_spec=pltpu.PrefetchScala...  13.2 us
    pallas_call x4, Pallas kernels, put(): pl.pallas_call(partial(place_kernel, bits, far, got), in_specs=[scalar, s...  12.6 us
    pallas_call x1, Pallas kernels, attend_back(): pl.pallas_call(attend_back_kernel, grid=(pairs,), in_specs=[rows_spec, ke...  12.2 us
  transfers between devices with their start and end apart: 43, of which 20 were waited for; matrix products, arithmetic and copies ran while one was open for 16% of the time, Pallas kernels for 37%

profile of v3, /device:TPU:0, one launch (start us, length us, event | category | flops | bytes accessed | tf_op | source)
XLA Modules:
  0.0 262.2 jit_solution(2140849883350307934)
XLA Ops:
  3.3 10.0 %shard_map.204 = (bf16[1024,768]{1,0:T(8,128)(2,1)}, bf16[1024,768]{1,0:T(8,128)(2,1)}, bf16[256,768]{1,0:T(8,128)(2,1)}, bf16[768,1536]{1,0:T(8,128)(2,1)}, f32...) custom-call(s32[1]{0:T(128)S(6)} %copy.98.context_ref.at_ref, s32[1]{0:T(128)S(6)} %copy.99.queries_ref, ...), custom_call_target="tpu_custom_call" | custom-call | flops 37748736 | bytes 172032 | tf_op jit(solution)/shard_map/pallas_call | solution.py:186
  13.8 9.4 %shard_map.205 = (bf16[256,768]{1,0:T(8,128)(2,1)}, f32[256,768]{1,0:T(8,128)}, f32[256,768]{1,0:T(8,128)}, f32[256,1]{1,0:T(8,128)}, f32[256,768]{1,0:T(8,128)}) custom-call(bf16[256,768]{1,0:T(8,128)(2,1)} %get-tuple-element.149.query_ref, bf16[768,1536]{1,0:T(8,128)(2,1)} %get-tuple-element.150.key_ref.value_ref, ...), custom_call_target="tpu_custom_call" | custom-call | flops 37748736 | bytes 73728 | tf_op jit(solution)/shard_map/pallas_call | solution.py:256
  23.2 2.5 collective-permute-done.got_ref
  26.5 13.2 %shard_map.206 = (f32[4,192,256]{2,1,0:T(8,128)}, f32[4,192,256]{2,1,0:T(8,128)}, f32[4,192,512]{2,1,0:T(8,128)}, f32[4,192,512]{2,1,0:T(8,128)}, f32[2,384,256]...) custom-call(s32[1]{0:T(128)} %bitcast.at_ref.me_ref, ...), custom_call_target="tpu_custom_call" | custom-call | flops 75497472 | bytes 221184 | tf_op jit(solution)/shard_map/pallas_call | solution.py:352
  39.9 2.8 %collective-permute-start.3 = (f32[4,192,256]{2,1,0:T(8,128)}, f32[4,192,256]{2,1,0:T(8,128)S(1)}, u32[]{:S(2)}, u32[]{:S(2)}) collective-permute-start(f32[4,192,256]{2,1,0:T(8,128)} %get-tuple-element.166), channel_id=1, source_target_pairs={{0,2},{1,3},{2,0},{3,1},{4,6},{5,7},{6,4},{7,5},{8,10},{9,11},{10,... | collective-permute-start | bytes 2359304 | tf_op jit(solution)/shard_map/ppermute | solution.py:810
  45.3 12.2 %shard_map.207 = (bf16[256,768]{1,0:T(8,128)(2,1)}, bf16[768,768]{1,0:T(8,128)(2,1)}, bf16[768,768]{1,0:T(8,128)(2,1)}, f32[256,768]{1,0:T(8,128)}, bf16[256,768]{1,0:T(8,128)(2,1)}, /*index=5*/f32[2,768]{1,0:T(2,128)}) custom-call(bf16[256,768]{1,0:T(8,128)(2,1)} %get-tuple-element.149.query_ref, bf16[768,1536]{1,0:T(8,128)(2,1)} %get-tuple-element.150.key_ref.value_ref, ...), custom_call_target="tpu_custom_call" | custom-call | flops 94371840 | bytes 92160 | tf_op jit(solution)/shard_map/pallas_call | solution.py:500
  57.5 7.7 %shard_map.208 = (f32[768,768]{1,0:T(8,128)}, f32[768,768]{1,0:T(8,128)}, f32[768,768]{1,0:T(8,128)}, f32[768,768]{1,0:T(8,128)}) custom-call(s32[1]{0:T(128)} %bitcast.at_ref.me_ref, bf16[1024,768]{1,0:T(8,128)(2,1)} %get-tuple-element.148.norm_ref, bf16[256,768]{1,0:T(8,128)(2,1)} %get-tuple-element.154.attended_ref, ...), custom_call_target="tpu_custom_call" | custom-call | flops 37748736 | bytes 184320 | tf_op jit(solution)/shard_map/pallas_call | solution.py:582
  70.2 2.1 dynamic-slice_add_fusion.1
  73.5 2.0 dynamic-slice_add_fusion
  84.8 4.9 %shard_map.210 = (f32[256,768]{1,0:T(8,128)}, f32[256,768]{1,0:T(8,128)}) custom-call(s32[1]{0:T(128)} %bitcast.at_ref.me_ref, bf16[512,1536]{1,0:T(8,128)(2,1)} %get-tuple-element.189.left_ref, bf16[3072,768]{1,0:T(8,128)(2,1)} %refs_11_.1), custom_call_target="tpu_custom_call" | custom-call | flops 18874368 | bytes 73728 | tf_op jit(solution)/shard_map/pallas_call | solution.py:409
  89.7 3.7 %collective-permute-done.11 = f32[2,2,96,256]{3,2,0,1:T(8,128)} collective-permute-done((f32[2,2,96,256]{3,2,0,1:T(8,128)}, f32[2,2,96,256]{3,2,0,1:T(8,128)}, u32[]{:S(2)}, u32[]{:S(2)}) %collective-permute-start.11) | collective-permute-done | bytes 393248 | tf_op jit(solution)/shard_map/ppermute | solution.py:810
  93.4 2.0 fusion.37
  97.7 8.8 %shard_map.209 = (f32[1024,768]{1,0:T(8,128)}, f32[2,768]{1,0:T(2,128)}) custom-call(bf16[256,768]{1,0:T(8,128)(2,1)} %get-tuple-element.182.dq_ref, bf16[768,768]{1,0:T(8,128)(2,1)} %get-tuple-element.183.dk_ref, bf16[768,768]{1,0:T(8,128)(2,1)} %get-tuple-element.184.dv_ref, bf16[1024,768]{1,0:T(8,128)(2,1)} %get-tuple-element.153.rows_ref, ...), custom_call_target="tpu_custom_call" | custom-call | flops 37748736 | bytes 147456 | tf_op jit(solution)/shard_map/pallas_call | solution.py:630
  106.6 3.8 %convolution_convert_fusion.query_ref = bf16[768,768]{1,0:T(8,128)(2,1)} fusion(bf16[768,768]{1,0:T(8,128)(2,1)} %slice.69, bf16[768,2304]{1,0:T(8,128)(2,1)} %wv.1), kind=kOutput, calls=%fused_computation.4 | convolution fusion | flops 906559488 | bytes 3538944 | tf_op jit(solution)/shard_map/dot_general | solution.py:28
  112.5 2.2 bitcast_add_fusion.2
  118.6 9.6 %shard_map.211 = (bf16[256,768]{1,0:T(8,128)(2,1)}, f32[256,768]{1,0:T(8,128)}, f32[256,768]{1,0:T(8,128)}, f32[256,1]{1,0:T(8,128)}) custom-call(bf16[768,768]{1,0:T(8,128)(2,1)} %convolution_convert_fusion.query_ref, bf16[768,1536]{1,0:T(8,128)(2,1)} %get-tuple-element.150.key_ref.value_ref, bf16[768,1536]{1,0:T(8,128)(2,1)} %get-tuple-element.150.key_ref.value_ref, ...), custom_call_target="tpu_custom_call" | custom-call | flops 37748736 | bytes 73728 | tf_op jit(solution)/shard_map/pallas_call | solution.py:256
  128.2 3.2 %collective-permute-done.17 = f32[8,768]{1,0:T(8,128)S(1)} collective-permute-done((f32[8,768]{1,0:T(8,128)S(1)}, f32[8,768]{1,0:T(8,128)S(1)}, u32[]{:S(2)}, u32[]{:S(2)}) %collective-permute-start.17) | collective-permute-done | bytes 24608 | tf_op jit(solution)/shard_map/ppermute | solution.py:810
  140.0 9.7 %shard_map.212 = (bf16[256,768]{1,0:T(8,128)(2,1)}, f32[256,768]{1,0:T(8,128)}, f32[256,768]{1,0:T(8,128)}, f32[256,1]{1,0:T(8,128)}) custom-call(bf16[768,768]{1,0:T(8,128)(2,1)} %convolution_convert_fusion.query_ref, bf16[768,1536]{1,0:T(8,128)(2,1)} %get-tuple-element.150.key_ref.value_ref, bf16[768,1536]{1,0:T(8,128)(2,1)} %get-tuple-element.150.key_ref.value_ref, ...), custom_call_target="tpu_custom_call" | custom-call | flops 37748736 | bytes 73728 | tf_op jit(solution)/shard_map/pallas_call | solution.py:256
  152.6 2.1 fusion.10
  155.3 9.6 %shard_map.213 = (bf16[256,768]{1,0:T(8,128)(2,1)}, f32[256,768]{1,0:T(8,128)}, f32[256,768]{1,0:T(8,128)}, f32[256,1]{1,0:T(8,128)}) custom-call(bf16[768,768]{1,0:T(8,128)(2,1)} %convolution_convert_fusion.query_ref, bf16[768,1536]{1,0:T(8,128)(2,1)} %get-tuple-element.150.key_ref.value_ref, bf16[768,1536]{1,0:T(8,128)(2,1)} %get-tuple-element.150.key_ref.value_ref, ...), custom_call_target="tpu_custom_call" | custom-call | flops 37748736 | bytes 73728 | tf_op jit(solution)/shard_map/pallas_call | solution.py:256
  165.0 3.2 %collective-permute-done.20 = f32[4,192,512]{2,1,0:T(8,128)} collective-permute-done((f32[4,192,512]{2,1,0:T(8,128)}, f32[4,192,512]{2,1,0:T(8,128)}, u32[]{:S(2)}, u32[]{:S(2)}) %collective-permute-start.20) | collective-permute-done | bytes 1572896 | tf_op jit(solution)/shard_map/ppermute | solution.py:810
  179.5 2.3 collective-permute-done.25
  181.8 4.0 %collective-permute-done.23 = f32[2,2,96,256]{3,2,1,0:T(8,128)S(1)} collective-permute-done((f32[2,2,96,256]{3,2,1,0:T(8,128)S(1)}, f32[2,2,96,256]{3,2,1,0:T(8,128)S(1)}, u32[]{:S(2)}, u32[]{:S(2)}) %collective-permute-start.23) | collective-permute-done | bytes 393248 | tf_op jit(solution)/shard_map/ppermute | solution.py:810
  194.8 6.5 %collective-permute-done.27 = f32[8,768]{1,0:T(8,128)S(1)} collective-permute-done((f32[8,768]{1,0:T(8,128)}, f32[8,768]{1,0:T(8,128)S(1)}, u32[]{:S(2)}, u32[]{:S(2)}) %collective-permute-start.27) | collective-permute-done | bytes 24608 | tf_op jit(solution)/shard_map/ppermute | solution.py:810
  208.1 3.2 %fusion = f32[1024,768]{1,0:T(8,128)} fusion(s32[]{:T(128)S(6)} %select_n.156, f32[1024,768]{1,0:T(8,128)S(1)} %broadcast_multiply_fusion), kind=kLoop, calls=%fused_computation.2 | loop fusion | flops 786432 | bytes 6291460 | tf_op jit(solution)/shard_map/concatenate | solution.py:926
  211.9 6.8 %collective-permute-done.32 = f32[2,2,48,768]{3,2,1,0:T(8,128)S(1)} collective-permute-done((f32[2,2,48,768]{3,2,1,0:T(8,128)S(1)}, f32[2,2,48,768]{3,2,1,0:T(8,128)S(1)}, u32[]{:S(2)}, u32[]{:S(2)}) %collective-permute-start.32) | collective-permute-done | bytes 589856 | tf_op jit(solution)/shard_map/ppermute | solution.py:810
  224.1 3.1 %shard_map.214 = (f32[768,2304]{1,0:T(8,128)}, f32[768,768]{1,0:T(8,128)}) custom-call(s32[1]{0:T(128)} %bitcast.at_ref.me_ref, f32[1,1]{1,0:T(1,128)} %div.6.factor_ref, f32[384,768]{1,0:T(8,128)} %bitcast.206, f32[384,768]{1,0:T(8,128)} %bitcast.203), custom_call_target="tpu_custom_call" | custom-call | bytes 73728 | tf_op jit(solution)/shard_map/pallas_call | solution.py:693
  227.2 15.1 %shard_map.216 = bf16[1024,768]{1,0:T(8,128)(2,1)} custom-call(s32[1]{0:T(128)S(6)} %copy.98.context_ref.at_ref, f32[256,768]{1,0:T(8,128)} %get-tuple-element.264.refs_0_, f32[256,768]{1,0:T(8,128)} %get-tuple-element.265.refs_1_, f32[256,768]{1,0:T(8,128)} %get-tuple-element.266.refs_2_, f32[256,768]{1,0:T(8,128)} %get-tuple-element.267.refs_3_, ...), custom_call_target="tpu_custom_call" | custom-call | flops 7247757312 | bytes 18874368 | tf_op jit(solution)/shard_map/pallas_call | solution.py:752
  242.3 3.2 %shard_map.215 = (f32[768,2304]{1,0:T(8,128)}, f32[768,768]{1,0:T(8,128)}) custom-call(s32[1]{0:T(128)} %bitcast.at_ref.me_ref, f32[1,1]{1,0:T(1,128)} %div.6.factor_ref, f32[384,768]{1,0:T(8,128)} %collective-permute-done.38.a_ref, f32[384,768]{1,0:T(8,128)} %collective-permute-done.39.b_ref, ...), custom_call_target="tpu_custom_call", output_to_operand_aliasing={{0}: (4, {}), {1}: (5, {})} | custom-call | bytes 73728 | tf_op jit(solution)/shard_map/pallas_call | solution.py:693
  246.1 2.0 collective-permute-done.36.b_ref
  251.7 3.1 %shard_map.217 = (f32[768,2304]{1,0:T(8,128)}, f32[768,768]{1,0:T(8,128)}) custom-call(s32[1]{0:T(128)} %bitcast.at_ref.me_ref, f32[1,1]{1,0:T(1,128)} %div.6.factor_ref, f32[384,768]{1,0:T(8,128)} %collective-permute-done.35.a_ref, f32[384,768]{1,0:T(8,128)} %collective-permute-done.36.b_ref, ...), custom_call_target="tpu_custom_call", output_to_operand_aliasing={{0}: (4, {}), {1}: (5, {})} | custom-call | bytes 73728 | tf_op jit(solution)/shard_map/pallas_call | solution.py:693
  258.8 3.2 %shard_map.218 = (f32[768,2304]{1,0:T(8,128)}, f32[768,768]{1,0:T(8,128)}) custom-call(s32[1]{0:T(128)} %bitcast.at_ref.me_ref, f32[1,1]{1,0:T(1,128)} %div.6.factor_ref, f32[384,768]{1,0:T(8,128)} %copy-done.13, f32[384,768]{1,0:T(8,128)} %copy-done.14, f32[768,2304]{1,0:T(8,128)} %get-tuple-element.280.refs_0_, ...), custom_call_target="tpu_custom_call", output_to_operand_aliasing={{0}: (4, {}), {1}: (5, {})} | custom-call | bytes 73728 | tf_op jit(solution)/shard_map/pallas_call | solution.py:693
  (186 shorter events, 81.8 us)
Async XLA Ops:
  13.3 9.9 %collective-permute-start.1 = (f32[256,768]{1,0:T(8,128)}, f32[256,768]{1,0:T(8,128)S(1)}, u32[]{:S(2)}, u32[]{:S(2)}) collective-permute-start(f32[256,768]{1,0:T(8,128)} %get-tuple-element.157.grad_ref.upstream_ref), channel_id=1, source_target_pairs={{0,1},{1,0},{2,3},{3,2},{4,5},{5,4},{6,7},{7,6},{8,9},{9,8},{10,11... | collective-permute-start | bytes 2359304 | tf_op jit(solution)/shard_map/ppermute | solution.py:810
  39.9 25.2 %collective-permute-start.3 = (f32[4,192,256]{2,1,0:T(8,128)}, f32[4,192,256]{2,1,0:T(8,128)S(1)}, u32[]{:S(2)}, u32[]{:S(2)}) collective-permute-start(f32[4,192,256]{2,1,0:T(8,128)} %get-tuple-element.166), channel_id=1, source_target_pairs={{0,2},{1,3},{2,0},{3,1},{4,6},{5,7},{6,4},{7,5},{8,10},{9,11},{10,... | collective-permute-start | bytes 2359304 | tf_op jit(solution)/shard_map/ppermute | solution.py:810
  42.7 22.5 %collective-permute-start.4 = (f32[2,384,256]{2,1,0:T(8,128)}, f32[2,384,256]{2,1,0:T(8,128)S(1)}, u32[]{:S(2)}, u32[]{:S(2)}) collective-permute-start(f32[2,384,256]{2,1,0:T(8,128)} %get-tuple-element.167), channel_id=1, source_target_pairs={{0,4},{1,5},{2,6},{3,7},{4,0},{5,1},{6,2},{7,3},{8,12},{9,13},{10,... | collective-permute-start | bytes 2359304 | tf_op jit(solution)/shard_map/ppermute | solution.py:810
  67.6 11.0 %collective-permute-start.8 = (f32[2,2,96,256]{3,2,1,0:T(8,128)S(1)}, f32[2,2,96,256]{3,2,1,0:T(8,128)}, u32[]{:S(2)}, u32[]{:S(2)}) collective-permute-start(f32[2,2,96,256]{3,2,1,0:T(8,128)S(1)} %get-tuple-element.325), channel_id=1, source_target_pairs={{0,2},{1,3},{2,0},{3,1},{4,6},{5,7},{6,4},{7,5},{8,10},{9,11},{10,... | collective-permute-start | bytes 1179656 | tf_op jit(solution)/shard_map/ppermute | solution.py:810
  68.2 11.2 %collective-permute-start.7 = (f32[2,2,96,256]{3,2,1,0:T(8,128)S(1)}, f32[2,2,96,256]{3,2,1,0:T(8,128)}, u32[]{:S(2)}, u32[]{:S(2)}) collective-permute-start(f32[2,2,96,256]{3,2,1,0:T(8,128)S(1)} %get-tuple-element.342), channel_id=1, source_target_pairs={{0,4},{1,5},{2,6},{3,7},{4,0},{5,1},{6,2},{7,3},{8,12},{9,13},{10,... | collective-permute-start | bytes 1179656 | tf_op jit(solution)/shard_map/ppermute | solution.py:810
  79.4 31.0 %collective-permute-start.9 = (f32[2,2,2,48,768]{4,3,2,0,1:T(8,128)}, f32[2,2,2,48,768]{4,3,2,0,1:T(8,128)}, u32[]{:S(2)}, u32[]{:S(2)}) collective-permute-start(f32[2,2,2,48,768]{4,3,2,0,1:T(8,128)} %get-tuple-element.177), channel_id=1, source_target_pairs={{0,2},{1,3},{2,0},{3,1},{4,6},{5,7},{6,4},{7,5},{8,10},{9,11},{10,... | collective-permute-start | bytes 3538952 | tf_op jit(solution)/shard_map/ppermute | solution.py:810
  80.3 30.0 %collective-permute-start.10 = (f32[2,2,2,48,768]{4,3,2,0,1:T(8,128)}, f32[2,2,2,48,768]{4,3,2,0,1:T(8,128)}, u32[]{:S(2)}, u32[]{:S(2)}) collective-permute-start(f32[2,2,2,48,768]{4,3,2,0,1:T(8,128)} %get-tuple-element.178), channel_id=1, source_target_pairs={{0,4},{1,5},{2,6},{3,7},{4,0},{5,1},{6,2},{7,3},{8,12},{9,13},{10,... | collective-permute-start | bytes 3538952 | tf_op jit(solution)/shard_map/ppermute | solution.py:810
  83.3 10.1 %collective-permute-start.11 = (f32[2,2,96,256]{3,2,0,1:T(8,128)}, f32[2,2,96,256]{3,2,0,1:T(8,128)}, u32[]{:S(2)}, u32[]{:S(2)}) collective-permute-start(f32[2,2,96,256]{3,2,0,1:T(8,128)} %fusion.33), channel_id=1, source_target_pairs={{0,8},{1,9},{2,10},{3,11},{4,12},{5,13},{6,14},{7,15},{8,0},{9,1},... | collective-permute-start | bytes 1179656 | tf_op jit(solution)/shard_map/ppermute | solution.py:810
  89.7 20.6 %collective-permute-start.13 = (f32[256,768]{1,0:T(8,128)}, f32[256,768]{1,0:T(8,128)}, u32[]{:S(2)}, u32[]{:S(2)}) collective-permute-start(f32[256,768]{1,0:T(8,128)} %get-tuple-element.191), channel_id=1, source_target_pairs={{0,1},{1,0},{2,3},{3,2},{4,5},{5,4},{6,7},{7,6},{8,9},{9,8},{10,11... | collective-permute-start | bytes 2359304 | tf_op jit(solution)/shard_map/ppermute | solution.py:810
  95.3 15.0 %collective-permute-start.12 = (f32[2,2,96,256]{3,2,0,1:T(8,128)}, f32[2,2,96,256]{3,2,0,1:T(8,128)S(1)}, u32[]{:S(2)}, u32[]{:S(2)}) collective-permute-start(f32[2,2,96,256]{3,2,0,1:T(8,128)} %fusion.37), channel_id=1, source_target_pairs={{1,17},{3,19},{5,21},{7,23},{9,25},{11,27},{13,29},{15,31},{16,0},... | collective-permute-start | bytes 1179656 | tf_op jit(solution)/shard_map/ppermute | solution.py:892
  114.7 17.3 %collective-permute-start.14 = (f32[2,2,48,768]{3,2,1,0:T(8,128)S(1)}, f32[2,2,48,768]{3,2,1,0:T(8,128)S(1)}, u32[]{:S(2)}, u32[]{:S(2)}) collective-permute-start(f32[2,2,48,768]{3,2,1,0:T(8,128)S(1)} %get-tuple-element.197), channel_id=1, source_target_pairs={{0,4},{1,5},{2,6},{3,7},{4,0},{5,1},{6,2},{7,3},{8,12},{9,13},{10,... | collective-permute-start | bytes 1769480 | tf_op jit(solution)/shard_map/ppermute | solution.py:810
  115.1 16.9 %collective-permute-start.15 = (f32[2,2,48,768]{3,2,1,0:T(8,128)}, f32[2,2,48,768]{3,2,1,0:T(8,128)S(1)}, u32[]{:S(2)}, u32[]{:S(2)}) collective-permute-start(f32[2,2,48,768]{3,2,1,0:T(8,128)} %get-tuple-element.198), channel_id=1, source_target_pairs={{0,2},{1,3},{2,0},{3,1},{4,6},{5,7},{6,4},{7,5},{8,10},{9,11},{10,... | collective-permute-start | bytes 1769480 | tf_op jit(solution)/shard_map/ppermute | solution.py:810
  118.0 13.4 %collective-permute-start.17 = (f32[8,768]{1,0:T(8,128)S(1)}, f32[8,768]{1,0:T(8,128)S(1)}, u32[]{:S(2)}, u32[]{:S(2)}) collective-permute-start(f32[8,768]{1,0:T(8,128)S(1)} %fusion.53), channel_id=1, source_target_pairs={{0,2},{1,3},{2,0},{3,1},{4,6},{5,7},{6,4},{7,5},{8,10},{9,11},{10,... | collective-permute-start | bytes 73736 | tf_op jit(solution)/shard_map/ppermute | solution.py:810
  132.0 36.2 %collective-permute-start.20 = (f32[4,192,512]{2,1,0:T(8,128)}, f32[4,192,512]{2,1,0:T(8,128)}, u32[]{:S(2)}, u32[]{:S(2)}) collective-permute-start(f32[4,192,512]{2,1,0:T(8,128)} %get-tuple-element.222), channel_id=1, source_target_pairs={{0,2},{1,3},{2,0},{3,1},{4,6},{5,7},{6,4},{7,5},{8,10},{9,11},{10,... | collective-permute-start | bytes 4718600 | tf_op jit(solution)/shard_map/ppermute | solution.py:810
  133.7 36.0 %collective-permute-start.21 = (f32[2,384,512]{2,1,0:T(8,128)}, f32[2,384,512]{2,1,0:T(8,128)}, u32[]{:S(2)}, u32[]{:S(2)}) collective-permute-start(f32[2,384,512]{2,1,0:T(8,128)} %get-tuple-element.223), channel_id=1, source_target_pairs={{0,4},{1,5},{2,6},{3,7},{4,0},{5,1},{6,2},{7,3},{8,12},{9,13},{10,... | collective-permute-start | bytes 4718600 | tf_op jit(solution)/shard_map/ppermute | solution.py:810
  136.1 16.4 %collective-permute-start.18 = (f32[2,2,48,768]{3,2,1,0:T(8,128)}, f32[2,2,48,768]{3,2,1,0:T(8,128)}, u32[]{:S(2)}, u32[]{:S(2)}) collective-permute-start(f32[2,2,48,768]{3,2,1,0:T(8,128)} %fusion.6), channel_id=1, source_target_pairs={{0,8},{1,9},{2,10},{3,11},{4,12},{5,13},{6,14},{7,15},{8,0},{9,1},... | collective-permute-start | bytes 1769480 | tf_op jit(solution)/shard_map/ppermute | solution.py:810
  137.7 13.5 %collective-permute-start.19 = (f32[8,768]{1,0:T(8,128)}, f32[8,768]{1,0:T(8,128)}, u32[]{:S(2)}, u32[]{:S(2)}) collective-permute-start(f32[8,768]{1,0:T(8,128)} %add.381), channel_id=1, source_target_pairs={{0,8},{1,9},{2,10},{3,11},{4,12},{5,13},{6,14},{7,15},{8,0},{9,1},... | collective-permute-start | bytes 73736 | tf_op jit(solution)/shard_map/ppermute | solution.py:810
  154.7 27.1 %collective-permute-start.25 = (f32[2,2,48,768]{3,2,1,0:T(8,128)}, f32[2,2,48,768]{3,2,1,0:T(8,128)S(1)}, u32[]{:S(2)}, u32[]{:S(2)}) collective-permute-start(f32[2,2,48,768]{3,2,1,0:T(8,128)} %fusion.10), channel_id=1, source_target_pairs={{0,16},{1,17},{2,18},{3,19},{4,20},{5,21},{6,22},{7,23},{8,24},{9,... | collective-permute-start | bytes 1769480 | tf_op jit(solution)/shard_map/ppermute | solution.py:810
  176.7 9.1 %collective-permute-start.23 = (f32[2,2,96,256]{3,2,1,0:T(8,128)S(1)}, f32[2,2,96,256]{3,2,1,0:T(8,128)S(1)}, u32[]{:S(2)}, u32[]{:S(2)}) collective-permute-start(f32[2,2,96,256]{3,2,1,0:T(8,128)S(1)} %get-tuple-element.228), channel_id=1, source_target_pairs={{0,4},{1,5},{2,6},{3,7},{4,0},{5,1},{6,2},{7,3},{8,12},{9,13},{10,... | collective-permute-start | bytes 1179656 | tf_op jit(solution)/shard_map/ppermute | solution.py:810
  188.0 15.5 %collective-permute-start.26 = (f32[2,2,48,768]{3,2,1,0:T(8,128)S(1)}, f32[2,2,48,768]{3,2,1,0:T(8,128)S(1)}, u32[]{:S(2)}, u32[]{:S(2)}) collective-permute-start(f32[2,2,48,768]{3,2,1,0:T(8,128)S(1)} %add.397), channel_id=1, source_target_pairs={{0,8},{1,9},{2,10},{3,11},{4,12},{5,13},{6,14},{7,15},{8,0},{9,1},... | collective-permute-start | bytes 1769480 | tf_op jit(solution)/shard_map/ppermute | solution.py:810
  190.6 11.9 %collective-permute-start.28 = (f32[2,96,256]{2,1,0:T(8,128)S(1)}, f32[2,96,256]{2,1,0:T(8,128)S(1)}, u32[]{:S(2)}, u32[]{:S(2)}) collective-permute-start(f32[2,96,256]{2,1,0:T(8,128)S(1)} %add_bitcast_fusion.1), channel_id=1, source_target_pairs={{0,1},{1,0},{2,3},{3,2},{4,5},{5,4},{6,7},{7,6},{8,9},{9,8},{10,11... | collective-permute-start | bytes 589832 | tf_op jit(solution)/shard_map/ppermute | solution.py:810
  190.7 13.0 %collective-permute-start.29 = (f32[2,2,96,256]{3,2,1,0:T(8,128)}, f32[2,2,96,256]{3,2,1,0:T(8,128)S(1)}, u32[]{:S(2)}, u32[]{:S(2)}) collective-permute-start(f32[2,2,96,256]{3,2,1,0:T(8,128)} %get-tuple-element.309), channel_id=1, source_target_pairs={{0,4},{1,5},{2,6},{3,7},{4,0},{5,1},{6,2},{7,3},{8,12},{9,13},{10,... | collective-permute-start | bytes 1179656 | tf_op jit(solution)/shard_map/ppermute | solution.py:810
  191.8 11.8 %collective-permute-start.30 = (f32[2,2,96,256]{3,2,1,0:T(8,128)}, f32[2,2,96,256]{3,2,1,0:T(8,128)S(1)}, u32[]{:S(2)}, u32[]{:S(2)}) collective-permute-start(f32[2,2,96,256]{3,2,1,0:T(8,128)} %get-tuple-element.307), channel_id=1, source_target_pairs={{0,2},{1,3},{2,0},{3,1},{4,6},{5,7},{6,4},{7,5},{8,10},{9,11},{10,... | collective-permute-start | bytes 1179656 | tf_op jit(solution)/shard_map/ppermute | solution.py:810
  201.3 18.1 %collective-permute-start.33 = (f32[2,2,96,256]{3,2,0,1:T(8,128)S(1)}, f32[2,2,96,256]{3,2,0,1:T(8,128)S(1)}, u32[]{:S(2)}, u32[]{:S(2)}) collective-permute-start(f32[2,2,96,256]{3,2,0,1:T(8,128)S(1)} %get-tuple-element.251), channel_id=1, source_target_pairs={{0,8},{1,9},{2,10},{3,11},{4,12},{5,13},{6,14},{7,15},{8,0},{9,1},... | collective-permute-start | bytes 1179656 | tf_op jit(solution)/shard_map/ppermute | solution.py:810
  204.3 15.2 %collective-permute-start.34 = (f32[2,2,96,256]{3,2,0,1:T(8,128)S(1)}, f32[2,2,96,256]{3,2,0,1:T(8,128)S(1)}, u32[]{:S(2)}, u32[]{:S(2)}) collective-permute-start(f32[2,2,96,256]{3,2,0,1:T(8,128)S(1)} %get-tuple-element.304), channel_id=1, source_target_pairs={{0,8},{1,9},{2,10},{3,11},{4,12},{5,13},{6,14},{7,15},{8,0},{9,1},... | collective-permute-start | bytes 1179656 | tf_op jit(solution)/shard_map/ppermute | solution.py:810
  205.3 13.4 %collective-permute-start.32 = (f32[2,2,48,768]{3,2,1,0:T(8,128)S(1)}, f32[2,2,48,768]{3,2,1,0:T(8,128)S(1)}, u32[]{:S(2)}, u32[]{:S(2)}) collective-permute-start(f32[2,2,48,768]{3,2,1,0:T(8,128)S(1)} %get-tuple-element.330), channel_id=1, source_target_pairs={{0,2},{1,3},{2,0},{3,1},{4,6},{5,7},{6,4},{7,5},{8,10},{9,11},{10,... | collective-permute-start | bytes 1769480 | tf_op jit(solution)/shard_map/ppermute | solution.py:810
  206.1 12.9 %collective-permute-start.31 = (f32[2,2,48,768]{3,2,1,0:T(8,128)S(1)}, f32[2,2,48,768]{3,2,1,0:T(8,128)S(1)}, u32[]{:S(2)}, u32[]{:S(2)}) collective-permute-start(f32[2,2,48,768]{3,2,1,0:T(8,128)S(1)} %get-tuple-element.331), channel_id=1, source_target_pairs={{0,4},{1,5},{2,6},{3,7},{4,0},{5,1},{6,2},{7,3},{8,12},{9,13},{10,... | collective-permute-start | bytes 1769480 | tf_op jit(solution)/shard_map/ppermute | solution.py:810
  219.5 22.9 %collective-permute-start.39 = (f32[384,768]{1,0:T(8,128)S(1)}, f32[384,768]{1,0:T(8,128)}, u32[]{:S(2)}, u32[]{:S(2)}) collective-permute-start(f32[384,768]{1,0:T(8,128)S(1)} %bitcast.201), channel_id=1, source_target_pairs={{0,1},{1,0},{2,3},{3,2},{4,5},{5,4},{6,7},{7,6},{8,9},{9,8},{10,11... | collective-permute-start | bytes 3538952 | tf_op jit(solution)/shard_map/ppermute | solution.py:810
  219.5 22.8 %collective-permute-start.38 = (f32[384,768]{1,0:T(8,128)S(1)}, f32[384,768]{1,0:T(8,128)}, u32[]{:S(2)}, u32[]{:S(2)}) collective-permute-start(f32[384,768]{1,0:T(8,128)S(1)} %bitcast.204), channel_id=1, source_target_pairs={{0,1},{1,0},{2,3},{3,2},{4,5},{5,4},{6,7},{7,6},{8,9},{9,8},{10,11... | collective-permute-start | bytes 3538952 | tf_op jit(solution)/shard_map/ppermute | solution.py:810
  220.4 27.7 %collective-permute-start.36 = (f32[384,768]{1,0:T(8,128)S(1)}, f32[384,768]{1,0:T(8,128)}, u32[]{:S(2)}, u32[]{:S(2)}) collective-permute-start(f32[384,768]{1,0:T(8,128)S(1)} %bitcast.202), channel_id=1, source_target_pairs={{0,4},{1,5},{2,6},{3,7},{4,0},{5,1},{6,2},{7,3},{8,12},{9,13},{10,... | collective-permute-start | bytes 3538952 | tf_op jit(solution)/shard_map/ppermute | solution.py:810
  221.3 27.5 %collective-permute-start.35 = (f32[384,768]{1,0:T(8,128)S(1)}, f32[384,768]{1,0:T(8,128)}, u32[]{:S(2)}, u32[]{:S(2)}) collective-permute-start(f32[384,768]{1,0:T(8,128)S(1)} %bitcast.205), channel_id=1, source_target_pairs={{0,2},{1,3},{2,0},{3,1},{4,6},{5,7},{6,4},{7,5},{8,10},{9,11},{10,... | collective-permute-start | bytes 3538952 | tf_op jit(solution)/shard_map/ppermute | solution.py:810
  222.8 23.3 %collective-permute-start.37 = (f32[4,2,96,256]{3,2,0,1:T(8,128)S(1)}, f32[4,2,96,256]{3,2,0,1:T(8,128)}, u32[]{:S(2)}, u32[]{:S(2)}) collective-permute-start(f32[4,2,96,256]{3,2,0,1:T(8,128)S(1)} %maximum_add_fusion), channel_id=1, source_target_pairs={{1,17},{3,19},{5,21},{7,23},{9,25},{11,27},{13,29},{15,31},{16,0},... | collective-permute-start | bytes 2359304 | tf_op jit(solution)/shard_map/ppermute | solution.py:892
  (43 other events, 197.5 us)
